TPU v7x, 256 devices: a whole 4x4x8 slice. The times are simulated.
256 devices in a mesh: dp: 64 (over x, z, core), mp: 4 (over y).
Axes of the slice: x: 4, y: 4, z: 8, core: 2. Of those that a mesh axis runs over, the one named last changes fastest.
Arguments:
- partials: bfloat16 [64, 8, 640, 1024], P('dp', None, None, 'mp'), may hold values from -16 to 16
- owner: int32 [8], replicated, may hold values from 0 to 63, as said below
- rowblock: int32 [8, 64], replicated, may hold values from 0 to 63, each once within a row
- factor: float32 [64, 640, 2, 640], P('dp', 'mp'), as said below
- basis: float32 [64, 640, 2, 640], P('dp', 'mp'), may hold values from -0.25 to 0.25
- moment1: float32 [64, 2, 640, 1024], P('dp', None, None, 'mp'), may hold values from -1.5 to 1.5
- moment2: float32 [64, 2, 640, 1024], P('dp', None, None, 'mp'), may hold values from 0.001 to 0.02
- master: float32 [64, 2, 640, 1024], P('dp', None, None, 'mp'), may hold values from -6 to 6
Outputs:
- train_weights: float32 [8, 64, 10, 1024], P(None, 'dp', None, 'mp')
- new_basis: float32 [64, 640, 2, 640], P('dp', 'mp')
Inputs may be any that keep to these rules, and one draw needn't show every extreme that they name: `owner`: each data group owns at most 2 matrices and one owns exactly 2; the first and the last data group each own a matrix. `rowblock`: each row is a permutation of the data groups' row blocks. `factor`: symmetric in its two 640 dimensions.
All inputs are finite; a program needn't handle non-finite values.
Results may differ from a plain program's by a relative error of at most 0.0003.
Values sent between devices are 32-bit elements; how exact they have to be, the bound alone decides.
No kernel may reach another device: no remote copies, remote signals or barrier semaphores. Data moves between devices by JAX's collectives and lax.ppermute only.
A program may use at most 128 MiB of HBM per device.

v0:
```python
import jax
import jax.numpy as jnp
from jax import lax
from jax.sharding import PartitionSpec as P

NS_ITERS = 4


def body(partials, owner, rowblock, factor, basis, moment1, moment2, master):
    top_precision = lax.Precision.HIGHEST
    groups = lax.axis_size("dp")
    my_index = lax.axis_index("dp")
    count = owner.shape[0]
    slots = factor.shape[2]
    order = jnp.arange(count)
    same = owner[:, None] == owner[None, :]
    slot = jnp.sum((same & (order[None, :] < order[:, None])).astype(jnp.int32), axis=1)
    hits = (owner[None, None, :] == jnp.arange(groups)[:, None, None]) & (
        slot[None, None, :] == jnp.arange(slots)[None, :, None]
    )
    hit_float = hits.astype(jnp.float32)
    my_hits = lax.dynamic_index_in_dim(hit_float, my_index, 0, keepdims=False)
    valid = jnp.sum(my_hits, axis=1)
    my_matrix = jnp.sum(my_hits.astype(jnp.int32) * order[None, :], axis=1)
    local = partials[0].astype(jnp.float32)
    summed = lax.psum(local, "dp")
    query_gradient = jnp.einsum("sm,mdc->sdc", my_hits, summed, precision=top_precision) / groups
    complete_eigvectors = lax.all_gather(basis[0], "mp", axis=0, tiled=True)
    turned_gradient = jnp.einsum(
        "tnu,ntg->nug", complete_eigvectors, query_gradient, precision=top_precision
    )
    leading_moment = 0.9 * moment1[0] + 0.1 * turned_gradient
    trailing_moment = 0.95 * moment2[0] + 0.05 * turned_gradient * turned_gradient
    direction = jnp.einsum(
        "uoh,ohz->ouz",
        complete_eigvectors,
        leading_moment / (jnp.sqrt(trailing_moment) + 1e-08),
        precision=top_precision,
    )
    held = master[0]
    weights = held - 0.1 * (direction + 0.1 * held)
    outer = lax.psum_scatter(
        jnp.einsum("src,sec->rse", query_gradient, query_gradient, precision=top_precision),
        "mp",
        scatter_dimension=0,
        tiled=True,
    )
    statistic = 0.95 * factor[0] + 0.05 * outer
    power = jnp.einsum("rse,esf->rsf", statistic, complete_eigvectors, precision=top_precision)
    total = lax.psum(jnp.sum(power * power, axis=(0, 2)), "mp")
    iterate = power / jnp.sqrt(total + 1e-06)[None, :, None]
    for step in range(NS_ITERS):
        gathered = lax.all_gather(iterate, "mp", axis=0, tiled=True)
        inner = jnp.einsum("rsf,esf->rse", iterate, gathered, precision=top_precision)
        inner_whole = lax.all_gather(inner, "mp", axis=0, tiled=True)
        squared = jnp.einsum("rse,esg->rsg", inner, inner_whole, precision=top_precision)
        merged_update = -4.775 * inner + 2.0315 * squared
        iterate = 3.4445 * iterate + jnp.einsum(
            "rse,esf->rsf", merged_update, gathered, precision=top_precision
        )
    new_basis = (iterate * valid[None, :, None])[None]
    block_rows = weights.shape[1] // groups
    columns = weights.shape[2]
    shaped = weights.reshape(slots, groups, block_rows, columns)
    chosen = jnp.take(rowblock, my_matrix, axis=0)
    sending = jnp.take_along_axis(shaped, chosen[:, :, None, None], axis=1)
    received = lax.all_to_all(sending, "dp", split_axis=1, concat_axis=0, tiled=True)
    train_weights = jnp.take(received, owner * slots + slot, axis=0)
    return (train_weights, new_basis)


def solution(mesh):
    placed = (
        P("dp", None, None, "mp"),
        P(),
        P(),
        P("dp", "mp", None, None),
        P("dp", "mp", None, None),
        P("dp", None, None, "mp"),
        P("dp", None, None, "mp"),
        P("dp", None, None, "mp"),
    )
    return jax.shard_map(
        body,
        mesh=mesh,
        in_specs=placed,
        out_specs=(P(None, "dp", None, "mp"), P("dp", "mp", None, None)),
        check_vma=False,
    )
```

profile of v0, /device:TPU:1, one launch (start us, length us, event | category | flops | bytes accessed | tf_op | source)
XLA Modules:
  0.0 822.0 jit_solution(15459246994509950012)
XLA Ops:
  7.2 5.6 bitcast_convert_fusion
  12.9 0.6 copy-done.17
  13.5 0.2 convert_reduce_fusion
  13.8 199.6 %all-reduce.4.cloned.1.call-done = f32[8,640,256]{2,0,1:T(8,128)} async-done(((f32[8,640,256]{2,0,1:T(8,128)}), f32[8,640,256]{2,0,1:T(8,128)}) %all-reduce.4.cloned.1.call-update) | async-done | bytes 5242896 | tf_op jit(solution)/shard_map/psum | solution.py:26
  213.4 5.0 fusion.54
  218.3 1.1 copy-done.10
  219.4 3.5 convolution_bitcast_fusion
  223.0 6.5 copy.101
  229.5 0.0 all-gather.27.cloned.1.call-start
  229.6 1.1 copy-done.15
  230.6 0.9 copy.92
  231.6 0.2 all-gather.11.cloned.1.call-start
  231.8 0.6 dynamic-slice
  233.1 80.0 %all-reduce.6.cloned.1.call-done = f32[640,2,640]{2,1,0:T(2,128)} async-done(((f32[640,2,640]{2,1,0:T(2,128)}), f32[640,2,640]{2,1,0:T(2,128)}) %all-reduce.6.cloned.1.call-update) | async-done | bytes 3276816
  313.1 2.0 fusion.44
  315.1 43.4 %all-gather.27.cloned.1.call-done = f32[1,640,2,640]{3,1,2,0:T(8,128)} async-done(((f32[1,160,2,640]{3,1,2,0:T(8,128)}), f32[1,640,2,640]{3,1,2,0:T(8,128)}) %all-gather.27.cloned.1.call-update) | async-done | bytes 3276816 | tf_op jit(solution)/shard_map/all_gather | solution.py:28
  358.5 4.7 multiply_reduce_fusion
  363.1 6.6 psum.15
  369.7 1.0 divide_bitcast_fusion
  370.8 44.7 %all-gather.11.cloned.1.call-done = f32[640,2,640]{2,0,1:T(8,128)} async-done(((f32[160,2,640]{2,0,1:T(8,128)}), f32[640,2,640]{2,0,1:T(8,128)}) %all-gather.11.cloned.1.call-update) | async-done | bytes 3276816 | tf_op jit(solution)/shard_map/all_gather | solution.py:53
  415.5 6.5 convolution_bitcast_fusion.8
  422.1 0.3 all-gather.15.cloned.1.call-start
  422.3 43.2 %all-gather.13.cloned.1.call-done = f32[640,2,640]{2,0,1:T(8,128)} async-done(((f32[160,2,640]{2,0,1:T(8,128)}), f32[640,2,640]{2,0,1:T(8,128)}) %all-gather.13.cloned.1.call-update) | async-done | bytes 3276816 | tf_op jit(solution)/shard_map/all_gather | solution.py:55
  465.6 5.3 fusion.43
  470.9 3.7 fusion.41
  474.7 43.5 %all-gather.15.cloned.1.call-done = f32[640,2,640]{2,0,1:T(8,128)} async-done(((f32[160,2,640]{2,0,1:T(8,128)}), f32[640,2,640]{2,0,1:T(8,128)}) %all-gather.15.cloned.1.call-update) | async-done | bytes 3276816 | tf_op jit(solution)/shard_map/all_gather | solution.py:53
  518.2 6.5 convolution_bitcast_fusion.6
  524.8 0.5 all-gather.19.cloned.1.call-start
  525.3 43.0 %all-gather.17.cloned.1.call-done = f32[640,2,640]{2,0,1:T(8,128)} async-done(((f32[160,2,640]{2,0,1:T(8,128)}), f32[640,2,640]{2,0,1:T(8,128)}) %all-gather.17.cloned.1.call-update) | async-done | bytes 3276816 | tf_op jit(solution)/shard_map/all_gather | solution.py:55
  568.3 5.3 fusion.40
  573.6 3.7 fusion.38
  577.4 43.5 %all-gather.19.cloned.1.call-done = f32[640,2,640]{2,0,1:T(8,128)} async-done(((f32[160,2,640]{2,0,1:T(8,128)}), f32[640,2,640]{2,0,1:T(8,128)}) %all-gather.19.cloned.1.call-update) | async-done | bytes 3276816 | tf_op jit(solution)/shard_map/all_gather | solution.py:53
  620.8 6.5 convolution_bitcast_fusion.4
  627.4 43.5 %all-gather.21.cloned.1.call-done = f32[640,2,640]{2,0,1:T(8,128)} async-done(((f32[160,2,640]{2,0,1:T(8,128)}), f32[640,2,640]{2,0,1:T(8,128)}) %all-gather.21.cloned.1.call-update) | async-done | bytes 3276816 | tf_op jit(solution)/shard_map/all_gather | solution.py:55
  670.9 5.3 fusion.37
  676.2 3.7 fusion.35
  679.9 0.2 all-gather.25.cloned.1.call-start
  680.2 0.1 fusion.58
  680.3 43.2 %all-gather.23.cloned.1.call-done = f32[640,2,640]{2,0,1:T(8,128)} async-done(((f32[160,2,640]{2,0,1:T(8,128)}), f32[640,2,640]{2,0,1:T(8,128)}) %all-gather.23.cloned.1.call-update) | async-done | bytes 3276816 | tf_op jit(solution)/shard_map/all_gather | solution.py:53
  723.5 6.5 convolution_bitcast_fusion.2
  730.1 0.6 gather_fusion
  730.6 0.1 fusion.61
  730.7 0.1 reshape.173
  730.8 1.5 copy.88
  732.3 2.9 copy.89
  735.2 2.8 copy.94
  738.0 0.1 compare_and_fusion
  738.1 0.1 copy.87
  738.2 5.6 fusion.6
  743.9 6.0 fusion.18
  749.9 2.6 copy.95
  752.5 1.6 copy.96
  754.1 2.5 gather_fusion.2
  756.6 2.2 copy_select_fusion
  758.8 10.8 %all-to-all-start = ((f32[2,64,10,256]{3,0,2,1:T(2,128)}), f32[2,64,10,256]{3,0,2,1:T(2,128)S(1)}, u32[]{:S(2)}, u32[]{:S(2)}) async-start(f32[2,64,10,256]{3,0,2,1:T(2,128)} %copy_select_fusion), calls=%async_computation | async-start | bytes 2621440 | tf_op jit(solution)/shard_map/all_to_all | solution.py:67
  769.6 0.1 convert_reduce_fusion.1
  769.8 34.0 %all-to-all-done = f32[2,64,10,256]{3,0,2,1:T(2,128)S(1)} async-done(((f32[2,64,10,256]{3,0,2,1:T(2,128)}), f32[2,64,10,256]{3,0,2,1:T(2,128)S(1)}, u32[]{:S(2)}, u32[]{:S(2)}) %all-to-all-start) | async-done | bytes 1310752 | tf_op jit(solution)/shard_map/all_to_all | solution.py:67
  803.8 0.3 copy.106
  804.0 0.6 gather_fusion.1
  804.6 0.1 bitcast_select_fusion
  804.7 0.7 copy.103
  805.4 5.4 fusion.34
  810.8 2.9 fusion.32
  813.7 1.5 copy.104
  (62 shorter events, 0.6 us)
Async XLA Ops:
  7.2 722.9 %copy-start = (s32[8,64]{1,0:T(8,128)S(1)}, s32[8,64]{1,0:T(8,128)}, u32[]{:S(2)}) copy-start(s32[8,64]{1,0:T(8,128)} %param.10) | copy-start | bytes 6148
  7.2 206.2 %all-reduce.4.cloned.1.call-start = ((), (), s32[]{:S(2)}) async-start(), calls=%async_computation.1 | async-start | bytes 10485760 | tf_op jit(solution)/shard_map/psum | solution.py:26
  12.9 0.7 copy-start.17
  12.9 300.2 %all-reduce.6.cloned.1.call-start = ((), (), s32[]{:S(2)}) async-start(), calls=%async_computation.11 | async-start | bytes 6553600
  218.3 1.1 copy-start.10
  229.5 1.1 copy-start.15
  229.5 2.3 copy-start.18
  229.5 83.6 %copy-start.16 = (f32[1,160,2,640]{3,2,1,0:T(2,128)S(1)}, f32[1,160,2,640]{3,2,1,0:T(2,128)}, u32[]{:S(2)}) copy-start(f32[1,160,2,640]{3,2,1,0:T(2,128)} %param.11) | copy-start | bytes 2457604
  229.5 129.0 %all-gather.27.cloned.1.call-start = ((), (), s32[]{:S(2)}) async-start(), calls=%async_computation.10 | async-start | bytes 4096000 | tf_op jit(solution)/shard_map/all_gather | solution.py:28
  231.6 183.9 %all-gather.11.cloned.1.call-start = ((), (), s32[]{:S(2)}) async-start(), calls=%async_computation.2 | async-start | bytes 4096000 | tf_op jit(solution)/shard_map/all_gather | solution.py:53
  370.8 94.8 %all-gather.13.cloned.1.call-start = ((), (), s32[]{:S(2)}) async-start(), calls=%async_computation.3 | async-start | bytes 4096000 | tf_op jit(solution)/shard_map/all_gather | solution.py:55
  422.1 48.9 %copy-start.3 = (f32[160,2,640]{2,0,1:T(8,128)S(1)}, f32[160,2,640]{2,0,1:T(8,128)}, u32[]{:S(2)}) copy-start(f32[160,2,640]{2,0,1:T(8,128)} %divide_bitcast_fusion) | copy-start | bytes 2457604
  422.1 96.1 %all-gather.15.cloned.1.call-start = ((), (), s32[]{:S(2)}) async-start(), calls=%async_computation.4 | async-start | bytes 4096000 | tf_op jit(solution)/shard_map/all_gather | solution.py:53
  465.6 5.4 copy-start.4
  474.7 93.6 %all-gather.17.cloned.1.call-start = ((), (), s32[]{:S(2)}) async-start(), calls=%async_computation.5 | async-start | bytes 4096000 | tf_op jit(solution)/shard_map/all_gather | solution.py:55
  524.8 48.8 %copy-start.5 = (f32[640,2,640]{2,0,1:T(8,128)S(1)}, f32[640,2,640]{2,0,1:T(8,128)}, u32[]{:S(2)}) copy-start(f32[640,2,640]{2,0,1:T(8,128)} %all-gather.15.cloned.1.call-done) | copy-start | bytes 9830404
  524.8 96.1 %all-gather.19.cloned.1.call-start = ((), (), s32[]{:S(2)}) async-start(), calls=%async_computation.6 | async-start | bytes 4096000 | tf_op jit(solution)/shard_map/all_gather | solution.py:53
  568.3 5.3 copy-start.8
  577.3 93.6 %all-gather.21.cloned.1.call-start = ((), (), s32[]{:S(2)}) async-start(), calls=%async_computation.7 | async-start | bytes 4096000 | tf_op jit(solution)/shard_map/all_gather | solution.py:55
  627.4 48.8 %copy-start.6 = (f32[640,2,640]{2,0,1:T(8,128)S(1)}, f32[640,2,640]{2,0,1:T(8,128)}, u32[]{:S(2)}) copy-start(f32[640,2,640]{2,0,1:T(8,128)} %all-gather.19.cloned.1.call-done) | copy-start | bytes 9830404
  627.4 96.1 %all-gather.23.cloned.1.call-start = ((), (), s32[]{:S(2)}) async-start(), calls=%async_computation.8 | async-start | bytes 4096000 | tf_op jit(solution)/shard_map/all_gather | solution.py:53
  670.9 5.3 copy-start.9
  679.9 125.5 %all-gather.25.cloned.1.call-start = ((), (), s32[]{:S(2)}) async-start(), calls=%async_computation.9 | async-start | bytes 4096000 | tf_op jit(solution)/shard_map/all_gather | solution.py:55
  680.3 50.5 %copy-start.14 = (f32[1,2,640,256]{3,2,1,0:T(8,128)S(1)}, f32[1,2,640,256]{3,2,1,0:T(8,128)}, u32[]{:S(2)}) copy-start(f32[1,2,640,256]{3,2,1,0:T(8,128)} %param.15) | copy-start | bytes 3932164
  732.3 5.9 copy-start.1
  738.2 5.7 copy-start.11
  738.2 5.7 copy-start.12
  738.2 5.7 copy-start.13
  758.8 45.0 %all-to-all-start = ((f32[2,64,10,256]{3,0,2,1:T(2,128)}), f32[2,64,10,256]{3,0,2,1:T(2,128)S(1)}, u32[]{:S(2)}, u32[]{:S(2)}) async-start(f32[2,64,10,256]{3,0,2,1:T(2,128)} %copy_select_fusion), calls=%async_computation | async-start | bytes 2621440 | tf_op jit(solution)/shard_map/all_to_all | solution.py:67
  804.6 6.2 copy-start.2
  805.4 5.4 copy-start.7
Sparse Core Ops, SparseCore 0:
  13.0 200.3 all-reduce.3
  229.6 83.3 all-reduce.5
  315.5 42.9 all-gather.26
  370.9 44.5 all-gather.10
  422.2 43.3 all-gather.12
  474.8 43.3 all-gather.14
  524.9 43.3 all-gather.16
  577.4 43.3 all-gather.18
  627.5 43.3 all-gather.20
  680.1 43.3 all-gather.22
  730.1 43.3 all-gather.24
where the time goes:
time: 829 us; the launch traced here: 822 us
  waiting for transfers between devices  662 us (80%)
  matrix products  86.2 us (10%)
  local copies, waits for them, and re-layouts  28.6 us (3%)
  between operations  15.1 us (2%)
  starting transfers between devices  12.3 us (1%)
  other arithmetic  11.6 us (1%)
    psum x1, waiting for transfers between devices, body(): summed = lax.psum(local, 'dp')  200 us
    all_gather x4, waiting for transfers between devices, body(): gathered = lax.all_gather(iterate, 'mp', axis=0, tiled=True)  175 us
    all_gather x4, waiting for transfers between devices, body(): inner_whole = lax.all_gather(inner, 'mp', axis=0, tiled=True)  130 us
    unnamed x12, waiting for transfers between devices  80.2 us
    all_gather x1, waiting for transfers between devices, body(): complete_eigvectors = lax.all_gather(basis[0], 'mp', axis=0, tiled=True)  43.4 us
    all_to_all x1, waiting for transfers between devices, body(): lax.all_to_all(sending, 'dp', split_axis=1, concat_axis=0, tiled=True)  34 us
    dot_general x4, matrix products, body(): jnp.einsum('rsf,esf->rse', iterate, gathered, precision=top_precision)  26.1 us
    dot_general x4, matrix products, body(): jnp.einsum('rse,esg->rsg', inner, inner_whole, precision=top_precision)  21.2 us
  transfers between devices with their start and end apart: 12, of which 11 were waited for; matrix products, arithmetic and copies ran while one was open for 4% of the time, Pallas kernels for 0%

commit v1 on v0

v1 whole, which is shorter than its diff:
```python
import jax
import jax.numpy as jnp
from jax import lax
from jax.experimental import pallas as pl
from jax.experimental.pallas import tpu as pltpu
from jax.sharding import PartitionSpec as P

NS_ITERS = 4
NT = (((1,), (1,)), ((), ()))
NN = (((1,), (0,)), ((), ()))


def split(x):
    hi = x.astype(jnp.bfloat16)
    lo = (x - hi.astype(jnp.float32)).astype(jnp.bfloat16)
    return hi, lo


def mm(left, right, dims):
    return lax.dot_general(left, right, dims, preferred_element_type=jnp.float32)


def refresh_kernel(g0, g1, g2, g3, f_ref, b_ref, o_ref, gl, gr, left, right, stack, x_ref):
    d = f_ref.shape[0]
    w = g0.shape[1]
    kc = 4 * w
    for b, g_ref in enumerate((g0, g1, g2, g3)):
        hi, lo = split(g_ref[...])
        gl[:, b * w:(b + 1) * w] = hi
        gl[:, kc + b * w:kc + (b + 1) * w] = hi
        gl[:, 2 * kc + b * w:2 * kc + (b + 1) * w] = lo
        gr[:, b * w:(b + 1) * w] = hi
        gr[:, kc + b * w:kc + (b + 1) * w] = lo
        gr[:, 2 * kc + b * w:2 * kc + (b + 1) * w] = hi

    def put_left(v):
        hi, lo = split(v)
        left[:, :d] = hi
        left[:, d:2 * d] = hi
        left[:, 2 * d:] = lo
        return hi, lo

    def put_right(hi, lo):
        right[:, :d] = hi
        right[:, d:2 * d] = lo
        right[:, 2 * d:] = hi

    def put_stack(hi, lo):
        stack[:d] = hi
        stack[d:2 * d] = lo
        stack[2 * d:] = hi

    outer = mm(gl[...], gr[...], NT)
    put_left(0.95 * f_ref[...] + 0.05 * outer)
    put_stack(*split(b_ref[...]))
    power = mm(left[...], stack[...], NN)
    total = jnp.sum(power * power)
    x_ref[...] = power / jnp.sqrt(jnp.full((1, 1), total + 1e-06, jnp.float32))

    def step(_, carry):
        hi, lo = put_left(x_ref[...])
        put_stack(hi, lo)
        put_right(hi, lo)
        inner = mm(left[...], right[...], NT)
        hi, lo = put_left(inner)
        put_right(hi, lo)
        squared = mm(left[...], right[...], NT)
        put_left(-4.775 * inner + 2.0315 * squared)
        x_ref[...] = 3.4445 * x_ref[...] + mm(left[...], stack[...], NN)
        return carry

    lax.fori_loop(0, NS_ITERS, step, 0)
    o_ref[...] = x_ref[...]


def refresh(pieces, f, b):
    d = f.shape[0]
    kc = 4 * pieces[0].shape[1]
    return pl.pallas_call(
        refresh_kernel,
        out_shape=jax.ShapeDtypeStruct((d, d), jnp.float32),
        in_specs=[pl.BlockSpec(memory_space=pltpu.VMEM)] * 6,
        out_specs=pl.BlockSpec(memory_space=pltpu.VMEM),
        scratch_shapes=[
            pltpu.VMEM((d, 3 * kc), jnp.bfloat16),
            pltpu.VMEM((d, 3 * kc), jnp.bfloat16),
            pltpu.VMEM((d, 3 * d), jnp.bfloat16),
            pltpu.VMEM((d, 3 * d), jnp.bfloat16),
            pltpu.VMEM((3 * d, d), jnp.bfloat16),
            pltpu.VMEM((d, d), jnp.float32),
        ],
        compiler_params=pltpu.CompilerParams(vmem_limit_bytes=40 << 20),
        cost_estimate=pl.CostEstimate(
            flops=6 * 14 * d**3, bytes_accessed=16 * d * d, transcendentals=0
        ),
        name="refresh",
    )(*pieces, f, b)


def body(partials, owner, rowblock, factor, basis, moment1, moment2, master):
    precision = lax.Precision.HIGH
    groups = lax.axis_size("dp")
    cols = lax.axis_size("mp")
    d = lax.axis_index("dp")
    y = lax.axis_index("mp")
    core = d % 2
    count = owner.shape[0]
    slots = factor.shape[2]
    rows = factor.shape[1]
    order = jnp.arange(count)
    same = owner[:, None] == owner[None, :]
    slot = jnp.sum((same & (order[None, :] < order[:, None])).astype(jnp.int32), axis=1)
    mine = (owner[None, :] == d) & (slot[None, :] == jnp.arange(slots)[:, None])
    valid = jnp.any(mine, axis=1)
    my_matrix = jnp.sum(jnp.where(mine, order[None, :], 0), axis=1)

    everyone = [(g, j) for g in range(groups) for j in range(cols)]

    def ring(shift, parity):
        return [
            (g * cols + j, g * cols + (j + shift) % cols)
            for g, j in everyone
            if parity is None or (j - g) % 2 == parity
        ]

    def move(x, shift, parity=None):
        return lax.ppermute(x, ("dp", "mp"), ring(shift, parity))

    def target_slot(at):
        return ((at - core) % cols) // 2

    even = (y - core) % 2 == 0
    own_slot = target_slot(y)
    left_slot = target_slot(y - 1)

    def pick(pair, which):
        return jnp.where(which == 0, pair[0], pair[1])

    def to_targets(pair):
        return (
            pick(pair, own_slot),
            move(pick(pair, left_slot), -1, 1),
            move(pick(pair, 1 - own_slot), 2, 0),
            move(pick(pair, 1 - left_slot), 1, 1),
        )

    def in_order(blocks):
        whole = jnp.concatenate(blocks + blocks, axis=0)
        start = ((cols - y) % cols) * rows
        return lax.dynamic_slice_in_dim(whole, start, cols * rows, 0)

    factor_full = in_order(to_targets((factor[0, :, 0], factor[0, :, 1])))
    basis_rows = jnp.concatenate([basis[0, :, 0], basis[0, :, 1]], axis=1)
    basis_full = in_order(
        (
            basis_rows,
            move(basis_rows, -1),
            move(basis_rows, 2),
            move(basis_rows, 1),
        )
    )
    wide = basis_full.shape[1] // 2
    bases = (basis_full[:, :wide], basis_full[:, wide:])

    summed = lax.psum(partials[0].astype(jnp.float32), "dp")
    gradients = tuple(
        lax.dynamic_index_in_dim(summed, my_matrix[s], 0, keepdims=False) / groups
        for s in range(slots)
    )

    pieces = to_targets(gradients)
    refreshed = refresh(pieces, factor_full, pick(bases, own_slot))

    sent = []
    for s in range(slots):
        turned = lax.dot_general(
            bases[s], gradients[s], (((0,), (0,)), ((), ())), precision=precision
        )
        first = 0.9 * moment1[0, s] + 0.1 * turned
        second = 0.95 * moment2[0, s] + 0.05 * turned * turned
        direction = lax.dot_general(
            bases[s], first / (jnp.sqrt(second) + 1e-08), NN, precision=precision
        )
        held = master[0, s]
        weights = held - 0.1 * (direction + 0.1 * held)
        block_rows = weights.shape[0] // groups
        shaped = weights.reshape(groups, block_rows, weights.shape[1])
        chosen = lax.dynamic_index_in_dim(rowblock, my_matrix[s], 0, keepdims=False)
        sent.append(jnp.take(shaped, chosen, axis=0))
    received = lax.all_to_all(
        jnp.stack(sent, axis=0), "dp", split_axis=1, concat_axis=0, tiled=True
    )
    train_weights = jnp.take(received, owner * slots + slot, axis=0)

    keep = jnp.where(own_slot == 0, valid[0], valid[1])
    refreshed = jnp.where(keep, refreshed, 0.0)

    def row_block(at):
        return lax.dynamic_slice_in_dim(refreshed, ((at + cols) % cols) * rows, rows, 0)

    own = row_block(y)
    from_left = move(row_block(y + 1), 1, 0)
    from_far = move(row_block(y + 2), 2, 0)
    from_right = move(row_block(y - 1), -1, 0)
    near = jnp.where(even, own, from_left)
    far = jnp.where(even, from_far, from_right)
    near_first = jnp.where(even, own_slot, left_slot) == 0
    new_basis = jnp.stack(
        [jnp.where(near_first, near, far), jnp.where(near_first, far, near)], axis=1
    )
    return (train_weights, new_basis[None])


def solution(mesh):
    placed = (
        P("dp", None, None, "mp"),
        P(),
        P(),
        P("dp", "mp", None, None),
        P("dp", "mp", None, None),
        P("dp", None, None, "mp"),
        P("dp", None, None, "mp"),
        P("dp", None, None, "mp"),
    )
    return jax.shard_map(
        body,
        mesh=mesh,
        in_specs=placed,
        out_specs=(P(None, "dp", None, "mp"), P("dp", "mp", None, None)),
        check_vma=False,
    )
```

time: 829 us -> 338 us (0.41)
  waiting for transfers between devices: 662 us -> 174 us
  matrix products: 86.2 us -> 14.3 us
  Pallas kernels: 0 us -> 38.1 us
  starting transfers between devices: 12.3 us -> 32.7 us
  local copies, waits for them, and re-layouts: 28.6 us -> 40.1 us
    all_gather x9 -> x0, waiting for transfers between devices: 348 us -> none  [the longest x4 175 us: body(): gathered = lax.all_gather(iterate, 'mp', axis=0, tiled=True)]
    unnamed x12 -> x1, waiting for transfers between devices: 80.2 us -> 0.02 us
    dot_general x17 -> x4, matrix products: 86.2 us -> 14.3 us  [the longest x2 8.19 us: body(): lax.dot_general(bases[s], first / (jnp.sqrt(second) + 1e-08), NN, precisi...]
    psum x1, waiting for transfers between devices: 200 us -> 129 us  [body(): summed = lax.psum(partials[0].astype(jnp.float32), 'dp')]
    ppermute x0 -> x12, waiting for transfers between devices: none -> 45.6 us  [move(): return lax.ppermute(x, ('dp', 'mp'), ring(shift, parity))]
    pallas_call x0 -> x1, Pallas kernels: none -> 38.1 us  [refresh(): pl.pallas_call(refresh_kernel, out_shape=jax.ShapeDtypeStruct((d, d), jnp...]
    all_to_all x1, waiting for transfers between devices: 34 us -> 0.01 us  [body(): lax.all_to_all(jnp.stack(sent, axis=0), 'dp', split_axis=1, concat_axis=0...]
    ppermute x0 -> x12, starting transfers between devices: none -> 24 us  [move(): return lax.ppermute(x, ('dp', 'mp'), ring(shift, parity))]
  transfers between devices with their start and end apart: 12 -> 14, of which waited for: 11 -> 4; matrix products, arithmetic and copies ran while one was open for 4% -> 13% of each run, Pallas kernels for 0% -> 11%
where the time goes in v1:
time: 338 us; the launch traced here: 337 us
  waiting for transfers between devices  174 us (51%)
  local copies, waits for them, and re-layouts  40.1 us (12%)
  Pallas kernels  38.1 us (11%)
  starting transfers between devices  32.7 us (10%)
  between operations  19.3 us (6%)
  other arithmetic  18.3 us (5%)
  matrix products  14.3 us (4%)
    psum x1, waiting for transfers between devices, body(): summed = lax.psum(partials[0].astype(jnp.float32), 'dp')  129 us
    ppermute x12, waiting for transfers between devices, move(): return lax.ppermute(x, ('dp', 'mp'), ring(shift, parity))  45.6 us
    pallas_call x1, Pallas kernels, refresh(): pl.pallas_call(refresh_kernel, out_shape=jax.ShapeDtypeStruct((d, d), jnp...  38.1 us
    ppermute x12, starting transfers between devices, move(): return lax.ppermute(x, ('dp', 'mp'), ring(shift, parity))  24 us
    unnamed x20, local copies, waits for them, and re-layouts  16.5 us
    all_to_all x1, starting transfers between devices, body(): lax.all_to_all(jnp.stack(sent, axis=0), 'dp', split_axis=1, concat_axis=0...  8.71 us
    dot_general x2, matrix products, body(): lax.dot_general(bases[s], first / (jnp.sqrt(second) + 1e-08), NN, precisi...  8.19 us
  transfers between devices with their start and end apart: 14, of which 4 were waited for; matrix products, arithmetic and copies ran while one was open for 13% of the time, Pallas kernels for 11%

profile of v1, /device:TPU:1, one launch (start us, length us, event | category | flops | bytes accessed | tf_op | source)
XLA Modules:
  0.0 337.2 jit_solution(13856070240647416161)
XLA Ops:
  7.2 2.2 fusion.82
  9.5 1.3 pad_maximum_fusion.1
  10.8 3.6 %collective-permute-start = (f32[160,1280]{1,0:T(8,128)}, f32[160,1280]{1,0:T(8,128)S(1)}, u32[]{:S(2)}, u32[]{:S(2)}) collective-permute-start(f32[160,1280]{1,0:T(8,128)} %get-tuple-element.33), channel_id=1, source_target_pairs={{0,3},{1,0},{2,1},{3,2},{4,7},{5,4},{6,5},{7,6},{8,11},{9,8},{10,9... | collective-permute-start | bytes 2457608 | tf_op jit(solution)/shard_map/ppermute | solution.py:127
  14.4 0.3 collective-permute-start.1
  14.7 2.7 bitcast_convert_fusion
  17.6 1.0 copy-done.2
  18.6 0.6 fusion.81
  19.2 1.1 select_bitcast_fusion.4
  20.4 2.5 collective-permute-start.6
  22.9 0.7 collective-permute-start.7
  23.6 3.8 %collective-permute-start.8 = (f32[160,640]{1,0:T(8,128)}, f32[160,640]{1,0:T(8,128)}, u32[]{:S(2)}, u32[]{:S(2)}) collective-permute-start(f32[160,640]{1,0:T(8,128)} %get-tuple-element.28), channel_id=1, source_target_pairs={{1,2},{3,0},{4,5},{6,7},{9,10},{11,8},{12,13},{14,15},{17,18},{19,... | collective-permute-start | bytes 1228808 | tf_op jit(solution)/shard_map/ppermute | solution.py:127
  27.7 0.6 fusion.84
  30.8 0.8 bitcast_dynamic-update-slice_fusion
  32.9 0.6 fusion.83
  33.5 0.8 compare_and_fusion.1
  35.5 23.6 %collective-permute-done.6 = f32[160,640]{1,0:T(8,128)S(1)} collective-permute-done((f32[160,640]{1,0:T(8,128)}, f32[160,640]{1,0:T(8,128)S(1)}, u32[]{:S(2)}, u32[]{:S(2)}) %collective-permute-start.6) | collective-permute-done | bytes 409632 | tf_op jit(solution)/shard_map/ppermute | solution.py:127
  59.1 0.8 collective-permute-start.2
  59.8 0.8 constant_dynamic-update-slice_fusion.13
  60.6 0.8 constant_dynamic-update-slice_fusion.12
  61.4 1.8 constant_dynamic-update-slice_fusion.11
  63.2 0.8 bitcast_dynamic-update-slice_fusion.1
  64.0 0.8 constant_dynamic-update-slice_fusion.10
  64.8 0.8 constant_dynamic-update-slice_fusion.9
  65.6 1.8 constant_dynamic-update-slice_fusion.8
  67.4 1.5 constant_dynamic-slice_fusion.3.f_ref
  68.9 1.0 constant_dynamic-update-slice_fusion.6
  70.0 2.1 constant_dynamic-update-slice_fusion.5
  72.1 8.6 %collective-permute-done.2 = f32[160,1280]{1,0:T(8,128)S(1)} collective-permute-done((f32[160,1280]{1,0:T(8,128)}, f32[160,1280]{1,0:T(8,128)S(1)}, u32[]{:S(2)}, u32[]{:S(2)}) %collective-permute-start.2) | collective-permute-done | bytes 819232 | tf_op jit(solution)/shard_map/ppermute | solution.py:127
  80.7 0.9 constant_dynamic-update-slice_fusion.4
  81.7 1.0 constant_dynamic-update-slice_fusion.3
  82.6 1.0 constant_dynamic-update-slice_fusion.2
  83.6 2.1 constant_dynamic-update-slice_fusion.1
  85.7 1.0 constant_dynamic-update-slice_fusion
  86.7 2.1 dynamic-slice_select_fusion.b_ref
  88.8 128.6 %all-reduce.2.cloned.1.call-done = f32[8,640,256]{2,1,0:T(8,128)} async-done(((f32[8,640,256]{2,1,0:T(8,128)}), f32[8,640,256]{2,1,0:T(8,128)}) %all-reduce.2.cloned.1.call-update) | async-done | bytes 5242896 | tf_op jit(solution)/shard_map/psum | solution.py:165
  217.4 3.1 fusion.6
  220.5 4.1 %fusion.23 = f32[640,256]{1,0:T(8,128)} fusion(f32[1280,1280]{1,0:T(8,128)} %constant_dynamic-update-slice_fusion, s32[]{:T(128)S(6)} %select_n.211, s32[]{:T(128)S(6)} %add.153, f32[640,256]{1,0:T(8,128)S(1)} %fusion.6, f32[1,2,640,256]{3,2,1,0:T(8,128)} %param.16, f32[1,2,640,256]{3,2,1,0:T(8,128)} %param.15, f32[1,2,640,256]{3,2,1,0:T(8,128)} %param.17), kind=kOutput, calls=%fused_computation.19 | convolution fusion | flops 631275520 | bytes 4915208 | tf_op jit(solution)/shard_map/dot_general | solution.py:181
  224.6 2.2 reshape.56
  226.8 3.1 fusion.2
  229.9 4.1 %fusion.17 = f32[640,256]{1,0:T(8,128)} fusion(f32[1280,1280]{1,0:T(8,128)} %constant_dynamic-update-slice_fusion, s32[]{:T(128)S(6)} %select_n.211, f32[640,256]{1,0:T(8,128)S(1)} %fusion.2, f32[1,2,640,256]{3,2,1,0:T(8,128)} %param.16, f32[1,2,640,256]{3,2,1,0:T(8,128)} %param.15, f32[1,2,640,256]{3,2,1,0:T(8,128)} %param.17), kind=kOutput, calls=%fused_computation.17 | convolution fusion | flops 631275520 | bytes 4915204 | tf_op jit(solution)/shard_map/dot_general | solution.py:181
  234.0 2.2 reshape.55
  236.1 3.0 bitcast_select_fusion
  239.2 5.2 %collective-permute-start.3 = (f32[640,256]{1,0:T(8,128)}, f32[640,256]{1,0:T(8,128)}, u32[]{:S(2)}, u32[]{:S(2)}) collective-permute-start(f32[640,256]{1,0:T(8,128)} %get-tuple-element.21), channel_id=1, source_target_pairs={{1,0},{3,2},{4,7},{6,5},{9,8},{11,10},{12,15},{14,13},{17,16},{19,... | collective-permute-start | bytes 1966088 | tf_op jit(solution)/shard_map/ppermute | solution.py:127
  244.4 1.5 collective-permute-start.4
  245.9 2.3 collective-permute-start.5
  248.2 2.8 gather_fusion.2
  251.0 2.8 gather_fusion.1
  253.8 1.4 select_bitcast_fusion
  255.2 1.4 select_bitcast_fusion.1
  256.6 0.2 pad_maximum_fusion
  256.8 2.2 copy.43
  259.0 8.7 %all-to-all-start = ((f32[2,64,10,256]{3,0,2,1:T(2,128)}), f32[2,64,10,256]{3,0,2,1:T(2,128)}, u32[]{:S(2)}, u32[]{:S(2)}) async-start(f32[2,64,10,256]{3,0,2,1:T(2,128)} %copy.43), calls=%async_computation | async-start | bytes 2621440 | tf_op jit(solution)/shard_map/all_to_all | solution.py:190
  267.8 1.1 copy-done
  268.9 38.1 %refresh.1 = f32[640,640]{1,0:T(8,128)S(1)} custom-call(f32[640,256]{1,0:T(8,128)S(1)} %copy-done, f32[640,256]{1,0:T(8,128)} %collective-permute-done.3.g1, f32[640,256]{1,0:T(8,128)} %collective-permute-done.4.g2, f32[640,256]{1,0:T(8,128)} %collective-permute-done.5.g3, f32[640,640]{1,0:T(8,128)S(1)} %constant_dynamic-slice_fusion.3.f_ref, ...), custom_call_target="tpu_custom_call" | custom-call | flops 22020096000 | bytes 6553600 | tf_op jit(solution)/shard_map/refresh/pallas_call | solution.py:79
  307.1 0.8 constant_dynamic-slice_fusion.2
  307.9 0.7 collective-permute-start.10
  308.6 1.3 collective-permute-start.11
  309.9 1.3 collective-permute-start.9
  311.3 13.4 %collective-permute-done.11 = f32[160,640]{1,0:T(8,128)S(1)} collective-permute-done((f32[160,640]{1,0:T(8,128)S(1)}, f32[160,640]{1,0:T(8,128)S(1)}, u32[]{:S(2)}, u32[]{:S(2)}) %collective-permute-start.11) | collective-permute-done | bytes 409632 | tf_op jit(solution)/shard_map/ppermute | solution.py:127
  324.7 1.1 select_bitcast_fusion.3
  325.8 1.5 copy.50
  327.4 1.6 copy.51
  329.0 0.6 gather_fusion
  329.6 0.7 copy.49
  (28 shorter events, 0.8 us)
Async XLA Ops:
  7.2 210.3 %all-reduce.2.cloned.1.call-start = ((), (), s32[]{:S(2)}) async-start(), calls=%async_computation.1 | async-start | bytes 10485760 | tf_op jit(solution)/shard_map/psum | solution.py:165
  7.2 7.5 %copy-start.1 = (bf16[1,8,640,256]{3,2,1,0:T(8,128)(2,1)S(1)}, bf16[1,8,640,256]{3,2,1,0:T(8,128)(2,1)}, u32[]{:S(2)}) copy-start(bf16[1,8,640,256]{3,2,1,0:T(8,128)(2,1)} %param.10) | copy-start | bytes 7864324
  10.8 58.1 %collective-permute-start = (f32[160,1280]{1,0:T(8,128)}, f32[160,1280]{1,0:T(8,128)S(1)}, u32[]{:S(2)}, u32[]{:S(2)}) collective-permute-start(f32[160,1280]{1,0:T(8,128)} %get-tuple-element.33), channel_id=1, source_target_pairs={{0,3},{1,0},{2,1},{3,2},{4,7},{5,4},{6,5},{7,6},{8,11},{9,8},{10,9... | collective-permute-start | bytes 2457608 | tf_op jit(solution)/shard_map/ppermute | solution.py:127
  14.4 55.6 %collective-permute-start.1 = (f32[160,1280]{1,0:T(8,128)}, f32[160,1280]{1,0:T(8,128)}, u32[]{:S(2)}, u32[]{:S(2)}) collective-permute-start(f32[160,1280]{1,0:T(8,128)} %get-tuple-element.33), channel_id=1, source_target_pairs={{0,2},{1,3},{2,0},{3,1},{4,6},{5,7},{6,4},{7,5},{8,10},{9,11},{10,... | collective-permute-start | bytes 2457608 | tf_op jit(solution)/shard_map/ppermute | solution.py:127
  17.4 1.1 copy-start.2
  17.4 10.0 %copy-start.3 = (s32[8]{0:T(128)S(1)}, s32[8]{0:T(128)}, u32[]{:S(2)}) copy-start(s32[8]{0:T(128)} %param.11) | copy-start | bytes 100
  20.4 38.7 %collective-permute-start.6 = (f32[160,640]{1,0:T(8,128)}, f32[160,640]{1,0:T(8,128)S(1)}, u32[]{:S(2)}, u32[]{:S(2)}) collective-permute-start(f32[160,640]{1,0:T(8,128)} %get-tuple-element.29), channel_id=1, source_target_pairs={{1,0},{3,2},{4,7},{6,5},{9,8},{11,10},{12,15},{14,13},{17,16},{19,... | collective-permute-start | bytes 1228808 | tf_op jit(solution)/shard_map/ppermute | solution.py:127
  22.9 37.7 %collective-permute-start.7 = (f32[160,640]{1,0:T(8,128)}, f32[160,640]{1,0:T(8,128)S(1)}, u32[]{:S(2)}, u32[]{:S(2)}) collective-permute-start(f32[160,640]{1,0:T(8,128)} %get-tuple-element.30), channel_id=1, source_target_pairs={{0,2},{2,0},{5,7},{7,5},{8,10},{10,8},{13,15},{15,13},{16,18},{18,... | collective-permute-start | bytes 1228808 | tf_op jit(solution)/shard_map/ppermute | solution.py:127
  23.6 37.8 %collective-permute-start.8 = (f32[160,640]{1,0:T(8,128)}, f32[160,640]{1,0:T(8,128)}, u32[]{:S(2)}, u32[]{:S(2)}) collective-permute-start(f32[160,640]{1,0:T(8,128)} %get-tuple-element.28), channel_id=1, source_target_pairs={{1,2},{3,0},{4,5},{6,7},{9,10},{11,8},{12,13},{14,15},{17,18},{19,... | collective-permute-start | bytes 1228808 | tf_op jit(solution)/shard_map/ppermute | solution.py:127
  59.1 21.7 %collective-permute-start.2 = (f32[160,1280]{1,0:T(8,128)}, f32[160,1280]{1,0:T(8,128)S(1)}, u32[]{:S(2)}, u32[]{:S(2)}) collective-permute-start(f32[160,1280]{1,0:T(8,128)} %get-tuple-element.33), channel_id=1, source_target_pairs={{0,1},{1,2},{2,3},{3,0},{4,5},{5,6},{6,7},{7,4},{8,9},{9,10},{10,1... | collective-permute-start | bytes 2457608 | tf_op jit(solution)/shard_map/ppermute | solution.py:127
  239.2 28.5 %collective-permute-start.3 = (f32[640,256]{1,0:T(8,128)}, f32[640,256]{1,0:T(8,128)}, u32[]{:S(2)}, u32[]{:S(2)}) collective-permute-start(f32[640,256]{1,0:T(8,128)} %get-tuple-element.21), channel_id=1, source_target_pairs={{1,0},{3,2},{4,7},{6,5},{9,8},{11,10},{12,15},{14,13},{17,16},{19,... | collective-permute-start | bytes 1966088 | tf_op jit(solution)/shard_map/ppermute | solution.py:127
  244.4 23.3 %collective-permute-start.4 = (f32[640,256]{1,0:T(8,128)}, f32[640,256]{1,0:T(8,128)}, u32[]{:S(2)}, u32[]{:S(2)}) collective-permute-start(f32[640,256]{1,0:T(8,128)} %get-tuple-element.20), channel_id=1, source_target_pairs={{0,2},{2,0},{5,7},{7,5},{8,10},{10,8},{13,15},{15,13},{16,18},{18,... | collective-permute-start | bytes 1966088 | tf_op jit(solution)/shard_map/ppermute | solution.py:127
  245.9 21.8 %collective-permute-start.5 = (f32[640,256]{1,0:T(8,128)}, f32[640,256]{1,0:T(8,128)}, u32[]{:S(2)}, u32[]{:S(2)}) collective-permute-start(f32[640,256]{1,0:T(8,128)} %get-tuple-element.19), channel_id=1, source_target_pairs={{1,2},{3,0},{4,5},{6,7},{9,10},{11,8},{12,13},{14,15},{17,18},{19,... | collective-permute-start | bytes 1966088 | tf_op jit(solution)/shard_map/ppermute | solution.py:127
  259.0 68.4 %all-to-all-start = ((f32[2,64,10,256]{3,0,2,1:T(2,128)}), f32[2,64,10,256]{3,0,2,1:T(2,128)}, u32[]{:S(2)}, u32[]{:S(2)}) async-start(f32[2,64,10,256]{3,0,2,1:T(2,128)} %copy.43), calls=%async_computation | async-start | bytes 2621440 | tf_op jit(solution)/shard_map/all_to_all | solution.py:190
  267.8 1.1 copy-start
  307.9 3.3 collective-permute-start.10
  308.6 16.1 %collective-permute-start.11 = (f32[160,640]{1,0:T(8,128)S(1)}, f32[160,640]{1,0:T(8,128)S(1)}, u32[]{:S(2)}, u32[]{:S(2)}) collective-permute-start(f32[160,640]{1,0:T(8,128)S(1)} %get-tuple-element.26), channel_id=1, source_target_pairs={{0,3},{2,1},{5,4},{7,6},{8,11},{10,9},{13,12},{15,14},{16,19},{18,... | collective-permute-start | bytes 1228808 | tf_op jit(solution)/shard_map/ppermute | solution.py:127
  309.9 14.8 %collective-permute-start.9 = (f32[160,640]{1,0:T(8,128)S(1)}, f32[160,640]{1,0:T(8,128)}, u32[]{:S(2)}, u32[]{:S(2)}) collective-permute-start(f32[160,640]{1,0:T(8,128)S(1)} %get-tuple-element.25), channel_id=1, source_target_pairs={{0,1},{2,3},{5,6},{7,4},{8,9},{10,11},{13,14},{15,12},{16,17},{18,... | collective-permute-start | bytes 1228808 | tf_op jit(solution)/shard_map/ppermute | solution.py:127
Sparse Core Ops, SparseCore 0:
  17.6 199.8 all-reduce.1

commit v2 on v1

--- a/solution.py
+++ b/solution.py
@@ -5,7 +5,10 @@
 from jax.experimental.pallas import tpu as pltpu
 from jax.sharding import PartitionSpec as P
 
+
 NS_ITERS = 4
+SLOTS = 2
+NX, NZ, NC = 4, 8, 2
 NT = (((1,), (1,)), ((), ()))
 NN = (((1,), (0,)), ((), ()))
 
@@ -97,6 +100,43 @@
     )(*pieces, f, b)
 
 
+def line(x, z, core):
+    return (x * NZ + z) * NC + core
+
+
+def owned_gradients(local, owner, slot, d):
+    x, core = d // (NZ * NC), d % NC
+    count, rows, cols = local.shape
+    part = rows // NZ
+    paired = local.reshape(NX, NC, rows, cols)
+    others = lax.dynamic_index_in_dim(paired, 1 - core, 1, keepdims=False)
+    kept = lax.dynamic_index_in_dim(paired, core, 1, keepdims=False)
+    swap = [(line(a, b, c), line(a, b, 1 - c)) for a in range(NX) for b in range(NZ) for c in range(NC)]
+    came = lax.ppermute(others.astype(jnp.float32), "dp", swap)
+    chip = kept.astype(jnp.float32) + came
+    along_x = [[line(a, b, c) for a in range(NX)] for b in range(NZ) for c in range(NC)]
+    along_z = [[line(a, b, c) for b in range(NZ)] for a in range(NX) for c in range(NC)]
+    across = [[line(a, b, c) for a in range(NX) for c in range(NC)] for b in range(NZ)]
+
+    def exchange(v, lines):
+        return lax.all_to_all(v, "dp", 0, 0, axis_index_groups=lines, tiled=True)
+
+    over_x = jnp.sum(exchange(chip, along_x), axis=0)
+    over_z = jnp.sum(exchange(over_x.reshape(NZ, part, cols), along_z), axis=0)
+    mean = over_z * (1.0 / (NX * NZ * NC))
+    everything = exchange(jnp.broadcast_to(mean[None], (count, part, cols)), across)
+    groups = NX * NZ * NC
+    hits = (owner[None, None, :] == jnp.arange(groups)[:, None, None]) & (
+        slot[None, None, :] == jnp.arange(SLOTS)[None, :, None]
+    )
+    matrix_of = jnp.sum(jnp.where(hits, jnp.arange(count)[None, None, :], 0), axis=2)
+    wanted = lax.dynamic_index_in_dim(matrix_of.reshape(NX, NZ, NC, SLOTS), x, 0, keepdims=False)
+    wanted = lax.dynamic_index_in_dim(wanted, core, 1, keepdims=False)
+    outgoing = jnp.take(everything, wanted.reshape(-1), axis=0, mode="clip")
+    incoming = exchange(outgoing.reshape(NZ, SLOTS, part, cols), along_z)
+    return tuple(incoming[:, s].reshape(rows, cols) for s in range(SLOTS))
+
+
 def body(partials, owner, rowblock, factor, basis, moment1, moment2, master):
     precision = lax.Precision.HIGH
     groups = lax.axis_size("dp")
@@ -162,12 +202,7 @@
     wide = basis_full.shape[1] // 2
     bases = (basis_full[:, :wide], basis_full[:, wide:])
 
-    summed = lax.psum(partials[0].astype(jnp.float32), "dp")
-    gradients = tuple(
-        lax.dynamic_index_in_dim(summed, my_matrix[s], 0, keepdims=False) / groups
-        for s in range(slots)
-    )
-
+    gradients = owned_gradients(partials[0], owner, slot, d)
     pieces = to_targets(gradients)
     refreshed = refresh(pieces, factor_full, pick(bases, own_slot))
 

time: 338 us -> 245 us (0.72)
  waiting for transfers between devices: 174 us -> 58.1 us
  starting transfers between devices: 32.7 us -> 52.5 us
  local copies, waits for them, and re-layouts: 40.1 us -> 53.6 us
  between operations: 19.3 us -> 6.15 us
  other arithmetic: 18.3 us -> 22.2 us
    psum x1 -> x0, waiting for transfers between devices: 129 us -> none  [body(): summed = lax.psum(partials[0].astype(jnp.float32), 'dp')]
    all_to_all x0 -> x4, waiting for transfers between devices: none -> 39 us  [exchange(): return lax.all_to_all(v, 'dp', 0, 0, axis_index_groups=lines, tiled=True)]
    ppermute x12, waiting for transfers between devices: 45.6 us -> 15.8 us  [move(): return lax.ppermute(x, ('dp', 'mp'), ring(shift, parity))]
    all_to_all x0 -> x4, starting transfers between devices: none -> 20.4 us  [exchange(): return lax.all_to_all(v, 'dp', 0, 0, axis_index_groups=lines, tiled=True)]
    unnamed x20 -> x50, local copies, waits for them, and re-layouts: 16.5 us -> 23.6 us
    all_to_all x1, starting transfers between devices: 8.71 us -> 5.28 us  [body(): lax.all_to_all(jnp.stack(sent, axis=0), 'dp', split_axis=1, concat_axis=0...]
  transfers between devices with their start and end apart: 14 -> 18, of which waited for: 4 -> 8; matrix products, arithmetic and copies ran while one was open for 13% -> 22% of each run, Pallas kernels for 11% -> 16%
where the time goes in v2:
time: 245 us; the launch traced here: 244 us
  waiting for transfers between devices  58.1 us (24%)
  local copies, waits for them, and re-layouts  53.6 us (22%)
  starting transfers between devices  52.5 us (21%)
  Pallas kernels  38.1 us (16%)
  other arithmetic  22.2 us (9%)
  matrix products  13 us (5%)
  between operations  6.15 us (3%)
    all_to_all x4, waiting for transfers between devices, exchange(): return lax.all_to_all(v, 'dp', 0, 0, axis_index_groups=lines, tiled=True)  39 us
    pallas_call x1, Pallas kernels, refresh(): pl.pallas_call(refresh_kernel, out_shape=jax.ShapeDtypeStruct((d, d), jnp...  38.1 us
    ppermute x12, starting transfers between devices, move(): return lax.ppermute(x, ('dp', 'mp'), ring(shift, parity))  23.7 us
    unnamed x50, local copies, waits for them, and re-layouts  23.6 us
    all_to_all x4, starting transfers between devices, exchange(): return lax.all_to_all(v, 'dp', 0, 0, axis_index_groups=lines, tiled=True)  20.4 us
    ppermute x12, waiting for transfers between devices, move(): return lax.ppermute(x, ('dp', 'mp'), ring(shift, parity))  15.8 us
    dot_general x2, matrix products, body(): lax.dot_general(bases[s], first / (jnp.sqrt(second) + 1e-08), NN, precisi...  7.16 us
    select_n x3, other arithmetic, pick(): return jnp.where(which == 0, pair[0], pair[1])  6.4 us
  transfers between devices with their start and end apart: 18, of which 8 were waited for; matrix products, arithmetic and copies ran while one was open for 22% of the time, Pallas kernels for 16%

profile of v2, /device:TPU:1, one launch (start us, length us, event | category | flops | bytes accessed | tf_op | source)
XLA Modules:
  0.0 243.6 jit_solution(9238109898922510815)
XLA Ops:
  0.7 3.1 %bitcast_convert_fusion = f32[4,640,256]{2,1,0:T(8,128)} fusion(bf16[4,2,640,256]{3,2,1,0:T(8,128)(2,1)} %bitcast.104, s32[]{:T(128)S(6)} %select_n.237), kind=kLoop, calls=%fused_computation.15 | loop fusion | flops 655360 | bytes 3932164 | tf_op jit(solution)/shard_map/convert_element_type | solution.py:115
  3.8 3.2 %collective-permute-start.3 = (f32[4,640,256]{2,1,0:T(8,128)}, f32[4,640,256]{2,1,0:T(8,128)S(1)}, u32[]{:S(2)}, u32[]{:S(2)}) collective-permute-start(f32[4,640,256]{2,1,0:T(8,128)} %bitcast_convert_fusion), channel_id=1, source_target_pairs={{0,4},{4,0},{8,12},{12,8},{16,20},{20,16},{24,28},{28,24},{32,36},... | collective-permute-start | bytes 7864328 | tf_op jit(solution)/shard_map/ppermute | solution.py:115
  7.0 1.5 fusion.76
  8.5 3.2 %collective-permute-done.3 = f32[4,640,256]{2,1,0:T(8,128)S(1)} collective-permute-done((f32[4,640,256]{2,1,0:T(8,128)}, f32[4,640,256]{2,1,0:T(8,128)S(1)}, u32[]{:S(2)}, u32[]{:S(2)}) %collective-permute-start.3) | collective-permute-done | bytes 2621472 | tf_op jit(solution)/shard_map/ppermute | solution.py:115
  11.7 3.2 %convert_add_fusion = f32[4,640,256]{2,1,0:T(8,128)} fusion(f32[4,640,256]{2,1,0:T(8,128)S(1)} %collective-permute-done.3, bf16[4,2,640,256]{3,2,1,0:T(8,128)(2,1)} %bitcast.105, s32[]{:T(128)S(6)} %select_n.236), kind=kLoop, calls=%fused_computation.4 | loop fusion | flops 1310720 | bytes 6553604 | tf_op jit(solution)/shard_map/add | solution.py:116
  14.9 3.8 %all-to-all-start = ((f32[4,640,256]{2,1,0:T(8,128)}), f32[4,640,256]{2,1,0:T(8,128)S(1)}, u32[]{:S(2)}, u32[]{:S(2)}) async-start(f32[4,640,256]{2,1,0:T(8,128)} %convert_add_fusion), calls=%async_computation | async-start | bytes 5242880 | tf_op jit(solution)/shard_map/all_to_all | solution.py:122
  19.6 1.3 pad_maximum_fusion.1
  20.9 1.4 collective-permute-start
  23.3 2.1 fusion.75
  25.4 1.1 select_bitcast_fusion.4
  26.5 4.6 %collective-permute-start.7 = (f32[160,640]{1,0:T(8,128)}, f32[160,640]{1,0:T(8,128)}, u32[]{:S(2)}, u32[]{:S(2)}) collective-permute-start(f32[160,640]{1,0:T(8,128)} %get-tuple-element.31), channel_id=1, source_target_pairs={{1,0},{3,2},{4,7},{6,5},{9,8},{11,10},{12,15},{14,13},{17,16},{19,... | collective-permute-start | bytes 1228808 | tf_op jit(solution)/shard_map/ppermute | solution.py:167
  31.2 1.4 collective-permute-start.8
  36.2 14.1 %all-to-all-done = f32[4,640,256]{2,1,0:T(8,128)S(1)} async-done(((f32[4,640,256]{2,1,0:T(8,128)}), f32[4,640,256]{2,1,0:T(8,128)S(1)}, u32[]{:S(2)}, u32[]{:S(2)}) %all-to-all-start) | async-done | bytes 2621472 | tf_op jit(solution)/shard_map/all_to_all | solution.py:122
  50.4 1.1 reduce_sum.46
  51.4 6.7 %all-to-all-start.1 = ((f32[8,80,256]{2,1,0:T(8,128)}), f32[8,80,256]{2,1,0:T(8,128)S(1)}, u32[]{:S(2)}, u32[]{:S(2)}) async-start(f32[8,80,256]{2,1,0:T(8,128)} %bitcast.106), calls=%async_computation.1 | async-start | bytes 1310720 | tf_op jit(solution)/shard_map/all_to_all | solution.py:122
  63.4 3.6 %collective-permute-done.7 = f32[160,640]{1,0:T(8,128)} collective-permute-done((f32[160,640]{1,0:T(8,128)}, f32[160,640]{1,0:T(8,128)}, u32[]{:S(2)}, u32[]{:S(2)}) %collective-permute-start.7) | collective-permute-done | bytes 409632 | tf_op jit(solution)/shard_map/ppermute | solution.py:167
  67.0 2.5 %collective-permute-start.9 = (f32[160,640]{1,0:T(8,128)S(1)}, f32[160,640]{1,0:T(8,128)S(1)}, u32[]{:S(2)}, u32[]{:S(2)}) collective-permute-start(f32[160,640]{1,0:T(8,128)S(1)} %copy-done.11), channel_id=1, source_target_pairs={{1,2},{3,0},{4,5},{6,7},{9,10},{11,8},{12,13},{14,15},{17,18},{19,... | collective-permute-start | bytes 1228808 | tf_op jit(solution)/shard_map/ppermute | solution.py:167
  69.5 1.8 constant_dynamic-update-slice_fusion.13
  71.3 6.1 %all-to-all-done.1 = f32[8,80,256]{2,1,0:T(8,128)S(1)} async-done(((f32[8,80,256]{2,1,0:T(8,128)}), f32[8,80,256]{2,1,0:T(8,128)S(1)}, u32[]{:S(2)}, u32[]{:S(2)}) %all-to-all-start.1) | async-done | bytes 655392 | tf_op jit(solution)/shard_map/all_to_all | solution.py:122
  77.5 0.9 broadcast_in_dim.76
  78.4 5.4 %all-to-all-start.2 = ((f32[8,80,256]{2,1,0:T(8,128)}), f32[8,80,256]{2,1,0:T(8,128)S(1)}, u32[]{:S(2)}, u32[]{:S(2)}) async-start(f32[8,80,256]{2,1,0:T(8,128)} %broadcast_in_dim.76), calls=%async_computation.2 | async-start | bytes 1310720 | tf_op jit(solution)/shard_map/all_to_all | solution.py:122
  83.8 1.8 constant_dynamic-update-slice_fusion.12
  86.5 0.9 bitcast_dynamic-update-slice_fusion.1
  87.4 1.8 constant_dynamic-update-slice_fusion.10
  89.2 5.5 %all-to-all-done.2 = f32[8,80,256]{2,1,0:T(8,128)S(1)} async-done(((f32[8,80,256]{2,1,0:T(8,128)}), f32[8,80,256]{2,1,0:T(8,128)S(1)}, u32[]{:S(2)}, u32[]{:S(2)}) %all-to-all-start.2) | async-done | bytes 655392 | tf_op jit(solution)/shard_map/all_to_all | solution.py:122
  94.6 1.7 gather_fusion
  96.4 4.4 %all-to-all-start.3 = ((f32[8,2,80,256]{3,2,1,0:T(8,128)}), f32[8,2,80,256]{3,2,1,0:T(8,128)}, u32[]{:S(2)}, u32[]{:S(2)}) async-start(f32[8,2,80,256]{3,2,1,0:T(8,128)} %bitcast.10), calls=%async_computation.3 | async-start | bytes 2621440 | tf_op jit(solution)/shard_map/all_to_all | solution.py:122
  100.8 1.8 constant_dynamic-update-slice_fusion.9
  103.4 1.5 constant_dynamic-slice_fusion.3.f_ref
  105.0 2.2 constant_dynamic-update-slice_fusion.6
  107.1 2.1 constant_dynamic-update-slice_fusion.5
  109.2 2.1 constant_dynamic-update-slice_fusion.4
  111.3 0.9 constant_dynamic-update-slice_fusion.3
  112.3 2.1 constant_dynamic-update-slice_fusion.2
  114.4 2.1 constant_dynamic-update-slice_fusion.1
  116.5 2.1 constant_dynamic-update-slice_fusion
  118.6 2.1 dynamic-slice_select_fusion.b_ref
  120.7 13.3 %all-to-all-done.3 = f32[8,2,80,256]{3,2,1,0:T(8,128)} async-done(((f32[8,2,80,256]{3,2,1,0:T(8,128)}), f32[8,2,80,256]{3,2,1,0:T(8,128)}, u32[]{:S(2)}, u32[]{:S(2)}) %all-to-all-start.3) | async-done | bytes 1310752 | tf_op jit(solution)/shard_map/all_to_all | solution.py:122
  134.0 2.4 fusion.74
  136.3 0.8 copy-done.2
  137.2 2.9 %fusion.6 = f32[640,256]{1,0:T(8,128)S(1)} fusion(f32[640,256]{1,0:T(8,128)S(1)} %bitcast.103, f32[1280,1280]{1,0:T(8,128)} %constant_dynamic-update-slice_fusion, s32[]{:T(128)S(6)} %select_n.234, s32[]{:T(128)S(6)} %add.175), kind=kOutput, calls=%fused_computation.13 | convolution fusion | flops 629145600 | bytes 2949128 | tf_op jit(solution)/shard_map/dot_general | solution.py:211
  140.1 3.6 %fusion.23 = f32[640,256]{1,0:T(8,128)} fusion(f32[1280,1280]{1,0:T(8,128)} %constant_dynamic-update-slice_fusion, s32[]{:T(128)S(6)} %select_n.234, s32[]{:T(128)S(6)} %add.175, f32[640,256]{1,0:T(8,128)S(1)} %fusion.6, f32[1,2,640,256]{3,2,1,0:T(8,128)S(1)} %copy-done.13, f32[1,2,640,256]{3,2,1,0:T(8,128)S(1)} %copy-done.15, ...), kind=kOutput, calls=%fused_computation.21 | convolution fusion | flops 631275520 | bytes 4915208 | tf_op jit(solution)/shard_map/dot_general | solution.py:216
  143.7 2.1 reshape.120
  145.9 3.2 %broadcast_select_fusion.1 = (f32[640,256]{1,0:T(8,128)}, f32[640,256]{1,0:T(8,128)}, f32[640,256]{1,0:T(8,128)}, f32[640,256]{1,0:T(8,128)}) fusion(pred[]{:T(512)S(6)} %eq.115, f32[8,1,80,256]{3,2,1,0:T(8,128)} %copy-done.2, f32[8,1,80,256]{3,2,1,0:T(8,128)} %get-tuple-element.28, pred[]{:T(512)S(6)} %eq.112, pred[]{:T(512)S(6)} %eq.113, pred[]{:T(512)S(6)} %eq.114), kind=kLoop, calls=%fused_computation.74 | loop fusion | flops 655360 | bytes 3932164 | tf_op jit(solution)/shard_map/jit(_where)/select_n | solution.py:177
  149.1 2.9 %fusion.2 = f32[640,256]{1,0:T(8,128)S(1)} fusion(f32[640,256]{1,0:T(8,128)S(1)} %bitcast.102, f32[1280,1280]{1,0:T(8,128)} %constant_dynamic-update-slice_fusion, s32[]{:T(128)S(6)} %select_n.234), kind=kOutput, calls=%fused_computation.9 | convolution fusion | flops 629145600 | bytes 2949124 | tf_op jit(solution)/shard_map/dot_general | solution.py:211
  152.0 3.5 %fusion.17 = f32[640,256]{1,0:T(8,128)} fusion(f32[1280,1280]{1,0:T(8,128)} %constant_dynamic-update-slice_fusion, s32[]{:T(128)S(6)} %select_n.234, f32[640,256]{1,0:T(8,128)S(1)} %fusion.2, f32[1,2,640,256]{3,2,1,0:T(8,128)S(1)} %copy-done.14, f32[1,2,640,256]{3,2,1,0:T(8,128)S(1)} %copy-done.16, f32[1,2,640,256]{3,2,1,0:T(8,128)S(1)} %copy-done.18), kind=kOutput, calls=%fused_computation.19 | convolution fusion | flops 631275520 | bytes 4915204 | tf_op jit(solution)/shard_map/dot_general | solution.py:216
  155.6 2.2 reshape.119
  157.7 5.6 %collective-permute-start.4 = (f32[640,256]{1,0:T(8,128)}, f32[640,256]{1,0:T(8,128)}, u32[]{:S(2)}, u32[]{:S(2)}) collective-permute-start(f32[640,256]{1,0:T(8,128)} %get-tuple-element.26), channel_id=1, source_target_pairs={{1,0},{3,2},{4,7},{6,5},{9,8},{11,10},{12,15},{14,13},{17,16},{19,... | collective-permute-start | bytes 1966088 | tf_op jit(solution)/shard_map/ppermute | solution.py:167
  163.3 1.5 collective-permute-start.5
  164.8 2.3 collective-permute-start.6
  167.1 2.8 %gather_fusion.3 = f32[64,10,256]{2,1,0:T(8,128)} fusion(f32[64,10,256]{2,1,0:T(8,128)} %reshape.120, s32[1024]{0:T(1024)S(1)} %get-tuple-element.51), kind=kCustom, calls=%fused_computation.1.clone | custom fusion | bytes 1310976 | tf_op jit(solution)/shard_map/jit(_take)/gather | solution.py:224
  169.9 2.8 %gather_fusion.2 = f32[64,10,256]{2,1,0:T(8,128)} fusion(f32[64,10,256]{2,1,0:T(8,128)} %reshape.119, s32[1024]{0:T(1024)S(1)} %pad_clamp_fusion.2), kind=kCustom, calls=%fused_computation.clone | custom fusion | bytes 1310976 | tf_op jit(solution)/shard_map/jit(_take)/gather | solution.py:224
  172.8 1.4 select_bitcast_fusion
  174.6 2.3 copy.53
  176.9 5.3 %all-to-all-start.4 = ((f32[2,64,10,256]{3,0,2,1:T(2,128)}), f32[2,64,10,256]{3,0,2,1:T(2,128)}, u32[]{:S(2)}, u32[]{:S(2)}) async-start(f32[2,64,10,256]{3,0,2,1:T(2,128)} %copy.53), calls=%async_computation.4 | async-start | bytes 2621440 | tf_op jit(solution)/shard_map/all_to_all | solution.py:225
  182.2 1.1 copy-done
  183.3 38.1 %refresh.1 = f32[640,640]{1,0:T(8,128)S(1)} custom-call(f32[640,256]{1,0:T(8,128)S(1)} %copy-done, f32[640,256]{1,0:T(8,128)} %collective-permute-done.4.g1, f32[640,256]{1,0:T(8,128)} %collective-permute-done.5.g2, f32[640,256]{1,0:T(8,128)} %collective-permute-done.6.g3, f32[640,640]{1,0:T(8,128)S(1)} %constant_dynamic-slice_fusion.3.f_ref, ...), custom_call_target="tpu_custom_call" | custom-call | flops 22020096000 | bytes 6553600 | tf_op jit(solution)/shard_map/refresh/pallas_call | solution.py:82
  221.5 0.8 constant_dynamic-slice_fusion.2
  223.1 1.3 collective-permute-start.12
  224.4 1.3 collective-permute-start.10
  225.7 11.9 %collective-permute-done.12 = f32[160,640]{1,0:T(8,128)S(1)} collective-permute-done((f32[160,640]{1,0:T(8,128)S(1)}, f32[160,640]{1,0:T(8,128)S(1)}, u32[]{:S(2)}, u32[]{:S(2)}) %collective-permute-start.12) | collective-permute-done | bytes 409632 | tf_op jit(solution)/shard_map/ppermute | solution.py:167
  238.0 1.1 select_bitcast_fusion.3
  239.1 1.5 copy.60
  240.7 1.6 copy.61
  (79 shorter events, 10.3 us)
Async XLA Ops:
  0.6 6.3 %copy-start.10 = (f32[1,160,2,640]{3,2,1,0:T(2,128)S(1)}, f32[1,160,2,640]{3,2,1,0:T(2,128)}, u32[]{:S(2)}) copy-start(f32[1,160,2,640]{3,2,1,0:T(2,128)} %param.14) | copy-start | bytes 2457604
  3.8 7.9 %collective-permute-start.3 = (f32[4,640,256]{2,1,0:T(8,128)}, f32[4,640,256]{2,1,0:T(8,128)S(1)}, u32[]{:S(2)}, u32[]{:S(2)}) collective-permute-start(f32[4,640,256]{2,1,0:T(8,128)} %bitcast_convert_fusion), channel_id=1, source_target_pairs={{0,4},{4,0},{8,12},{12,8},{16,20},{20,16},{24,28},{28,24},{32,36},... | collective-permute-start | bytes 7864328 | tf_op jit(solution)/shard_map/ppermute | solution.py:115
  14.9 3.8 %copy-start.8 = (f32[1,160,1,640]{3,2,1,0:T(1,128)S(1)}, f32[1,160,1,640]{3,2,1,0:T(1,128)}, u32[]{:S(2)}) copy-start(f32[1,160,1,640]{3,2,1,0:T(1,128)} %get-tuple-element.37) | copy-start | bytes 1228804
  14.9 3.8 %copy-start.9 = (f32[1,160,1,640]{3,2,1,0:T(1,128)S(1)}, f32[1,160,1,640]{3,2,1,0:T(1,128)}, u32[]{:S(2)}) copy-start(f32[1,160,1,640]{3,2,1,0:T(1,128)} %get-tuple-element.38) | copy-start | bytes 1228804
  14.9 35.4 %all-to-all-start = ((f32[4,640,256]{2,1,0:T(8,128)}), f32[4,640,256]{2,1,0:T(8,128)S(1)}, u32[]{:S(2)}, u32[]{:S(2)}) async-start(f32[4,640,256]{2,1,0:T(8,128)} %convert_add_fusion), calls=%async_computation | async-start | bytes 5242880 | tf_op jit(solution)/shard_map/all_to_all | solution.py:122
  18.8 0.8 copy-start.4
  18.8 2.0 copy-start.6
  19.6 13.0 %copy-start.12 = (s32[8]{0:T(128)S(1)}, s32[8]{0:T(128)}, u32[]{:S(2)}) copy-start(s32[8]{0:T(128)} %param.11) | copy-start | bytes 100
  20.9 84.1 %collective-permute-start = (f32[160,1280]{1,0:T(8,128)}, f32[160,1280]{1,0:T(8,128)}, u32[]{:S(2)}, u32[]{:S(2)}) collective-permute-start(f32[160,1280]{1,0:T(8,128)} %get-tuple-element.35), channel_id=1, source_target_pairs={{0,3},{1,0},{2,1},{3,2},{4,7},{5,4},{6,5},{7,6},{8,11},{9,8},{10,9... | collective-permute-start | bytes 2457608 | tf_op jit(solution)/shard_map/ppermute | solution.py:167
  22.2 84.9 %collective-permute-start.1 = (f32[160,1280]{1,0:T(8,128)}, f32[160,1280]{1,0:T(8,128)}, u32[]{:S(2)}, u32[]{:S(2)}) collective-permute-start(f32[160,1280]{1,0:T(8,128)} %get-tuple-element.35), channel_id=1, source_target_pairs={{0,2},{1,3},{2,0},{3,1},{4,6},{5,7},{6,4},{7,5},{8,10},{9,11},{10,... | collective-permute-start | bytes 2457608 | tf_op jit(solution)/shard_map/ppermute | solution.py:167
  22.6 86.7 %collective-permute-start.2 = (f32[160,1280]{1,0:T(8,128)}, f32[160,1280]{1,0:T(8,128)}, u32[]{:S(2)}, u32[]{:S(2)}) collective-permute-start(f32[160,1280]{1,0:T(8,128)} %get-tuple-element.35), channel_id=1, source_target_pairs={{0,1},{1,2},{2,3},{3,0},{4,5},{5,6},{6,7},{7,4},{8,9},{9,10},{10,1... | collective-permute-start | bytes 2457608 | tf_op jit(solution)/shard_map/ppermute | solution.py:167
  26.5 40.5 %collective-permute-start.7 = (f32[160,640]{1,0:T(8,128)}, f32[160,640]{1,0:T(8,128)}, u32[]{:S(2)}, u32[]{:S(2)}) collective-permute-start(f32[160,640]{1,0:T(8,128)} %get-tuple-element.31), channel_id=1, source_target_pairs={{1,0},{3,2},{4,7},{6,5},{9,8},{11,10},{12,15},{14,13},{17,16},{19,... | collective-permute-start | bytes 1228808 | tf_op jit(solution)/shard_map/ppermute | solution.py:167
  31.2 52.7 %collective-permute-start.8 = (f32[160,640]{1,0:T(8,128)}, f32[160,640]{1,0:T(8,128)}, u32[]{:S(2)}, u32[]{:S(2)}) collective-permute-start(f32[160,640]{1,0:T(8,128)} %get-tuple-element.32), channel_id=1, source_target_pairs={{0,2},{2,0},{5,7},{7,5},{8,10},{10,8},{13,15},{15,13},{16,18},{18,... | collective-permute-start | bytes 1228808 | tf_op jit(solution)/shard_map/ppermute | solution.py:167
  51.4 15.5 %copy-start.11 = (f32[160,640]{1,0:T(8,128)S(1)}, f32[160,640]{1,0:T(8,128)}, u32[]{:S(2)}) copy-start(f32[160,640]{1,0:T(8,128)} %get-tuple-element.30) | copy-start | bytes 1228804
  51.4 26.0 %all-to-all-start.1 = ((f32[8,80,256]{2,1,0:T(8,128)}), f32[8,80,256]{2,1,0:T(8,128)S(1)}, u32[]{:S(2)}, u32[]{:S(2)}) async-start(f32[8,80,256]{2,1,0:T(8,128)} %bitcast.106), calls=%async_computation.1 | async-start | bytes 1310720 | tf_op jit(solution)/shard_map/all_to_all | solution.py:122
  67.0 18.7 %collective-permute-start.9 = (f32[160,640]{1,0:T(8,128)S(1)}, f32[160,640]{1,0:T(8,128)S(1)}, u32[]{:S(2)}, u32[]{:S(2)}) collective-permute-start(f32[160,640]{1,0:T(8,128)S(1)} %copy-done.11), channel_id=1, source_target_pairs={{1,2},{3,0},{4,5},{6,7},{9,10},{11,8},{12,13},{14,15},{17,18},{19,... | collective-permute-start | bytes 1228808 | tf_op jit(solution)/shard_map/ppermute | solution.py:167
  78.4 16.2 %all-to-all-start.2 = ((f32[8,80,256]{2,1,0:T(8,128)}), f32[8,80,256]{2,1,0:T(8,128)S(1)}, u32[]{:S(2)}, u32[]{:S(2)}) async-start(f32[8,80,256]{2,1,0:T(8,128)} %broadcast_in_dim.76), calls=%async_computation.2 | async-start | bytes 1310720 | tf_op jit(solution)/shard_map/all_to_all | solution.py:122
  96.4 37.6 %all-to-all-start.3 = ((f32[8,2,80,256]{3,2,1,0:T(8,128)}), f32[8,2,80,256]{3,2,1,0:T(8,128)}, u32[]{:S(2)}, u32[]{:S(2)}) async-start(f32[8,2,80,256]{3,2,1,0:T(8,128)} %bitcast.10), calls=%async_computation.3 | async-start | bytes 2621440 | tf_op jit(solution)/shard_map/all_to_all | solution.py:122
  104.9 6.4 %copy-start.5 = (f32[160,640]{1,0:T(8,128)S(1)}, f32[160,640]{1,0:T(8,128)}, u32[]{:S(2)}) copy-start(f32[160,640]{1,0:T(8,128)} %copy-done.4) | copy-start | bytes 1228804
  104.9 6.4 %copy-start.7 = (f32[160,640]{1,0:T(8,128)S(1)}, f32[160,640]{1,0:T(8,128)}, u32[]{:S(2)}) copy-start(f32[160,640]{1,0:T(8,128)} %copy-done.6) | copy-start | bytes 1228804
  133.9 6.2 %copy-start.13 = (f32[1,2,640,256]{3,2,1,0:T(8,128)S(1)}, f32[1,2,640,256]{3,2,1,0:T(8,128)}, u32[]{:S(2)}) copy-start(f32[1,2,640,256]{3,2,1,0:T(8,128)} %param.16) | copy-start | bytes 3932164
  133.9 6.2 %copy-start.15 = (f32[1,2,640,256]{3,2,1,0:T(8,128)S(1)}, f32[1,2,640,256]{3,2,1,0:T(8,128)}, u32[]{:S(2)}) copy-start(f32[1,2,640,256]{3,2,1,0:T(8,128)} %param.15) | copy-start | bytes 3932164
  133.9 6.2 %copy-start.17 = (f32[1,2,640,256]{3,2,1,0:T(8,128)S(1)}, f32[1,2,640,256]{3,2,1,0:T(8,128)}, u32[]{:S(2)}) copy-start(f32[1,2,640,256]{3,2,1,0:T(8,128)} %param.17) | copy-start | bytes 3932164
  136.3 0.9 copy-start.2
  145.9 3.2 %copy-start.1 = (f32[8,1,80,256]{3,2,1,0:T(8,128)S(1)}, f32[8,1,80,256]{3,2,1,0:T(8,128)}, u32[]{:S(2)}) copy-start(f32[8,1,80,256]{3,2,1,0:T(8,128)} %get-tuple-element.28) | copy-start | bytes 1966084
  145.9 6.1 %copy-start.14 = (f32[1,2,640,256]{3,2,1,0:T(8,128)S(1)}, f32[1,2,640,256]{3,2,1,0:T(8,128)}, u32[]{:S(2)}) copy-start(f32[1,2,640,256]{3,2,1,0:T(8,128)} %param.16) | copy-start | bytes 3932164
  145.9 6.1 %copy-start.16 = (f32[1,2,640,256]{3,2,1,0:T(8,128)S(1)}, f32[1,2,640,256]{3,2,1,0:T(8,128)}, u32[]{:S(2)}) copy-start(f32[1,2,640,256]{3,2,1,0:T(8,128)} %param.15) | copy-start | bytes 3932164
  145.9 6.1 %copy-start.18 = (f32[1,2,640,256]{3,2,1,0:T(8,128)S(1)}, f32[1,2,640,256]{3,2,1,0:T(8,128)}, u32[]{:S(2)}) copy-start(f32[1,2,640,256]{3,2,1,0:T(8,128)} %param.17) | copy-start | bytes 3932164
  157.7 24.5 %collective-permute-start.4 = (f32[640,256]{1,0:T(8,128)}, f32[640,256]{1,0:T(8,128)}, u32[]{:S(2)}, u32[]{:S(2)}) collective-permute-start(f32[640,256]{1,0:T(8,128)} %get-tuple-element.26), channel_id=1, source_target_pairs={{1,0},{3,2},{4,7},{6,5},{9,8},{11,10},{12,15},{14,13},{17,16},{19,... | collective-permute-start | bytes 1966088 | tf_op jit(solution)/shard_map/ppermute | solution.py:167
  163.3 18.9 %collective-permute-start.5 = (f32[640,256]{1,0:T(8,128)}, f32[640,256]{1,0:T(8,128)}, u32[]{:S(2)}, u32[]{:S(2)}) collective-permute-start(f32[640,256]{1,0:T(8,128)} %get-tuple-element.27), channel_id=1, source_target_pairs={{0,2},{2,0},{5,7},{7,5},{8,10},{10,8},{13,15},{15,13},{16,18},{18,... | collective-permute-start | bytes 1966088 | tf_op jit(solution)/shard_map/ppermute | solution.py:167
  164.8 17.4 %collective-permute-start.6 = (f32[640,256]{1,0:T(8,128)}, f32[640,256]{1,0:T(8,128)}, u32[]{:S(2)}, u32[]{:S(2)}) collective-permute-start(f32[640,256]{1,0:T(8,128)} %get-tuple-element.24), channel_id=1, source_target_pairs={{1,2},{3,0},{4,5},{6,7},{9,10},{11,8},{12,13},{14,15},{17,18},{19,... | collective-permute-start | bytes 1966088 | tf_op jit(solution)/shard_map/ppermute | solution.py:167
  172.8 1.5 copy-start.3
  176.9 63.7 %all-to-all-start.4 = ((f32[2,64,10,256]{3,0,2,1:T(2,128)}), f32[2,64,10,256]{3,0,2,1:T(2,128)}, u32[]{:S(2)}, u32[]{:S(2)}) async-start(f32[2,64,10,256]{3,0,2,1:T(2,128)} %copy.53), calls=%async_computation.4 | async-start | bytes 2621440 | tf_op jit(solution)/shard_map/all_to_all | solution.py:225
  182.2 1.1 copy-start
  222.4 3.3 %collective-permute-start.11 = (f32[160,640]{1,0:T(8,128)}, f32[160,640]{1,0:T(8,128)S(1)}, u32[]{:S(2)}, u32[]{:S(2)}) collective-permute-start(f32[160,640]{1,0:T(8,128)} %get-tuple-element.23), channel_id=1, source_target_pairs={{0,2},{2,0},{5,7},{7,5},{8,10},{10,8},{13,15},{15,13},{16,18},{18,... | collective-permute-start | bytes 1228808 | tf_op jit(solution)/shard_map/ppermute | solution.py:167
  223.1 14.6 %collective-permute-start.12 = (f32[160,640]{1,0:T(8,128)S(1)}, f32[160,640]{1,0:T(8,128)S(1)}, u32[]{:S(2)}, u32[]{:S(2)}) collective-permute-start(f32[160,640]{1,0:T(8,128)S(1)} %get-tuple-element.22), channel_id=1, source_target_pairs={{0,3},{2,1},{5,4},{7,6},{8,11},{10,9},{13,12},{15,14},{16,19},{18,... | collective-permute-start | bytes 1228808 | tf_op jit(solution)/shard_map/ppermute | solution.py:167
  224.4 13.6 %collective-permute-start.10 = (f32[160,640]{1,0:T(8,128)S(1)}, f32[160,640]{1,0:T(8,128)}, u32[]{:S(2)}, u32[]{:S(2)}) collective-permute-start(f32[160,640]{1,0:T(8,128)S(1)} %get-tuple-element.21), channel_id=1, source_target_pairs={{0,1},{2,3},{5,6},{7,4},{8,9},{10,11},{13,14},{15,12},{16,17},{18,... | collective-permute-start | bytes 1228808 | tf_op jit(solution)/shard_map/ppermute | solution.py:167

commit v3 on v2

v3 whole, which is shorter than its diff:
```python
import jax
import jax.numpy as jnp
from jax import lax
from jax.experimental import pallas as pl
from jax.experimental.pallas import tpu as pltpu
from jax.sharding import PartitionSpec as P


NS_ITERS = 4
SLOTS = 2
PARTS = (80,)
NX, NZ, NC = 4, 8, 2
NT = (((1,), (1,)), ((), ()))
NN = (((1,), (0,)), ((), ()))


def split(x):
    hi = x.astype(jnp.bfloat16)
    lo = (x - hi.astype(jnp.float32)).astype(jnp.bfloat16)
    return hi, lo


def mm(left, right, dims):
    return lax.dot_general(left, right, dims, preferred_element_type=jnp.float32)


def mm3(left, right, dims=NN):
    (lh, ll), (rh, rl) = left, right
    return mm(lh, rh, dims) + (mm(lh, rl, dims) + mm(ll, rh, dims))


def row_starts(y, rows, cols):
    return [pl.multiple_of(lax.rem(y + k, cols) * rows, 32) for k in range(cols)]


def scattered(part):
    lead = sum(PARTS[:part])
    whole = sum(PARTS)
    return [(z * PARTS[part], z * whole + lead, PARTS[part]) for z in range(NZ)]


def prepare_kernel(at, b0, b1, b2, b3, hi_ref, lo_ref, thi_ref, tlo_ref, whole):
    blocks = (b0, b1, b2, b3)
    rows, d = b0.shape[0], whole.shape[0]
    starts = row_starts(at[0], rows, len(blocks))
    for s in range(SLOTS):
        for start, block in zip(starts, blocks):
            whole[pl.ds(start, rows), :] = block[:, s * d:(s + 1) * d]
        b = whole[...]
        hi_ref[s], lo_ref[s] = split(b)
        thi_ref[s], tlo_ref[s] = split(b.T)


def prepare(scalars, blocks):
    d = blocks[0].shape[1] // SLOTS
    half = jax.ShapeDtypeStruct((SLOTS, d, d), jnp.bfloat16)
    vmem = pl.BlockSpec(memory_space=pltpu.VMEM)
    return pl.pallas_call(
        prepare_kernel,
        out_shape=[half] * 4,
        in_specs=[pl.BlockSpec(memory_space=pltpu.SMEM)] + [vmem] * 4,
        out_specs=[vmem] * 4,
        scratch_shapes=[pltpu.VMEM((d, d), jnp.float32)],
        compiler_params=pltpu.CompilerParams(vmem_limit_bytes=24 << 20),
        cost_estimate=pl.CostEstimate(flops=8 * d * d, bytes_accessed=24 * d * d, transcendentals=0),
        name="prepare",
    )(scalars, *blocks)


def update_kernel(chosen, *refs):
    incoming = refs[:len(PARTS)]
    hi, lo, thi, tlo, m1, m2, held, out, gh, gl, weights = refs[len(PARTS):]
    groups = out.shape[0]
    block = held.shape[1] // groups
    for s in range(SLOTS):
        for part, ref in enumerate(incoming):
            for z, (_, row, size) in enumerate(scattered(part)):
                gh[row:row + size], gl[row:row + size] = split(ref[z, s])
        turned = mm3((thi[s], tlo[s]), (gh[...], gl[...]))
        first = 0.9 * m1[s] + 0.1 * turned
        second = 0.95 * m2[s] + 0.05 * turned * turned
        direction = mm3((hi[s], lo[s]), split(first / (jnp.sqrt(second) + 1e-08)))
        fresh = held[s] - 0.1 * (direction + 0.1 * held[s])
        here = slice(s * block, (s + 1) * block)
        for j in range(groups):
            weights[j, here, :] = fresh[j * block:(j + 1) * block]

        def send(j, carry):
            out[j, here, :] = weights[chosen[s, j], here, :]
            return carry

        lax.fori_loop(0, groups, send, 0, unroll=4)


def update(chosen, incoming, halves, m1, m2, held):
    groups = chosen.shape[1]
    d, cols = m1.shape[1:]
    block = d // groups
    padded = -(-SLOTS * block // 8) * 8
    vmem = pl.BlockSpec(memory_space=pltpu.VMEM)
    return pl.pallas_call(
        update_kernel,
        out_shape=jax.ShapeDtypeStruct((groups, padded, cols), jnp.float32),
        in_specs=[pl.BlockSpec(memory_space=pltpu.SMEM)] + [vmem] * (7 + len(PARTS)),
        out_specs=vmem,
        scratch_shapes=[
            pltpu.VMEM((d, cols), jnp.bfloat16),
            pltpu.VMEM((d, cols), jnp.bfloat16),
            pltpu.VMEM((groups, padded, cols), jnp.float32),
        ],
        compiler_params=pltpu.CompilerParams(vmem_limit_bytes=24 << 20),
        cost_estimate=pl.CostEstimate(
            flops=24 * d * d * cols, bytes_accessed=36 * d * cols, transcendentals=2 * d * cols
        ),
        name="update",
    )(chosen, *incoming, *halves, m1, m2, held)


def refresh_kernel(at, g0, g1, g2, g3, f0, f1, f2, f3, b_hi, b_lo, o_ref, gl, gr, left, right, stack, x_ref):
    d = x_ref.shape[0]
    w = g0.shape[1]
    kc = 4 * w
    for b, g_ref in enumerate((g0, g1, g2, g3)):
        base = 0
        for part in range(len(PARTS)):
            for source, row, size in scattered(part):
                hi, lo = split(g_ref[base + source:base + source + size])
                gl[row:row + size, b * w:(b + 1) * w] = hi
                gl[row:row + size, kc + b * w:kc + (b + 1) * w] = hi
                gl[row:row + size, 2 * kc + b * w:2 * kc + (b + 1) * w] = lo
                gr[row:row + size, b * w:(b + 1) * w] = hi
                gr[row:row + size, kc + b * w:kc + (b + 1) * w] = lo
                gr[row:row + size, 2 * kc + b * w:2 * kc + (b + 1) * w] = hi
            base += NZ * PARTS[part]

    def put_left(v):
        hi, lo = split(v)
        left[:, :d] = hi
        left[:, d:2 * d] = hi
        left[:, 2 * d:] = lo
        return hi, lo

    def put_right(hi, lo):
        right[:, :d] = hi
        right[:, d:2 * d] = lo
        right[:, 2 * d:] = hi

    def put_stack(hi, lo):
        stack[:d] = hi
        stack[d:2 * d] = lo
        stack[2 * d:] = hi

    x_ref[...] = mm(gl[...], gr[...], NT)
    rows = f0.shape[0]
    for start, f_ref in zip(row_starts(at[0], rows, 4), (f0, f1, f2, f3)):
        here = pl.ds(start, rows)
        hi, lo = split(0.95 * f_ref[...] + 0.05 * x_ref[here, :])
        left[here, :d] = hi
        left[here, d:2 * d] = hi
        left[here, 2 * d:] = lo
    put_stack(b_hi[at[1]], b_lo[at[1]])
    power = mm(left[...], stack[...], NN)
    total = jnp.sum(power * power)
    x_ref[...] = power / jnp.sqrt(jnp.full((1, 1), total + 1e-06, jnp.float32))

    def step(_, carry):
        hi, lo = put_left(x_ref[...])
        put_stack(hi, lo)
        put_right(hi, lo)
        inner = mm(left[...], right[...], NT)
        hi, lo = put_left(inner)
        put_right(hi, lo)
        squared = mm(left[...], right[...], NT)
        put_left(-4.775 * inner + 2.0315 * squared)
        x_ref[...] = 3.4445 * x_ref[...] + mm(left[...], stack[...], NN)
        return carry

    lax.fori_loop(0, NS_ITERS, step, 0)
    o_ref[...] = jnp.where(at[2] > 0, x_ref[...], 0.0)


def refresh(scalars, pieces, factors, b_hi, b_lo):
    d = factors[0].shape[1]
    kc = 4 * pieces[0].shape[1]
    vmem = pl.BlockSpec(memory_space=pltpu.VMEM)
    return pl.pallas_call(
        refresh_kernel,
        out_shape=jax.ShapeDtypeStruct((d, d), jnp.float32),
        in_specs=[pl.BlockSpec(memory_space=pltpu.SMEM)] + [vmem] * 10,
        out_specs=vmem,
        scratch_shapes=[
            pltpu.VMEM((d, 3 * kc), jnp.bfloat16),
            pltpu.VMEM((d, 3 * kc), jnp.bfloat16),
            pltpu.VMEM((d, 3 * d), jnp.bfloat16),
            pltpu.VMEM((d, 3 * d), jnp.bfloat16),
            pltpu.VMEM((3 * d, d), jnp.bfloat16),
            pltpu.VMEM((d, d), jnp.float32),
        ],
        compiler_params=pltpu.CompilerParams(vmem_limit_bytes=40 << 20),
        cost_estimate=pl.CostEstimate(
            flops=6 * 14 * d**3, bytes_accessed=16 * d * d, transcendentals=0
        ),
        name="refresh",
    )(scalars, *pieces, *factors, b_hi, b_lo)


def line(x, z, core):
    return (x * NZ + z) * NC + core


def owned_gradients(local, owner, slot, d):
    x, core = d // (NZ * NC), d % NC
    count, rows, cols = local.shape
    groups = NX * NZ * NC
    along_x = [[line(a, b, c) for a in range(NX)] for b in range(NZ) for c in range(NC)]
    along_z = [[line(a, b, c) for b in range(NZ)] for a in range(NX) for c in range(NC)]
    across = [[line(a, b, c) for a in range(NX) for c in range(NC)] for b in range(NZ)]
    swap = [
        (line(a, b, c), line(a, b, 1 - c))
        for a in range(NX) for b in range(NZ) for c in range(NC)
    ]

    def exchange(v, lines):
        return lax.all_to_all(v, "dp", 0, 0, axis_index_groups=lines, tiled=True)

    hits = (owner[None, None, :] == jnp.arange(groups)[:, None, None]) & (
        slot[None, None, :] == jnp.arange(SLOTS)[None, :, None]
    )
    matrix_of = jnp.sum(jnp.where(hits, jnp.arange(count)[None, None, :], 0), axis=2)
    wanted = lax.dynamic_index_in_dim(matrix_of.reshape(NX, NZ, NC, SLOTS), x, 0, keepdims=False)
    wanted = lax.dynamic_index_in_dim(wanted, core, 1, keepdims=False).reshape(-1)

    paired = local.reshape(NX, NC, NZ, rows // NZ, cols)
    others = lax.dynamic_index_in_dim(paired, 1 - core, 1, keepdims=False)
    kept = lax.dynamic_index_in_dim(paired, core, 1, keepdims=False)
    outs = []
    lead = 0
    for size in PARTS:
        came = lax.ppermute(
            others[:, :, lead:lead + size].astype(jnp.float32).reshape(NX, NZ * size, cols), "dp", swap
        )
        chip = kept[:, :, lead:lead + size].astype(jnp.float32).reshape(NX, NZ * size, cols) + came
        lead += size
        outs.append(exchange(chip, along_x))
    incoming = []
    for part, size in enumerate(PARTS):
        over_x = jnp.sum(outs[part], axis=0)
        over_z = jnp.sum(exchange(over_x.reshape(NZ, size, cols), along_z), axis=0)
        mean = over_z * (1.0 / groups)
        everything = exchange(jnp.broadcast_to(mean[None], (count, size, cols)), across)
        outgoing = jnp.take(everything, wanted, axis=0, mode="clip")
        incoming.append(exchange(outgoing.reshape(NZ, SLOTS, size, cols), along_z))
    return incoming


def body(partials, owner, rowblock, factor, basis, moment1, moment2, master):
    groups = lax.axis_size("dp")
    cols = lax.axis_size("mp")
    d = lax.axis_index("dp")
    y = lax.axis_index("mp")
    core = d % NC
    count = owner.shape[0]
    rows = factor.shape[1]
    order = jnp.arange(count)
    same = owner[:, None] == owner[None, :]
    slot = jnp.sum((same & (order[None, :] < order[:, None])).astype(jnp.int32), axis=1)
    mine = (owner[None, :] == d) & (slot[None, :] == jnp.arange(SLOTS)[:, None])
    valid = jnp.any(mine, axis=1)
    my_matrix = jnp.sum(jnp.where(mine, order[None, :], 0), axis=1)

    everyone = [(g, j) for g in range(groups) for j in range(cols)]

    def ring(shift, parity):
        return [
            (g * cols + j, g * cols + (j + shift) % cols)
            for g, j in everyone
            if parity is None or (j - g) % 2 == parity
        ]

    def move(v, shift, parity=None):
        return lax.ppermute(v, ("dp", "mp"), ring(shift, parity))

    def target_slot(at):
        return ((at - core) % cols) // 2

    even = (y - core) % 2 == 0
    own_slot = target_slot(y)
    left_slot = target_slot(y - 1)

    def to_targets(pick):
        return (
            pick(own_slot),
            move(pick(left_slot), -1, 1),
            move(pick(1 - own_slot), 2, 0),
            move(pick(1 - left_slot), 1, 1),
        )

    keep = jnp.where(own_slot == 0, valid[0], valid[1])
    scalars = jnp.stack([y, own_slot, keep.astype(jnp.int32)]).astype(jnp.int32)
    basis_rows = jnp.concatenate([basis[0, :, 0], basis[0, :, 1]], axis=1)
    blocks = (basis_rows, move(basis_rows, -1), move(basis_rows, 2), move(basis_rows, 1))
    halves = prepare(scalars, blocks)
    factors = to_targets(lambda s: jnp.where(s == 0, factor[0, :, 0], factor[0, :, 1]))

    incoming = owned_gradients(partials[0], owner, slot, d)

    def block_of(s):
        return jnp.concatenate(
            [
                jnp.where(s == 0, v[:, 0], v[:, 1]).reshape(-1, v.shape[-1])
                for v in incoming
            ],
            axis=0,
        )

    pieces = to_targets(block_of)
    chosen = jnp.sum(jnp.where(mine[:, :, None], rowblock[None], 0), axis=1)
    sent = update(chosen, incoming, halves, moment1[0], moment2[0], master[0])
    received = lax.all_to_all(sent, "dp", split_axis=0, concat_axis=0, tiled=True)
    refreshed = refresh(scalars, pieces, factors, halves[0], halves[1])

    landed = jnp.take(received, owner, axis=0, mode="clip")
    block_rows = rows * cols // groups
    train_weights = jnp.where(
        (slot == 0)[:, None, None], landed[:, :block_rows], landed[:, block_rows:2 * block_rows]
    )[:, None]

    def row_block(at):
        return lax.dynamic_slice_in_dim(refreshed, ((at + cols) % cols) * rows, rows, 0)

    own = row_block(y)
    from_left = move(row_block(y + 1), 1, 0)
    from_far = move(row_block(y + 2), 2, 0)
    from_right = move(row_block(y - 1), -1, 0)
    near = jnp.where(even, own, from_left)
    far = jnp.where(even, from_far, from_right)
    near_first = jnp.where(even, own_slot, left_slot) == 0
    new_basis = jnp.stack(
        [jnp.where(near_first, near, far), jnp.where(near_first, far, near)], axis=1
    )
    return (train_weights, new_basis[None])


def solution(mesh):
    placed = (
        P("dp", None, None, "mp"),
        P(),
        P(),
        P("dp", "mp", None, None),
        P("dp", "mp", None, None),
        P("dp", None, None, "mp"),
        P("dp", None, None, "mp"),
        P("dp", None, None, "mp"),
    )

    return jax.shard_map(
        body,
        mesh=mesh,
        in_specs=placed,
        out_specs=(P(None, "dp", None, "mp"), P("dp", "mp", None, None)),
        check_vma=False,
    )
```

time: 245 us -> 241 us (0.984)
  local copies, waits for them, and re-layouts: 53.6 us -> 17.1 us
  blocking collectives: 0 us -> 34.2 us
  other arithmetic: 22.2 us -> 6.67 us
  matrix products: 13 us -> 0 us
  Pallas kernels: 38.1 us -> 51.1 us
  waiting for transfers between devices: 58.1 us -> 71 us
  starting transfers between devices: 52.5 us -> 57.9 us
  between operations: 6.15 us -> 2.34 us
    all_to_all x0 -> x1, blocking collectives: none -> 34.2 us  [exchange(): return lax.all_to_all(v, 'dp', 0, 0, axis_index_groups=lines, tiled=True)]
    unnamed x50 -> x28, local copies, waits for them, and re-layouts: 23.6 us -> 7.51 us
    dot_general x4 -> x0, matrix products: 13 us -> none  [the longest x2 7.16 us: body(): lax.dot_general(bases[s], first / (jnp.sqrt(second) + 1e-08), NN, precisi...]
    all_to_all x4 -> x3, waiting for transfers between devices: 39 us -> 52 us  [exchange(): return lax.all_to_all(v, 'dp', 0, 0, axis_index_groups=lines, tiled=True)]
    pallas_call x0 -> x2, Pallas kernels: none -> 12.2 us  [the longest x1 8.87 us: update(): pl.pallas_call(update_kernel, out_shape=jax.ShapeDtypeStruct((groups, pad...]
    ppermute x13, starting transfers between devices: 26.9 us -> 32.6 us  [the longest x12 29.3 us: move(): return lax.ppermute(v, ('dp', 'mp'), ring(shift, parity))]
    slice x3 -> x1, local copies, waits for them, and re-layouts: 5.09 us -> 0.63 us  [body(): factor[0, :, 0]]
    reshape x2 -> x0, local copies, waits for them, and re-layouts: 4.3 us -> none  [body(): shaped = weights.reshape(groups, block_rows, weights.shape[1])]
  transfers between devices with their start and end apart: 18 -> 17, of which waited for: 8 -> 7; matrix products, arithmetic and copies ran while one was open for 22% -> 4% of each run, Pallas kernels for 16% -> 21%
where the time goes in v3:
time: 241 us; the launch traced here: 240 us
  waiting for transfers between devices  71 us (29%)
  starting transfers between devices  57.9 us (24%)
  Pallas kernels  51.1 us (21%)
  blocking collectives  34.2 us (14%)
  local copies, waits for them, and re-layouts  17.1 us (7%)
  other arithmetic  6.67 us (3%)
    all_to_all x3, waiting for transfers between devices, exchange(): return lax.all_to_all(v, 'dp', 0, 0, axis_index_groups=lines, tiled=True)  52 us
    pallas_call x1, Pallas kernels, refresh(): pl.pallas_call(refresh_kernel, out_shape=jax.ShapeDtypeStruct((d, d), jnp...  39 us
    all_to_all x1, blocking collectives, exchange(): return lax.all_to_all(v, 'dp', 0, 0, axis_index_groups=lines, tiled=True)  34.2 us
    ppermute x12, starting transfers between devices, move(): return lax.ppermute(v, ('dp', 'mp'), ring(shift, parity))  29.3 us
    all_to_all x3, starting transfers between devices, exchange(): return lax.all_to_all(v, 'dp', 0, 0, axis_index_groups=lines, tiled=True)  17 us
    ppermute x12, waiting for transfers between devices, move(): return lax.ppermute(v, ('dp', 'mp'), ring(shift, parity))  14.5 us
    pallas_call x1, Pallas kernels, update(): pl.pallas_call(update_kernel, out_shape=jax.ShapeDtypeStruct((groups, pad...  8.87 us
    all_to_all x1, starting transfers between devices, body(): lax.all_to_all(sent, 'dp', split_axis=0, concat_axis=0, tiled=True)  8.4 us
  transfers between devices with their start and end apart: 17, of which 7 were waited for; matrix products, arithmetic and copies ran while one was open for 4% of the time, Pallas kernels for 21%

profile of v3, /device:TPU:1, one launch (start us, length us, event | category | flops | bytes accessed | tf_op | source)
XLA Modules:
  0.0 240.3 jit_solution(16469001457204854936)
XLA Ops:
  0.7 1.9 constant_dynamic-slice_fusion.5
  2.6 0.3 bitcast_convert_fusion
  2.9 3.3 %collective-permute-start = (f32[4,640,256]{2,1,0:T(8,128)S(1)}, f32[4,640,256]{2,1,0:T(8,128)S(1)}, u32[]{:S(2)}, u32[]{:S(2)}) collective-permute-start(f32[4,640,256]{2,1,0:T(8,128)S(1)} %bitcast_convert_fusion), channel_id=1, source_target_pairs={{0,4},{4,0},{8,12},{12,8},{16,20},{20,16},{24,28},{28,24},{32,36},... | collective-permute-start | bytes 7864328 | tf_op jit(solution)/shard_map/ppermute | solution.py:239
  6.2 4.5 %collective-permute-done = f32[4,640,256]{2,1,0:T(8,128)S(1)} collective-permute-done((f32[4,640,256]{2,1,0:T(8,128)S(1)}, f32[4,640,256]{2,1,0:T(8,128)S(1)}, u32[]{:S(2)}, u32[]{:S(2)}) %collective-permute-start) | collective-permute-done | bytes 2621472 | tf_op jit(solution)/shard_map/ppermute | solution.py:239
  10.7 0.4 convert_add_fusion
  11.1 34.2 %all_to_all.25 = f32[4,640,256]{2,1,0:T(8,128)S(1)} all-to-all(f32[4,640,256]{2,1,0:T(8,128)S(1)} %convert_add_fusion), channel_id=1, replica_groups={{0,64,128,192},{4,68,132,196},{8,72,136,200},{12,76,140,204},{16,80,144..., dimensions={0} | all-to-all | bytes 5242880 | tf_op jit(solution)/shard_map/all_to_all | solution.py:224
  45.3 1.1 reduce_sum.47
  46.3 7.2 %all-to-all-start.1 = ((f32[8,80,256]{2,1,0:T(8,128)}), f32[8,80,256]{2,1,0:T(8,128)S(1)}, u32[]{:S(2)}, u32[]{:S(2)}) async-start(f32[8,80,256]{2,1,0:T(8,128)} %bitcast.3), calls=%async_computation.1 | async-start | bytes 1310720 | tf_op jit(solution)/shard_map/all_to_all | solution.py:224
  53.6 0.1 iota_compare_fusion
  53.6 18.6 %all-to-all-done.1 = f32[8,80,256]{2,1,0:T(8,128)S(1)} async-done(((f32[8,80,256]{2,1,0:T(8,128)}), f32[8,80,256]{2,1,0:T(8,128)S(1)}, u32[]{:S(2)}, u32[]{:S(2)}) %all-to-all-start.1) | async-done | bytes 655392 | tf_op jit(solution)/shard_map/all_to_all | solution.py:224
  72.3 0.9 broadcast_in_dim.79
  73.2 6.0 %all-to-all-start.2 = ((f32[8,80,256]{2,1,0:T(8,128)}), f32[8,80,256]{2,1,0:T(8,128)S(1)}, u32[]{:S(2)}, u32[]{:S(2)}) async-start(f32[8,80,256]{2,1,0:T(8,128)} %broadcast_in_dim.79), calls=%async_computation.2 | async-start | bytes 1310720 | tf_op jit(solution)/shard_map/all_to_all | solution.py:224
  79.2 0.2 convert_reduce_fusion
  79.4 0.1 fusion.2
  79.5 0.1 select_reduce_fusion
  79.6 0.1 reshape.141
  79.7 0.1 constant_dynamic-slice_fusion.3
  79.8 0.1 copy.24
  80.0 0.1 reshape.148
  80.0 10.0 %all-to-all-done.2 = f32[8,80,256]{2,1,0:T(8,128)S(1)} async-done(((f32[8,80,256]{2,1,0:T(8,128)}), f32[8,80,256]{2,1,0:T(8,128)S(1)}, u32[]{:S(2)}, u32[]{:S(2)}) %all-to-all-start.2) | async-done | bytes 655392 | tf_op jit(solution)/shard_map/all_to_all | solution.py:224
  90.0 1.7 gather_fusion
  91.7 3.7 %all-to-all-start.3 = ((f32[8,2,80,256]{3,2,1,0:T(8,128)}), f32[8,2,80,256]{3,2,1,0:T(8,128)S(1)}, u32[]{:S(2)}, u32[]{:S(2)}) async-start(f32[8,2,80,256]{3,2,1,0:T(8,128)} %bitcast.4), calls=%async_computation.3 | async-start | bytes 2621440 | tf_op jit(solution)/shard_map/all_to_all | solution.py:224
  95.4 0.6 fusion.4
  96.1 0.0 copy-start.10
  96.1 0.1 copy_bitcast_fusion
  96.1 0.1 pad_maximum_fusion.b0
  96.2 2.8 %collective-permute-start.1 = (f32[160,1280]{1,0:T(8,128)S(1)}, f32[160,1280]{1,0:T(8,128)}, u32[]{:S(2)}, u32[]{:S(2)}) collective-permute-start(f32[160,1280]{1,0:T(8,128)S(1)} %pad_maximum_fusion.b0), channel_id=1, source_target_pairs={{0,3},{1,0},{2,1},{3,2},{4,7},{5,4},{6,5},{7,6},{8,11},{9,8},{10,9... | collective-permute-start | bytes 2457608 | tf_op jit(solution)/shard_map/ppermute | solution.py:281
  99.0 0.3 collective-permute-start.2
  99.4 0.7 collective-permute-start.3
  100.1 0.6 fusion.3
  100.8 1.2 select_bitcast_fusion.2
  102.0 4.8 %collective-permute-start.7 = (f32[160,640]{1,0:T(8,128)}, f32[160,640]{1,0:T(8,128)}, u32[]{:S(2)}, u32[]{:S(2)}) collective-permute-start(f32[160,640]{1,0:T(8,128)} %get-tuple-element.30), channel_id=1, source_target_pairs={{1,0},{3,2},{4,7},{6,5},{9,8},{11,10},{12,15},{14,13},{17,16},{19,... | collective-permute-start | bytes 1228808 | tf_op jit(solution)/shard_map/ppermute | solution.py:281
  106.8 23.4 %all-to-all-done.3.refs_0_ = f32[8,2,80,256]{3,2,1,0:T(8,128)S(1)} async-done(((f32[8,2,80,256]{3,2,1,0:T(8,128)}), f32[8,2,80,256]{3,2,1,0:T(8,128)S(1)}, u32[]{:S(2)}, u32[]{:S(2)}) %all-to-all-start.3) | async-done | bytes 1310752 | tf_op jit(solution)/shard_map/all_to_all | solution.py:224
  130.2 1.7 slice_select_fusion
  131.9 5.5 %collective-permute-start.4 = (f32[640,256]{1,0:T(8,128)}, f32[640,256]{1,0:T(8,128)}, u32[]{:S(2)}, u32[]{:S(2)}) collective-permute-start(f32[640,256]{1,0:T(8,128)} %bitcast.17), channel_id=1, source_target_pairs={{1,0},{3,2},{4,7},{6,5},{9,8},{11,10},{12,15},{14,13},{17,16},{19,... | collective-permute-start | bytes 1966088 | tf_op jit(solution)/shard_map/ppermute | solution.py:281
  137.4 1.7 collective-permute-done.7.f1
  139.1 1.5 collective-permute-start.5
  140.6 6.9 %collective-permute-start.6 = (f32[640,256]{1,0:T(8,128)}, f32[640,256]{1,0:T(8,128)}, u32[]{:S(2)}, u32[]{:S(2)}) collective-permute-start(f32[640,256]{1,0:T(8,128)} %bitcast.19), channel_id=1, source_target_pairs={{1,2},{3,0},{4,5},{6,7},{9,10},{11,8},{12,13},{14,15},{17,18},{19,... | collective-permute-start | bytes 1966088 | tf_op jit(solution)/shard_map/ppermute | solution.py:281
  147.6 0.6 fusion.5
  149.3 0.1 select_reduce_fusion.1.chosen
  149.4 0.0 collective-permute-done.2.b2
  149.4 1.4 collective-permute-start.8
  150.8 2.1 collective-permute-start.9
  152.9 0.1 pad_add_fusion.at
  153.0 3.3 %prepare.1 = (bf16[2,640,640]{2,1,0:T(8,128)(2,1)S(1)}, bf16[2,640,640]{2,1,0:T(8,128)(2,1)S(1)}, bf16[2,640,640]{2,1,0:T(8,128)(2,1)S(1)}, bf16[2,640,640]{2,1,0:T(8,128)(2,1)S(1)}) custom-call(s32[3]{0:T(128)S(1)} %pad_add_fusion.at, f32[160,1280]{1,0:T(8,128)S(1)} %pad_maximum_fusion.b0, f32[160,1280]{1,0:T(8,128)} %collective-permute-done.1.b1, ...), custom_call_target="tpu_custom_call" | custom-call | flops 3276800 | bytes 9830400 | tf_op jit(solution)/shard_map/prepare/pallas_call | solution.py:58
  156.3 8.9 %update.1 = f32[64,24,256]{2,1,0:T(8,128)} custom-call(s32[2,64]{1,0:T(2,128)S(1)} %select_reduce_fusion.1.chosen, f32[8,2,80,256]{3,2,1,0:T(8,128)S(1)} %all-to-all-done.3.refs_0_, bf16[2,640,640]{2,1,0:T(8,128)(2,1)S(1)} %get-tuple-element.6.refs_1_.b_hi, bf16[2,640,640]{2,1,0:T(8,128)(2,1)S(1)} %get-tuple-element.7.refs_2_.b_lo, ...), custom_call_target="tpu_custom_call" | custom-call | flops 2516582400 | bytes 5898240 | tf_op jit(solution)/shard_map/update/pallas_call | solution.py:101
  165.2 1.2 copy-done
  166.4 1.2 copy-done.2
  167.6 8.4 %all-to-all-start.4 = ((f32[64,24,256]{2,1,0:T(8,128)}), f32[64,24,256]{2,1,0:T(8,128)}, u32[]{:S(2)}, u32[]{:S(2)}) async-start(f32[64,24,256]{2,1,0:T(8,128)} %update.1), calls=%async_computation.4 | async-start | bytes 3145728 | tf_op jit(solution)/shard_map/all_to_all | solution.py:319
  176.1 1.4 copy-done.1
  177.5 1.4 copy-done.3
  179.0 39.0 %refresh.1 = f32[640,640]{1,0:T(8,128)S(1)} custom-call(s32[3]{0:T(128)S(1)} %pad_add_fusion.at, f32[640,256]{1,0:T(8,128)S(1)} %bitcast.50, f32[640,256]{1,0:T(8,128)} %collective-permute-done.4.g1, f32[640,256]{1,0:T(8,128)} %collective-permute-done.5.g2, f32[640,256]{1,0:T(8,128)} %collective-permute-done.6.g3, f32[160,640]{1,0:T(8,128)S(1)} %copy-done.8, ...), custom_call_target="tpu_custom_call" | custom-call | flops 22020096000 | bytes 6553600 | tf_op jit(solution)/shard_map/refresh/pallas_call | solution.py:186
  217.9 0.8 constant_dynamic-slice_fusion.2
  218.8 0.7 collective-permute-start.11
  219.5 1.3 collective-permute-start.12
  220.8 1.3 collective-permute-start.10
  222.2 11.3 %collective-permute-done.12 = f32[160,640]{1,0:T(8,128)S(1)} collective-permute-done((f32[160,640]{1,0:T(8,128)S(1)}, f32[160,640]{1,0:T(8,128)S(1)}, u32[]{:S(2)}, u32[]{:S(2)}) %collective-permute-start.12) | collective-permute-done | bytes 409632 | tf_op jit(solution)/shard_map/ppermute | solution.py:281
  233.4 1.4 collective-permute-done.10
  234.9 1.1 select_bitcast_fusion.1
  236.0 0.1 maximum_bitcast_fusion
  236.0 1.5 copy.30
  237.6 2.0 gather_fusion.1
  239.5 0.1 fusion
  239.6 0.7 copy.29
  (36 shorter events, 0.1 us)
Async XLA Ops:
  2.9 7.8 %collective-permute-start = (f32[4,640,256]{2,1,0:T(8,128)S(1)}, f32[4,640,256]{2,1,0:T(8,128)S(1)}, u32[]{:S(2)}, u32[]{:S(2)}) collective-permute-start(f32[4,640,256]{2,1,0:T(8,128)S(1)} %bitcast_convert_fusion), channel_id=1, source_target_pairs={{0,4},{4,0},{8,12},{12,8},{16,20},{20,16},{24,28},{28,24},{32,36},... | collective-permute-start | bytes 7864328 | tf_op jit(solution)/shard_map/ppermute | solution.py:239
  45.3 8.3 %copy-start.12 = (s32[8]{0:T(128)S(1)}, s32[8]{0:T(128)}, u32[]{:S(2)}) copy-start(s32[8]{0:T(128)} %param.9) | copy-start | bytes 100
  46.3 25.9 %all-to-all-start.1 = ((f32[8,80,256]{2,1,0:T(8,128)}), f32[8,80,256]{2,1,0:T(8,128)S(1)}, u32[]{:S(2)}, u32[]{:S(2)}) async-start(f32[8,80,256]{2,1,0:T(8,128)} %bitcast.3), calls=%async_computation.1 | async-start | bytes 1310720 | tf_op jit(solution)/shard_map/all_to_all | solution.py:224
  73.2 16.8 %all-to-all-start.2 = ((f32[8,80,256]{2,1,0:T(8,128)}), f32[8,80,256]{2,1,0:T(8,128)S(1)}, u32[]{:S(2)}, u32[]{:S(2)}) async-start(f32[8,80,256]{2,1,0:T(8,128)} %broadcast_in_dim.79), calls=%async_computation.2 | async-start | bytes 1310720 | tf_op jit(solution)/shard_map/all_to_all | solution.py:224
  91.7 3.7 %copy-start.9 = (f32[1,160,2,640]{3,2,1,0:T(2,128)S(1)}, f32[1,160,2,640]{3,2,1,0:T(2,128)}, u32[]{:S(2)}) copy-start(f32[1,160,2,640]{3,2,1,0:T(2,128)} %param.12) | copy-start | bytes 2457604
  91.7 38.5 %all-to-all-start.3 = ((f32[8,2,80,256]{3,2,1,0:T(8,128)}), f32[8,2,80,256]{3,2,1,0:T(8,128)S(1)}, u32[]{:S(2)}, u32[]{:S(2)}) async-start(f32[8,2,80,256]{3,2,1,0:T(8,128)} %bitcast.4), calls=%async_computation.3 | async-start | bytes 2621440 | tf_op jit(solution)/shard_map/all_to_all | solution.py:224
  96.1 4.0 %copy-start.10 = (f32[1,160,2,640]{3,2,1,0:T(2,128)S(1)}, f32[1,160,2,640]{3,2,1,0:T(2,128)}, u32[]{:S(2)}) copy-start(f32[1,160,2,640]{3,2,1,0:T(2,128)} %param.11) | copy-start | bytes 2457604
  96.2 44.4 %collective-permute-start.1 = (f32[160,1280]{1,0:T(8,128)S(1)}, f32[160,1280]{1,0:T(8,128)}, u32[]{:S(2)}, u32[]{:S(2)}) collective-permute-start(f32[160,1280]{1,0:T(8,128)S(1)} %pad_maximum_fusion.b0), channel_id=1, source_target_pairs={{0,3},{1,0},{2,1},{3,2},{4,7},{5,4},{6,5},{7,6},{8,11},{9,8},{10,9... | collective-permute-start | bytes 2457608 | tf_op jit(solution)/shard_map/ppermute | solution.py:281
  99.0 50.4 %collective-permute-start.2 = (f32[160,1280]{1,0:T(8,128)S(1)}, f32[160,1280]{1,0:T(8,128)}, u32[]{:S(2)}, u32[]{:S(2)}) collective-permute-start(f32[160,1280]{1,0:T(8,128)S(1)} %pad_maximum_fusion.b0), channel_id=1, source_target_pairs={{0,2},{1,3},{2,0},{3,1},{4,6},{5,7},{6,4},{7,5},{8,10},{9,11},{10,... | collective-permute-start | bytes 2457608 | tf_op jit(solution)/shard_map/ppermute | solution.py:281
  99.4 51.5 %collective-permute-start.3 = (f32[160,1280]{1,0:T(8,128)S(1)}, f32[160,1280]{1,0:T(8,128)}, u32[]{:S(2)}, u32[]{:S(2)}) collective-permute-start(f32[160,1280]{1,0:T(8,128)S(1)} %pad_maximum_fusion.b0), channel_id=1, source_target_pairs={{0,1},{1,2},{2,3},{3,0},{4,5},{5,6},{6,7},{7,4},{8,9},{9,10},{10,1... | collective-permute-start | bytes 2457608 | tf_op jit(solution)/shard_map/ppermute | solution.py:281
  102.0 47.3 %copy-start.11 = (s32[8,64]{1,0:T(8,128)S(1)}, s32[8,64]{1,0:T(8,128)}, u32[]{:S(2)}) copy-start(s32[8,64]{1,0:T(8,128)} %param.10) | copy-start | bytes 6148
  102.0 37.1 %collective-permute-start.7 = (f32[160,640]{1,0:T(8,128)}, f32[160,640]{1,0:T(8,128)}, u32[]{:S(2)}, u32[]{:S(2)}) collective-permute-start(f32[160,640]{1,0:T(8,128)} %get-tuple-element.30), channel_id=1, source_target_pairs={{1,0},{3,2},{4,7},{6,5},{9,8},{11,10},{12,15},{14,13},{17,16},{19,... | collective-permute-start | bytes 1228808 | tf_op jit(solution)/shard_map/ppermute | solution.py:281
  130.2 26.1 %copy-start.6 = (f32[1,2,640,256]{3,2,1,0:T(8,128)S(1)}, f32[1,2,640,256]{3,2,1,0:T(8,128)}, u32[]{:S(2)}) copy-start(f32[1,2,640,256]{3,2,1,0:T(8,128)} %param.15) | copy-start | bytes 3932164
  131.9 44.1 %collective-permute-start.4 = (f32[640,256]{1,0:T(8,128)}, f32[640,256]{1,0:T(8,128)}, u32[]{:S(2)}, u32[]{:S(2)}) collective-permute-start(f32[640,256]{1,0:T(8,128)} %bitcast.17), channel_id=1, source_target_pairs={{1,0},{3,2},{4,7},{6,5},{9,8},{11,10},{12,15},{14,13},{17,16},{19,... | collective-permute-start | bytes 1966088 | tf_op jit(solution)/shard_map/ppermute | solution.py:281
  139.1 36.9 %collective-permute-start.5 = (f32[640,256]{1,0:T(8,128)}, f32[640,256]{1,0:T(8,128)}, u32[]{:S(2)}, u32[]{:S(2)}) collective-permute-start(f32[640,256]{1,0:T(8,128)} %bitcast.18), channel_id=1, source_target_pairs={{0,2},{2,0},{5,7},{7,5},{8,10},{10,8},{13,15},{15,13},{16,18},{18,... | collective-permute-start | bytes 1966088 | tf_op jit(solution)/shard_map/ppermute | solution.py:281
  140.6 35.4 %collective-permute-start.6 = (f32[640,256]{1,0:T(8,128)}, f32[640,256]{1,0:T(8,128)}, u32[]{:S(2)}, u32[]{:S(2)}) collective-permute-start(f32[640,256]{1,0:T(8,128)} %bitcast.19), channel_id=1, source_target_pairs={{1,2},{3,0},{4,5},{6,7},{9,10},{11,8},{12,13},{14,15},{17,18},{19,... | collective-permute-start | bytes 1966088 | tf_op jit(solution)/shard_map/ppermute | solution.py:281
  149.4 26.6 %collective-permute-start.8 = (f32[160,640]{1,0:T(8,128)}, f32[160,640]{1,0:T(8,128)}, u32[]{:S(2)}, u32[]{:S(2)}) collective-permute-start(f32[160,640]{1,0:T(8,128)} %get-tuple-element.31), channel_id=1, source_target_pairs={{0,2},{2,0},{5,7},{7,5},{8,10},{10,8},{13,15},{15,13},{16,18},{18,... | collective-permute-start | bytes 1228808 | tf_op jit(solution)/shard_map/ppermute | solution.py:281
  150.8 25.2 %collective-permute-start.9 = (f32[160,640]{1,0:T(8,128)}, f32[160,640]{1,0:T(8,128)}, u32[]{:S(2)}, u32[]{:S(2)}) collective-permute-start(f32[160,640]{1,0:T(8,128)} %get-tuple-element.29), channel_id=1, source_target_pairs={{1,2},{3,0},{4,5},{6,7},{9,10},{11,8},{12,13},{14,15},{17,18},{19,... | collective-permute-start | bytes 1228808 | tf_op jit(solution)/shard_map/ppermute | solution.py:281
  153.0 3.3 %copy-start.4 = (f32[1,2,640,256]{3,2,1,0:T(8,128)S(1)}, f32[1,2,640,256]{3,2,1,0:T(8,128)}, u32[]{:S(2)}) copy-start(f32[1,2,640,256]{3,2,1,0:T(8,128)} %param.13) | copy-start | bytes 3932164
  153.0 3.3 %copy-start.5 = (f32[1,2,640,256]{3,2,1,0:T(8,128)S(1)}, f32[1,2,640,256]{3,2,1,0:T(8,128)}, u32[]{:S(2)}) copy-start(f32[1,2,640,256]{3,2,1,0:T(8,128)} %param.14) | copy-start | bytes 3932164
  165.2 1.2 copy-start
  166.4 1.2 copy-start.2
  167.6 8.5 %copy-start.7 = (f32[8,1,80,256]{3,2,1,0:T(8,128)S(1)}, f32[8,1,80,256]{3,2,1,0:T(8,128)}, u32[]{:S(2)}) copy-start(f32[8,1,80,256]{3,2,1,0:T(8,128)} %get-tuple-element.27) | copy-start | bytes 1966084
  167.6 8.5 %copy-start.8 = (f32[160,640]{1,0:T(8,128)S(1)}, f32[160,640]{1,0:T(8,128)}, u32[]{:S(2)}) copy-start(f32[160,640]{1,0:T(8,128)} %get-tuple-element.32.f0) | copy-start | bytes 1228804
  167.6 70.0 %all-to-all-start.4 = ((f32[64,24,256]{2,1,0:T(8,128)}), f32[64,24,256]{2,1,0:T(8,128)}, u32[]{:S(2)}, u32[]{:S(2)}) async-start(f32[64,24,256]{2,1,0:T(8,128)} %update.1), calls=%async_computation.4 | async-start | bytes 3145728 | tf_op jit(solution)/shard_map/all_to_all | solution.py:319
  176.1 1.4 copy-start.1
  177.5 1.4 copy-start.3
  218.8 3.4 %collective-permute-start.11 = (f32[160,640]{1,0:T(8,128)}, f32[160,640]{1,0:T(8,128)S(1)}, u32[]{:S(2)}, u32[]{:S(2)}) collective-permute-start(f32[160,640]{1,0:T(8,128)} %get-tuple-element.24), channel_id=1, source_target_pairs={{0,2},{2,0},{5,7},{7,5},{8,10},{10,8},{13,15},{15,13},{16,18},{18,... | collective-permute-start | bytes 1228808 | tf_op jit(solution)/shard_map/ppermute | solution.py:281
  219.5 14.0 %collective-permute-start.12 = (f32[160,640]{1,0:T(8,128)S(1)}, f32[160,640]{1,0:T(8,128)S(1)}, u32[]{:S(2)}, u32[]{:S(2)}) collective-permute-start(f32[160,640]{1,0:T(8,128)S(1)} %get-tuple-element.23), channel_id=1, source_target_pairs={{0,3},{2,1},{5,4},{7,6},{8,11},{10,9},{13,12},{15,14},{16,19},{18,... | collective-permute-start | bytes 1228808 | tf_op jit(solution)/shard_map/ppermute | solution.py:281
  220.8 14.1 %collective-permute-start.10 = (f32[160,640]{1,0:T(8,128)S(1)}, f32[160,640]{1,0:T(8,128)}, u32[]{:S(2)}, u32[]{:S(2)}) collective-permute-start(f32[160,640]{1,0:T(8,128)S(1)} %get-tuple-element.22), channel_id=1, source_target_pairs={{0,1},{2,3},{5,6},{7,4},{8,9},{10,11},{13,14},{15,12},{16,17},{18,... | collective-permute-start | bytes 1228808 | tf_op jit(solution)/shard_map/ppermute | solution.py:281

commit v4 on v3

--- a/solution.py
+++ b/solution.py
@@ -8,6 +8,8 @@
 
 NS_ITERS = 4
 SLOTS = 2
+BLOCK = 256
+VMEM = 63 << 20
 PARTS = (80,)
 NX, NZ, NC = 4, 8, 2
 NT = (((1,), (1,)), ((), ()))
@@ -39,48 +41,96 @@
     return [(z * PARTS[part], z * whole + lead, PARTS[part]) for z in range(NZ)]
 
 
-def prepare_kernel(at, b0, b1, b2, b3, hi_ref, lo_ref, thi_ref, tlo_ref, whole):
+def start_all(copies):
+    for copy in copies:
+        copy.start()
+
+
+def wait_all(copies):
+    for copy in copies:
+        copy.wait()
+
+
+def prepare_kernel(at, b0, b1, b2, b3, hi_ref, lo_ref, thi_ref, tlo_ref, held, whole, parts, in_sem, out_sem):
     blocks = (b0, b1, b2, b3)
     rows, d = b0.shape[0], whole.shape[0]
+    fetch = [pltpu.make_async_copy(b, held.at[k], in_sem.at[k]) for k, b in enumerate(blocks)]
+    start_all(fetch)
+    wait_all(fetch)
     starts = row_starts(at[0], rows, len(blocks))
+    stores = []
     for s in range(SLOTS):
-        for start, block in zip(starts, blocks):
-            whole[pl.ds(start, rows), :] = block[:, s * d:(s + 1) * d]
+        for k, start in enumerate(starts):
+            whole[pl.ds(start, rows), :] = held[k, :, s * d:(s + 1) * d]
         b = whole[...]
-        hi_ref[s], lo_ref[s] = split(b)
-        thi_ref[s], tlo_ref[s] = split(b.T)
+        parts[0, s], parts[1, s] = split(b)
+        parts[2, s], parts[3, s] = split(b.T)
+        mine = [
+            pltpu.make_async_copy(parts.at[k, s], ref.at[s], out_sem.at[k, s])
+            for k, ref in enumerate((hi_ref, lo_ref, thi_ref, tlo_ref))
+        ]
+        start_all(mine)
+        stores += mine
+    wait_all(stores)
 
 
 def prepare(scalars, blocks):
-    d = blocks[0].shape[1] // SLOTS
+    rows, wide = blocks[0].shape
+    d = wide // SLOTS
     half = jax.ShapeDtypeStruct((SLOTS, d, d), jnp.bfloat16)
-    vmem = pl.BlockSpec(memory_space=pltpu.VMEM)
+    hbm = pl.BlockSpec(memory_space=pltpu.HBM)
     return pl.pallas_call(
         prepare_kernel,
         out_shape=[half] * 4,
-        in_specs=[pl.BlockSpec(memory_space=pltpu.SMEM)] + [vmem] * 4,
-        out_specs=[vmem] * 4,
-        scratch_shapes=[pltpu.VMEM((d, d), jnp.float32)],
-        compiler_params=pltpu.CompilerParams(vmem_limit_bytes=24 << 20),
+        in_specs=[pl.BlockSpec(memory_space=pltpu.SMEM)] + [hbm] * 4,
+        out_specs=[hbm] * 4,
+        scratch_shapes=[
+            pltpu.VMEM((4, rows, wide), jnp.float32),
+            pltpu.VMEM((d, d), jnp.float32),
+            pltpu.VMEM((4, SLOTS, d, d), jnp.bfloat16),
+            pltpu.SemaphoreType.DMA((4,)),
+            pltpu.SemaphoreType.DMA((4, SLOTS)),
+        ],
+        compiler_params=pltpu.CompilerParams(vmem_limit_bytes=VMEM),
         cost_estimate=pl.CostEstimate(flops=8 * d * d, bytes_accessed=24 * d * d, transcendentals=0),
         name="prepare",
     )(scalars, *blocks)
 
 
 def update_kernel(chosen, *refs):
-    incoming = refs[:len(PARTS)]
-    hi, lo, thi, tlo, m1, m2, held, out, gh, gl, weights = refs[len(PARTS):]
+    count = len(PARTS)
+    incoming, sources, states, out = refs[:count], refs[count:count + 4], refs[count + 4:count + 7], refs[count + 7]
+    scratch = refs[count + 8:]
+    came, (parts, state, gh, gl, weights, came_sem, part_sem, state_sem) = scratch[:count], scratch[count:]
     groups = out.shape[0]
-    block = held.shape[1] // groups
+    block = state.shape[2] // groups
+    order = (2, 3, 0, 1)
+    get_came = [pltpu.make_async_copy(r, c, came_sem.at[k]) for k, (r, c) in enumerate(zip(incoming, came))]
+    get_part = [
+        [pltpu.make_async_copy(sources[k].at[s], parts.at[k, s], part_sem.at[k, s]) for k in order]
+        for s in range(SLOTS)
+    ]
+    get_state = [
+        [pltpu.make_async_copy(r.at[s], state.at[k, s], state_sem.at[k, s]) for k, r in enumerate(states)]
+        for s in range(SLOTS)
+    ]
+    start_all(get_came)
     for s in range(SLOTS):
-        for part, ref in enumerate(incoming):
+        start_all(get_part[s])
+        start_all(get_state[s])
+    wait_all(get_came)
+    for s in range(SLOTS):
+        for part, ref in enumerate(came):
             for z, (_, row, size) in enumerate(scattered(part)):
                 gh[row:row + size], gl[row:row + size] = split(ref[z, s])
-        turned = mm3((thi[s], tlo[s]), (gh[...], gl[...]))
-        first = 0.9 * m1[s] + 0.1 * turned
-        second = 0.95 * m2[s] + 0.05 * turned * turned
-        direction = mm3((hi[s], lo[s]), split(first / (jnp.sqrt(second) + 1e-08)))
-        fresh = held[s] - 0.1 * (direction + 0.1 * held[s])
+        wait_all(get_part[s][:2])
+        turned = mm3((parts[2, s], parts[3, s]), (gh[...], gl[...]))
+        wait_all(get_state[s])
+        first = 0.9 * state[0, s] + 0.1 * turned
+        second = 0.95 * state[1, s] + 0.05 * turned * turned
+        wait_all(get_part[s][2:])
+        direction = mm3((parts[0, s], parts[1, s]), split(first / (jnp.sqrt(second) + 1e-08)))
+        fresh = state[2, s] - 0.1 * (direction + 0.1 * state[2, s])
         here = slice(s * block, (s + 1) * block)
         for j in range(groups):
             weights[j, here, :] = fresh[j * block:(j + 1) * block]
@@ -97,18 +147,24 @@
     d, cols = m1.shape[1:]
     block = d // groups
     padded = -(-SLOTS * block // 8) * 8
-    vmem = pl.BlockSpec(memory_space=pltpu.VMEM)
+    hbm = pl.BlockSpec(memory_space=pltpu.HBM)
     return pl.pallas_call(
         update_kernel,
         out_shape=jax.ShapeDtypeStruct((groups, padded, cols), jnp.float32),
-        in_specs=[pl.BlockSpec(memory_space=pltpu.SMEM)] + [vmem] * (7 + len(PARTS)),
-        out_specs=vmem,
-        scratch_shapes=[
+        in_specs=[pl.BlockSpec(memory_space=pltpu.SMEM)] + [hbm] * (7 + len(PARTS)),
+        out_specs=pl.BlockSpec(memory_space=pltpu.VMEM),
+        scratch_shapes=[pltpu.VMEM(v.shape, jnp.float32) for v in incoming]
+        + [
+            pltpu.VMEM((4, SLOTS, d, d), jnp.bfloat16),
+            pltpu.VMEM((3, SLOTS, d, cols), jnp.float32),
             pltpu.VMEM((d, cols), jnp.bfloat16),
             pltpu.VMEM((d, cols), jnp.bfloat16),
             pltpu.VMEM((groups, padded, cols), jnp.float32),
+            pltpu.SemaphoreType.DMA((len(PARTS),)),
+            pltpu.SemaphoreType.DMA((4, SLOTS)),
+            pltpu.SemaphoreType.DMA((3, SLOTS)),
         ],
-        compiler_params=pltpu.CompilerParams(vmem_limit_bytes=24 << 20),
+        compiler_params=pltpu.CompilerParams(vmem_limit_bytes=VMEM),
         cost_estimate=pl.CostEstimate(
             flops=24 * d * d * cols, bytes_accessed=36 * d * cols, transcendentals=2 * d * cols
         ),
@@ -116,63 +172,86 @@
     )(chosen, *incoming, *halves, m1, m2, held)
 
 
-def refresh_kernel(at, g0, g1, g2, g3, f0, f1, f2, f3, b_hi, b_lo, o_ref, gl, gr, left, right, stack, x_ref):
+def refresh_kernel(
+    at, g0, g1, g2, g3, f0, f1, f2, f3, b_hi, b_lo, o_ref,
+    g_in, f_in, gbuf, xbuf, abuf, stack, x_ref, a_ref, g_sem, f_sem, b_sem,
+):
     d = x_ref.shape[0]
     w = g0.shape[1]
     kc = 4 * w
-    for b, g_ref in enumerate((g0, g1, g2, g3)):
+    rows = f0.shape[0]
+    get_g = [pltpu.make_async_copy(r, g_in.at[k], g_sem.at[k]) for k, r in enumerate((g0, g1, g2, g3))]
+    get_f = [
+        pltpu.make_async_copy(r, f_in.at[pl.ds(start, rows)], f_sem.at[k])
+        for k, (r, start) in enumerate(zip((f0, f1, f2, f3), row_starts(at[0], rows, 4)))
+    ]
+    get_b = [
+        pltpu.make_async_copy(r.at[at[1]], stack.at[pl.ds(k * d, d)], b_sem.at[k])
+        for k, r in enumerate((b_hi, b_hi, b_lo))
+    ]
+    start_all(get_g)
+    start_all(get_f)
+    start_all(get_b)
+
+    def put(buf, k, v, r=0, c=0):
+        hi, lo = split(v)
+        n, m = v.shape
+        buf[r:r + n, c:c + m] = lo
+        buf[r:r + n, k + c:k + c + m] = hi
+        buf[r:r + n, 2 * k + c:2 * k + c + m] = hi
+        return hi, lo
+
+    def gram(buf, k, use):
+        for c in range(0, d, BLOCK):
+            e = min(c + BLOCK, d)
+            p = mm(buf[c:, :2 * k], buf[c:e, k:], NT) + mm(buf[c:, k:2 * k], buf[c:e, :k], NT)
+            use(p, c, c)
+            if e < d:
+                use(p[e - c:].T, c, e)
+
+    def times_stack():
+        return mm(abuf[:, :2 * d], stack[:2 * d], NN) + mm(abuf[:, d:2 * d], stack[2 * d:], NN)
+
+    for b in range(4):
+        get_g[b].wait()
         base = 0
         for part in range(len(PARTS)):
             for source, row, size in scattered(part):
-                hi, lo = split(g_ref[base + source:base + source + size])
-                gl[row:row + size, b * w:(b + 1) * w] = hi
-                gl[row:row + size, kc + b * w:kc + (b + 1) * w] = hi
-                gl[row:row + size, 2 * kc + b * w:2 * kc + (b + 1) * w] = lo
-                gr[row:row + size, b * w:(b + 1) * w] = hi
-                gr[row:row + size, kc + b * w:kc + (b + 1) * w] = lo
-                gr[row:row + size, 2 * kc + b * w:2 * kc + (b + 1) * w] = hi
+                put(gbuf, kc, g_in[b, base + source:base + source + size], row, b * w)
             base += NZ * PARTS[part]
-
-    def put_left(v):
-        hi, lo = split(v)
-        left[:, :d] = hi
-        left[:, d:2 * d] = hi
-        left[:, 2 * d:] = lo
-        return hi, lo
-
-    def put_right(hi, lo):
-        right[:, :d] = hi
-        right[:, d:2 * d] = lo
-        right[:, 2 * d:] = hi
-
-    def put_stack(hi, lo):
-        stack[:d] = hi
-        stack[d:2 * d] = lo
-        stack[2 * d:] = hi
-
-    x_ref[...] = mm(gl[...], gr[...], NT)
-    rows = f0.shape[0]
-    for start, f_ref in zip(row_starts(at[0], rows, 4), (f0, f1, f2, f3)):
-        here = pl.ds(start, rows)
-        hi, lo = split(0.95 * f_ref[...] + 0.05 * x_ref[here, :])
-        left[here, :d] = hi
-        left[here, d:2 * d] = hi
-        left[here, 2 * d:] = lo
-    put_stack(b_hi[at[1]], b_lo[at[1]])
-    power = mm(left[...], stack[...], NN)
+    wait_all(get_f)
+
+    def use_outer(v, r, c):
+        n, m = v.shape
+        put(abuf, d, 0.95 * f_in[r:r + n, c:c + m] + 0.05 * v, r, c)
+
+    gram(gbuf, kc, use_outer)
+    wait_all(get_b)
+    power = times_stack()
     total = jnp.sum(power * power)
     x_ref[...] = power / jnp.sqrt(jnp.full((1, 1), total + 1e-06, jnp.float32))
 
     def step(_, carry):
-        hi, lo = put_left(x_ref[...])
-        put_stack(hi, lo)
-        put_right(hi, lo)
-        inner = mm(left[...], right[...], NT)
-        hi, lo = put_left(inner)
-        put_right(hi, lo)
-        squared = mm(left[...], right[...], NT)
-        put_left(-4.775 * inner + 2.0315 * squared)
-        x_ref[...] = 3.4445 * x_ref[...] + mm(left[...], stack[...], NN)
+        hi, lo = put(xbuf, d, x_ref[...])
+        stack[:d] = hi
+        stack[d:2 * d] = hi
+        stack[2 * d:] = lo
+
+        def use_inner(v, r, c):
+            n, m = v.shape
+            a_ref[r:r + n, c:c + m] = v
+            put(abuf, d, v, r, c)
+
+        def use_squared(v, r, c):
+            n, m = v.shape
+            a_ref[r:r + n, c:c + m] = -4.775 * a_ref[r:r + n, c:c + m] + 2.0315 * v
+
+        gram(xbuf, d, use_inner)
+        gram(abuf, d, use_squared)
+        hi, lo = split(a_ref[...])
+        abuf[:, :d] = lo
+        abuf[:, d:2 * d] = hi
+        x_ref[...] = 3.4445 * x_ref[...] + times_stack()
         return carry
 
     lax.fori_loop(0, NS_ITERS, step, 0)
@@ -181,24 +260,29 @@
 
 def refresh(scalars, pieces, factors, b_hi, b_lo):
     d = factors[0].shape[1]
-    kc = 4 * pieces[0].shape[1]
-    vmem = pl.BlockSpec(memory_space=pltpu.VMEM)
+    w = pieces[0].shape[1]
+    hbm = pl.BlockSpec(memory_space=pltpu.HBM)
     return pl.pallas_call(
         refresh_kernel,
         out_shape=jax.ShapeDtypeStruct((d, d), jnp.float32),
-        in_specs=[pl.BlockSpec(memory_space=pltpu.SMEM)] + [vmem] * 10,
-        out_specs=vmem,
+        in_specs=[pl.BlockSpec(memory_space=pltpu.SMEM)] + [hbm] * 10,
+        out_specs=pl.BlockSpec(memory_space=pltpu.VMEM),
         scratch_shapes=[
-            pltpu.VMEM((d, 3 * kc), jnp.bfloat16),
-            pltpu.VMEM((d, 3 * kc), jnp.bfloat16),
+            pltpu.VMEM((4, d, w), jnp.float32),
+            pltpu.VMEM((d, d), jnp.float32),
+            pltpu.VMEM((d, 12 * w), jnp.bfloat16),
             pltpu.VMEM((d, 3 * d), jnp.bfloat16),
             pltpu.VMEM((d, 3 * d), jnp.bfloat16),
             pltpu.VMEM((3 * d, d), jnp.bfloat16),
             pltpu.VMEM((d, d), jnp.float32),
+            pltpu.VMEM((d, d), jnp.float32),
+            pltpu.SemaphoreType.DMA((4,)),
+            pltpu.SemaphoreType.DMA((4,)),
+            pltpu.SemaphoreType.DMA((3,)),
         ],
-        compiler_params=pltpu.CompilerParams(vmem_limit_bytes=40 << 20),
+        compiler_params=pltpu.CompilerParams(vmem_limit_bytes=VMEM),
         cost_estimate=pl.CostEstimate(
-            flops=6 * 14 * d**3, bytes_accessed=16 * d * d, transcendentals=0
+            flops=6 * 10 * d**3, bytes_accessed=16 * d * d, transcendentals=0
         ),
         name="refresh",
     )(scalars, *pieces, *factors, b_hi, b_lo)

time: 241 us -> 256 us (1.062)
  waiting for transfers between devices: 71 us -> 91.9 us
  starting transfers between devices: 57.9 us -> 53.5 us
  local copies, waits for them, and re-layouts: 17.1 us -> 13.3 us
    ppermute x12, waiting for transfers between devices: 14.5 us -> 58.9 us  [move(): return lax.ppermute(v, ('dp', 'mp'), ring(shift, parity))]
    all_to_all x3, waiting for transfers between devices: 52 us -> 28.5 us  [exchange(): return lax.all_to_all(v, 'dp', 0, 0, axis_index_groups=lines, tiled=True)]
    pallas_call x1, Pallas kernels: 39 us -> 30.6 us  [refresh(): pl.pallas_call(refresh_kernel, out_shape=jax.ShapeDtypeStruct((d, d), jnp...]
    ppermute x12, starting transfers between devices: 29.3 us -> 23.9 us  [move(): return lax.ppermute(v, ('dp', 'mp'), ring(shift, parity))]
    pallas_call x1, Pallas kernels: 8.87 us -> 14 us  [update(): pl.pallas_call(update_kernel, out_shape=jax.ShapeDtypeStruct((groups, pad...]
    unnamed x28 -> x22, local copies, waits for them, and re-layouts: 7.51 us -> 3.18 us
    pallas_call x1, Pallas kernels: 3.29 us -> 6.42 us  [prepare(): pl.pallas_call(prepare_kernel, out_shape=[half] * 4, in_specs=[pl.BlockSp...]
  transfers between devices with their start and end apart: 17 -> 17, of which waited for: 7 -> 9; matrix products, arithmetic and copies ran while one was open for 4% -> 5% of each run, Pallas kernels for 21% -> 20%
where the time goes in v4:
time: 256 us; the launch traced here: 255 us
  waiting for transfers between devices  91.9 us (36%)
  starting transfers between devices  53.5 us (21%)
  Pallas kernels  51.1 us (20%)
  blocking collectives  34.2 us (13%)
  local copies, waits for them, and re-layouts  13.3 us (5%)
  other arithmetic  8.62 us (3%)
    ppermute x12, waiting for transfers between devices, move(): return lax.ppermute(v, ('dp', 'mp'), ring(shift, parity))  58.9 us
    all_to_all x1, blocking collectives, exchange(): return lax.all_to_all(v, 'dp', 0, 0, axis_index_groups=lines, tiled=True)  34.2 us
    pallas_call x1, Pallas kernels, refresh(): pl.pallas_call(refresh_kernel, out_shape=jax.ShapeDtypeStruct((d, d), jnp...  30.6 us
    all_to_all x3, waiting for transfers between devices, exchange(): return lax.all_to_all(v, 'dp', 0, 0, axis_index_groups=lines, tiled=True)  28.5 us
    ppermute x12, starting transfers between devices, move(): return lax.ppermute(v, ('dp', 'mp'), ring(shift, parity))  23.9 us
    all_to_all x3, starting transfers between devices, exchange(): return lax.all_to_all(v, 'dp', 0, 0, axis_index_groups=lines, tiled=True)  17.7 us
    pallas_call x1, Pallas kernels, update(): pl.pallas_call(update_kernel, out_shape=jax.ShapeDtypeStruct((groups, pad...  14 us
    all_to_all x1, starting transfers between devices, body(): lax.all_to_all(sent, 'dp', split_axis=0, concat_axis=0, tiled=True)  8.62 us
  transfers between devices with their start and end apart: 17, of which 9 were waited for; matrix products, arithmetic and copies ran while one was open for 5% of the time, Pallas kernels for 20%

profile of v4, /device:TPU:1, one launch (start us, length us, event | category | flops | bytes accessed | tf_op | source)
XLA Modules:
  0.0 254.9 jit_solution(18065344657226715243)
XLA Ops:
  0.7 1.9 constant_dynamic-slice_fusion.5
  2.6 0.3 bitcast_convert_fusion
  2.9 3.3 %collective-permute-start = (f32[4,640,256]{2,1,0:T(8,128)S(1)}, f32[4,640,256]{2,1,0:T(8,128)S(1)}, u32[]{:S(2)}, u32[]{:S(2)}) collective-permute-start(f32[4,640,256]{2,1,0:T(8,128)S(1)} %bitcast_convert_fusion), channel_id=1, source_target_pairs={{0,4},{4,0},{8,12},{12,8},{16,20},{20,16},{24,28},{28,24},{32,36},... | collective-permute-start | bytes 7864328 | tf_op jit(solution)/shard_map/ppermute | solution.py:323
  6.2 4.5 %collective-permute-done = f32[4,640,256]{2,1,0:T(8,128)S(1)} collective-permute-done((f32[4,640,256]{2,1,0:T(8,128)S(1)}, f32[4,640,256]{2,1,0:T(8,128)S(1)}, u32[]{:S(2)}, u32[]{:S(2)}) %collective-permute-start) | collective-permute-done | bytes 2621472 | tf_op jit(solution)/shard_map/ppermute | solution.py:323
  10.7 0.4 convert_add_fusion
  11.1 34.2 %all_to_all.25 = f32[4,640,256]{2,1,0:T(8,128)S(1)} all-to-all(f32[4,640,256]{2,1,0:T(8,128)S(1)} %convert_add_fusion), channel_id=1, replica_groups={{0,64,128,192},{4,68,132,196},{8,72,136,200},{12,76,140,204},{16,80,144..., dimensions={0} | all-to-all | bytes 5242880 | tf_op jit(solution)/shard_map/all_to_all | solution.py:308
  45.3 1.1 reduce_sum.47
  46.3 7.2 %all-to-all-start.1 = ((f32[8,80,256]{2,1,0:T(8,128)}), f32[8,80,256]{2,1,0:T(8,128)S(1)}, u32[]{:S(2)}, u32[]{:S(2)}) async-start(f32[8,80,256]{2,1,0:T(8,128)} %bitcast.3), calls=%async_computation.1 | async-start | bytes 1310720 | tf_op jit(solution)/shard_map/all_to_all | solution.py:308
  53.6 0.1 iota_compare_fusion
  53.6 18.6 %all-to-all-done.1 = f32[8,80,256]{2,1,0:T(8,128)S(1)} async-done(((f32[8,80,256]{2,1,0:T(8,128)}), f32[8,80,256]{2,1,0:T(8,128)S(1)}, u32[]{:S(2)}, u32[]{:S(2)}) %all-to-all-start.1) | async-done | bytes 655392 | tf_op jit(solution)/shard_map/all_to_all | solution.py:308
  72.3 0.9 broadcast_in_dim.79
  73.2 6.0 %all-to-all-start.2 = ((f32[8,80,256]{2,1,0:T(8,128)}), f32[8,80,256]{2,1,0:T(8,128)S(1)}, u32[]{:S(2)}, u32[]{:S(2)}) async-start(f32[8,80,256]{2,1,0:T(8,128)} %broadcast_in_dim.79), calls=%async_computation.2 | async-start | bytes 1310720 | tf_op jit(solution)/shard_map/all_to_all | solution.py:308
  79.2 0.2 convert_reduce_fusion
  79.4 0.1 fusion.2
  79.5 0.1 select_reduce_fusion
  79.6 0.1 reshape.141
  79.7 0.1 constant_dynamic-slice_fusion.3
  79.8 0.1 copy.24
  80.0 0.1 reshape.148
  80.0 10.0 %all-to-all-done.2 = f32[8,80,256]{2,1,0:T(8,128)S(1)} async-done(((f32[8,80,256]{2,1,0:T(8,128)}), f32[8,80,256]{2,1,0:T(8,128)S(1)}, u32[]{:S(2)}, u32[]{:S(2)}) %all-to-all-start.2) | async-done | bytes 655392 | tf_op jit(solution)/shard_map/all_to_all | solution.py:308
  90.0 1.7 gather_fusion
  91.7 4.4 %all-to-all-start.3 = ((f32[8,2,80,256]{3,2,1,0:T(8,128)}), f32[8,2,80,256]{3,2,1,0:T(8,128)}, u32[]{:S(2)}, u32[]{:S(2)}) async-start(f32[8,2,80,256]{3,2,1,0:T(8,128)} %bitcast.4), calls=%async_computation.3 | async-start | bytes 2621440 | tf_op jit(solution)/shard_map/all_to_all | solution.py:308
  96.1 0.6 fusion.4
  96.7 0.0 copy-start.2
  96.8 0.1 copy_bitcast_fusion
  96.8 0.1 pad_maximum_fusion.b0
  96.9 0.0 copy-start
  96.9 2.8 %collective-permute-start.1 = (f32[160,1280]{1,0:T(8,128)S(1)}, f32[160,1280]{1,0:T(8,128)S(1)}, u32[]{:S(2)}, u32[]{:S(2)}) collective-permute-start(f32[160,1280]{1,0:T(8,128)S(1)} %pad_maximum_fusion.b0), channel_id=1, source_target_pairs={{0,3},{1,0},{2,1},{3,2},{4,7},{5,4},{6,5},{7,6},{8,11},{9,8},{10,9... | collective-permute-start | bytes 2457608 | tf_op jit(solution)/shard_map/ppermute | solution.py:365
  99.7 0.3 collective-permute-start.2
  100.1 0.7 collective-permute-start.3
  100.8 0.6 fusion.3
  101.4 0.0 copy-start.7
  101.4 1.3 select_bitcast_fusion.2
  102.7 4.7 %collective-permute-start.7 = (f32[160,640]{1,0:T(8,128)}, f32[160,640]{1,0:T(8,128)}, u32[]{:S(2)}, u32[]{:S(2)}) collective-permute-start(f32[160,640]{1,0:T(8,128)} %get-tuple-element.30), channel_id=1, source_target_pairs={{1,0},{3,2},{4,7},{6,5},{9,8},{11,10},{12,15},{14,13},{17,16},{19,... | collective-permute-start | bytes 1228808 | tf_op jit(solution)/shard_map/ppermute | solution.py:365
  107.3 0.6 fusion.5
  109.3 0.6 pad_add_fusion.at
  109.9 0.6 select_reduce_fusion.1.chosen
  110.5 6.9 %collective-permute-done.1.b1 = f32[160,1280]{1,0:T(8,128)S(1)} collective-permute-done((f32[160,1280]{1,0:T(8,128)S(1)}, f32[160,1280]{1,0:T(8,128)S(1)}, u32[]{:S(2)}, u32[]{:S(2)}) %collective-permute-start.1) | collective-permute-done | bytes 819232 | tf_op jit(solution)/shard_map/ppermute | solution.py:365
  117.4 2.4 collective-permute-done.2.b2
  119.8 0.9 copy-done.4
  120.7 18.3 %collective-permute-done.3.b3 = f32[160,1280]{1,0:T(8,128)} collective-permute-done((f32[160,1280]{1,0:T(8,128)S(1)}, f32[160,1280]{1,0:T(8,128)}, u32[]{:S(2)}, u32[]{:S(2)}) %collective-permute-start.3) | collective-permute-done | bytes 819232 | tf_op jit(solution)/shard_map/ppermute | solution.py:365
  139.0 6.4 %prepare.1 = (bf16[2,640,640]{2,1,0:T(8,128)(2,1)}, bf16[2,640,640]{2,1,0:T(8,128)(2,1)}, bf16[2,640,640]{2,1,0:T(8,128)(2,1)}, bf16[2,640,640]{2,1,0:T(8,128)(2,1)}) custom-call(s32[3]{0:T(128)} %pad_add_fusion.at, f32[160,1280]{1,0:T(8,128)} %copy-done, f32[160,1280]{1,0:T(8,128)} %copy-done.3, f32[160,1280]{1,0:T(8,128)} %copy-done.4, ...), custom_call_target="tpu_custom_call" | custom-call | flops 3276800 | bytes 9830400 | tf_op jit(solution)/shard_map/prepare/pallas_call | solution.py:82
  145.5 14.0 %update.1 = f32[64,24,256]{2,1,0:T(8,128)} custom-call(s32[2,64]{1,0:T(2,128)} %select_reduce_fusion.1.chosen, f32[8,2,80,256]{3,2,1,0:T(8,128)} %all-to-all-done.3.refs_0_, bf16[2,640,640]{2,1,0:T(8,128)(2,1)} %get-tuple-element.6.refs_1_.b_hi, bf16[2,640,640]{2,1,0:T(8,128)(2,1)} %get-tuple-element.7.refs_2_.b_lo, ...), custom_call_target="tpu_custom_call" | custom-call | flops 2516582400 | bytes 5898240 | tf_op jit(solution)/shard_map/update/pallas_call | solution.py:151
  159.5 8.6 %all-to-all-start.4 = ((f32[64,24,256]{2,1,0:T(8,128)}), f32[64,24,256]{2,1,0:T(8,128)}, u32[]{:S(2)}, u32[]{:S(2)}) async-start(f32[64,24,256]{2,1,0:T(8,128)} %update.1), calls=%async_computation.4 | async-start | bytes 3145728 | tf_op jit(solution)/shard_map/all_to_all | solution.py:403
  168.1 2.5 slice_select_fusion
  170.7 5.2 %collective-permute-start.4 = (f32[640,256]{1,0:T(8,128)S(1)}, f32[640,256]{1,0:T(8,128)}, u32[]{:S(2)}, u32[]{:S(2)}) collective-permute-start(f32[640,256]{1,0:T(8,128)S(1)} %bitcast.54), channel_id=1, source_target_pairs={{1,0},{3,2},{4,7},{6,5},{9,8},{11,10},{12,15},{14,13},{17,16},{19,... | collective-permute-start | bytes 1966088 | tf_op jit(solution)/shard_map/ppermute | solution.py:365
  175.9 1.5 collective-permute-start.5
  177.4 2.2 collective-permute-start.6
  179.6 0.7 collective-permute-start.8
  180.4 2.5 collective-permute-start.9
  182.8 15.7 %collective-permute-done.9.f3 = f32[160,640]{1,0:T(8,128)} collective-permute-done((f32[160,640]{1,0:T(8,128)S(1)}, f32[160,640]{1,0:T(8,128)}, u32[]{:S(2)}, u32[]{:S(2)}) %collective-permute-start.9) | collective-permute-done | bytes 409632 | tf_op jit(solution)/shard_map/ppermute | solution.py:365
  198.5 30.6 %refresh.1 = f32[640,640]{1,0:T(8,128)} custom-call(s32[3]{0:T(128)} %pad_add_fusion.at, f32[640,256]{1,0:T(8,128)} %bitcast.51, f32[640,256]{1,0:T(8,128)} %collective-permute-done.4.g1, f32[640,256]{1,0:T(8,128)} %collective-permute-done.5.g2, f32[640,256]{1,0:T(8,128)} %collective-permute-done.6.g3, f32[160,640]{1,0:T(8,128)} %get-tuple-element.32.f0, ...), custom_call_target="tpu_custom_call" | custom-call | flops 15728640000 | bytes 6553600 | tf_op jit(solution)/shard_map/refresh/pallas_call | solution.py:265
  229.2 1.3 constant_dynamic-slice_fusion.2
  230.5 0.7 collective-permute-start.11
  231.2 1.3 collective-permute-start.12
  232.5 1.3 collective-permute-start.10
  233.9 12.6 %collective-permute-done.12 = f32[160,640]{1,0:T(8,128)S(1)} collective-permute-done((f32[160,640]{1,0:T(8,128)S(1)}, f32[160,640]{1,0:T(8,128)S(1)}, u32[]{:S(2)}, u32[]{:S(2)}) %collective-permute-start.12) | collective-permute-done | bytes 409632 | tf_op jit(solution)/shard_map/ppermute | solution.py:365
  246.5 3.0 %collective-permute-done.10 = f32[160,640]{1,0:T(8,128)S(1)} collective-permute-done((f32[160,640]{1,0:T(8,128)S(1)}, f32[160,640]{1,0:T(8,128)S(1)}, u32[]{:S(2)}, u32[]{:S(2)}) %collective-permute-start.10) | collective-permute-done | bytes 409632 | tf_op jit(solution)/shard_map/ppermute | solution.py:365
  249.5 1.1 select_bitcast_fusion.1
  250.6 0.1 maximum_bitcast_fusion
  250.6 1.5 copy.30
  252.2 2.0 gather_fusion.1
  254.1 0.1 fusion
  254.2 0.7 copy.29
  (30 shorter events, 0.1 us)
Async XLA Ops:
  2.9 7.8 %collective-permute-start = (f32[4,640,256]{2,1,0:T(8,128)S(1)}, f32[4,640,256]{2,1,0:T(8,128)S(1)}, u32[]{:S(2)}, u32[]{:S(2)}) collective-permute-start(f32[4,640,256]{2,1,0:T(8,128)S(1)} %bitcast_convert_fusion), channel_id=1, source_target_pairs={{0,4},{4,0},{8,12},{12,8},{16,20},{20,16},{24,28},{28,24},{32,36},... | collective-permute-start | bytes 7864328 | tf_op jit(solution)/shard_map/ppermute | solution.py:323
  45.3 8.3 %copy-start.8 = (s32[8]{0:T(128)S(1)}, s32[8]{0:T(128)}, u32[]{:S(2)}) copy-start(s32[8]{0:T(128)} %param.9) | copy-start | bytes 100
  46.3 25.9 %all-to-all-start.1 = ((f32[8,80,256]{2,1,0:T(8,128)}), f32[8,80,256]{2,1,0:T(8,128)S(1)}, u32[]{:S(2)}, u32[]{:S(2)}) async-start(f32[8,80,256]{2,1,0:T(8,128)} %bitcast.3), calls=%async_computation.1 | async-start | bytes 1310720 | tf_op jit(solution)/shard_map/all_to_all | solution.py:308
  73.2 16.8 %all-to-all-start.2 = ((f32[8,80,256]{2,1,0:T(8,128)}), f32[8,80,256]{2,1,0:T(8,128)S(1)}, u32[]{:S(2)}, u32[]{:S(2)}) async-start(f32[8,80,256]{2,1,0:T(8,128)} %broadcast_in_dim.79), calls=%async_computation.2 | async-start | bytes 1310720 | tf_op jit(solution)/shard_map/all_to_all | solution.py:308
  91.7 4.4 %copy-start.1 = (f32[1,160,2,640]{3,2,1,0:T(2,128)S(1)}, f32[1,160,2,640]{3,2,1,0:T(2,128)}, u32[]{:S(2)}) copy-start(f32[1,160,2,640]{3,2,1,0:T(2,128)} %param.12) | copy-start | bytes 2457604
  91.7 53.8 %all-to-all-start.3 = ((f32[8,2,80,256]{3,2,1,0:T(8,128)}), f32[8,2,80,256]{3,2,1,0:T(8,128)}, u32[]{:S(2)}, u32[]{:S(2)}) async-start(f32[8,2,80,256]{3,2,1,0:T(8,128)} %bitcast.4), calls=%async_computation.3 | async-start | bytes 2621440 | tf_op jit(solution)/shard_map/all_to_all | solution.py:308
  96.7 4.0 %copy-start.2 = (f32[1,160,2,640]{3,2,1,0:T(2,128)S(1)}, f32[1,160,2,640]{3,2,1,0:T(2,128)}, u32[]{:S(2)}) copy-start(f32[1,160,2,640]{3,2,1,0:T(2,128)} %param.11) | copy-start | bytes 2457604
  96.9 5.8 %copy-start = (f32[160,1280]{1,0:T(8,128)}, f32[160,1280]{1,0:T(8,128)S(1)}, u32[]{:S(2)}) copy-start(f32[160,1280]{1,0:T(8,128)S(1)} %pad_maximum_fusion.b0) | copy-start | bytes 2457604
  96.9 20.5 %collective-permute-start.1 = (f32[160,1280]{1,0:T(8,128)S(1)}, f32[160,1280]{1,0:T(8,128)S(1)}, u32[]{:S(2)}, u32[]{:S(2)}) collective-permute-start(f32[160,1280]{1,0:T(8,128)S(1)} %pad_maximum_fusion.b0), channel_id=1, source_target_pairs={{0,3},{1,0},{2,1},{3,2},{4,7},{5,4},{6,5},{7,6},{8,11},{9,8},{10,9... | collective-permute-start | bytes 2457608 | tf_op jit(solution)/shard_map/ppermute | solution.py:365
  99.7 20.1 %collective-permute-start.2 = (f32[160,1280]{1,0:T(8,128)S(1)}, f32[160,1280]{1,0:T(8,128)S(1)}, u32[]{:S(2)}, u32[]{:S(2)}) collective-permute-start(f32[160,1280]{1,0:T(8,128)S(1)} %pad_maximum_fusion.b0), channel_id=1, source_target_pairs={{0,2},{1,3},{2,0},{3,1},{4,6},{5,7},{6,4},{7,5},{8,10},{9,11},{10,... | collective-permute-start | bytes 2457608 | tf_op jit(solution)/shard_map/ppermute | solution.py:365
  100.1 39.0 %collective-permute-start.3 = (f32[160,1280]{1,0:T(8,128)S(1)}, f32[160,1280]{1,0:T(8,128)}, u32[]{:S(2)}, u32[]{:S(2)}) collective-permute-start(f32[160,1280]{1,0:T(8,128)S(1)} %pad_maximum_fusion.b0), channel_id=1, source_target_pairs={{0,1},{1,2},{2,3},{3,0},{4,5},{5,6},{6,7},{7,4},{8,9},{9,10},{10,1... | collective-permute-start | bytes 2457608 | tf_op jit(solution)/shard_map/ppermute | solution.py:365
  101.4 8.5 %copy-start.7 = (s32[8,64]{1,0:T(8,128)S(1)}, s32[8,64]{1,0:T(8,128)}, u32[]{:S(2)}) copy-start(s32[8,64]{1,0:T(8,128)} %param.10) | copy-start | bytes 6148
  102.7 77.7 %collective-permute-start.7 = (f32[160,640]{1,0:T(8,128)}, f32[160,640]{1,0:T(8,128)}, u32[]{:S(2)}, u32[]{:S(2)}) collective-permute-start(f32[160,640]{1,0:T(8,128)} %get-tuple-element.30), channel_id=1, source_target_pairs={{1,0},{3,2},{4,7},{6,5},{9,8},{11,10},{12,15},{14,13},{17,16},{19,... | collective-permute-start | bytes 1228808 | tf_op jit(solution)/shard_map/ppermute | solution.py:365
  117.4 21.6 %copy-start.3 = (f32[160,1280]{1,0:T(8,128)}, f32[160,1280]{1,0:T(8,128)S(1)}, u32[]{:S(2)}) copy-start(f32[160,1280]{1,0:T(8,128)S(1)} %collective-permute-done.1.b1) | copy-start | bytes 2457604
  119.8 0.9 copy-start.4
  159.5 92.7 %all-to-all-start.4 = ((f32[64,24,256]{2,1,0:T(8,128)}), f32[64,24,256]{2,1,0:T(8,128)}, u32[]{:S(2)}, u32[]{:S(2)}) async-start(f32[64,24,256]{2,1,0:T(8,128)} %update.1), calls=%async_computation.4 | async-start | bytes 3145728 | tf_op jit(solution)/shard_map/all_to_all | solution.py:403
  168.1 11.5 %copy-start.6 = (f32[160,640]{1,0:T(8,128)S(1)}, f32[160,640]{1,0:T(8,128)}, u32[]{:S(2)}) copy-start(f32[160,640]{1,0:T(8,128)} %get-tuple-element.31) | copy-start | bytes 1228804
  168.1 12.2 %copy-start.5 = (f32[160,640]{1,0:T(8,128)S(1)}, f32[160,640]{1,0:T(8,128)}, u32[]{:S(2)}) copy-start(f32[160,640]{1,0:T(8,128)} %get-tuple-element.29) | copy-start | bytes 1228804
  170.7 27.8 %collective-permute-start.4 = (f32[640,256]{1,0:T(8,128)S(1)}, f32[640,256]{1,0:T(8,128)}, u32[]{:S(2)}, u32[]{:S(2)}) collective-permute-start(f32[640,256]{1,0:T(8,128)S(1)} %bitcast.54), channel_id=1, source_target_pairs={{1,0},{3,2},{4,7},{6,5},{9,8},{11,10},{12,15},{14,13},{17,16},{19,... | collective-permute-start | bytes 1966088 | tf_op jit(solution)/shard_map/ppermute | solution.py:365
  175.9 22.6 %collective-permute-start.5 = (f32[640,256]{1,0:T(8,128)S(1)}, f32[640,256]{1,0:T(8,128)}, u32[]{:S(2)}, u32[]{:S(2)}) collective-permute-start(f32[640,256]{1,0:T(8,128)S(1)} %bitcast.53), channel_id=1, source_target_pairs={{0,2},{2,0},{5,7},{7,5},{8,10},{10,8},{13,15},{15,13},{16,18},{18,... | collective-permute-start | bytes 1966088 | tf_op jit(solution)/shard_map/ppermute | solution.py:365
  177.4 21.1 %collective-permute-start.6 = (f32[640,256]{1,0:T(8,128)S(1)}, f32[640,256]{1,0:T(8,128)}, u32[]{:S(2)}, u32[]{:S(2)}) collective-permute-start(f32[640,256]{1,0:T(8,128)S(1)} %bitcast.52), channel_id=1, source_target_pairs={{1,2},{3,0},{4,5},{6,7},{9,10},{11,8},{12,13},{14,15},{17,18},{19,... | collective-permute-start | bytes 1966088 | tf_op jit(solution)/shard_map/ppermute | solution.py:365
  179.6 3.2 %collective-permute-start.8 = (f32[160,640]{1,0:T(8,128)S(1)}, f32[160,640]{1,0:T(8,128)S(1)}, u32[]{:S(2)}, u32[]{:S(2)}) collective-permute-start(f32[160,640]{1,0:T(8,128)S(1)} %copy-done.6), channel_id=1, source_target_pairs={{0,2},{2,0},{5,7},{7,5},{8,10},{10,8},{13,15},{15,13},{16,18},{18,... | collective-permute-start | bytes 1228808 | tf_op jit(solution)/shard_map/ppermute | solution.py:365
  180.4 18.1 %collective-permute-start.9 = (f32[160,640]{1,0:T(8,128)S(1)}, f32[160,640]{1,0:T(8,128)}, u32[]{:S(2)}, u32[]{:S(2)}) collective-permute-start(f32[160,640]{1,0:T(8,128)S(1)} %copy-done.5), channel_id=1, source_target_pairs={{1,2},{3,0},{4,5},{6,7},{9,10},{11,8},{12,13},{14,15},{17,18},{19,... | collective-permute-start | bytes 1228808 | tf_op jit(solution)/shard_map/ppermute | solution.py:365
  182.8 15.7 %copy-start.9 = (f32[160,640]{1,0:T(8,128)}, f32[160,640]{1,0:T(8,128)S(1)}, u32[]{:S(2)}) copy-start(f32[160,640]{1,0:T(8,128)S(1)} %collective-permute-done.8.f2) | copy-start | bytes 1228804
  230.5 3.4 %collective-permute-start.11 = (f32[160,640]{1,0:T(8,128)S(1)}, f32[160,640]{1,0:T(8,128)S(1)}, u32[]{:S(2)}, u32[]{:S(2)}) collective-permute-start(f32[160,640]{1,0:T(8,128)S(1)} %get-tuple-element.24), channel_id=1, source_target_pairs={{0,2},{2,0},{5,7},{7,5},{8,10},{10,8},{13,15},{15,13},{16,18},{18,... | collective-permute-start | bytes 1228808 | tf_op jit(solution)/shard_map/ppermute | solution.py:365
  231.2 15.3 %collective-permute-start.12 = (f32[160,640]{1,0:T(8,128)S(1)}, f32[160,640]{1,0:T(8,128)S(1)}, u32[]{:S(2)}, u32[]{:S(2)}) collective-permute-start(f32[160,640]{1,0:T(8,128)S(1)} %get-tuple-element.23), channel_id=1, source_target_pairs={{0,3},{2,1},{5,4},{7,6},{8,11},{10,9},{13,12},{15,14},{16,19},{18,... | collective-permute-start | bytes 1228808 | tf_op jit(solution)/shard_map/ppermute | solution.py:365
  232.5 16.9 %collective-permute-start.10 = (f32[160,640]{1,0:T(8,128)S(1)}, f32[160,640]{1,0:T(8,128)S(1)}, u32[]{:S(2)}, u32[]{:S(2)}) collective-permute-start(f32[160,640]{1,0:T(8,128)S(1)} %get-tuple-element.22), channel_id=1, source_target_pairs={{0,1},{2,3},{5,6},{7,4},{8,9},{10,11},{13,14},{15,12},{16,17},{18,... | collective-permute-start | bytes 1228808 | tf_op jit(solution)/shard_map/ppermute | solution.py:365

commit v5 on v4

--- a/solution.py
+++ b/solution.py
@@ -9,6 +9,7 @@
 NS_ITERS = 4
 SLOTS = 2
 BLOCK = 256
+FIRST = 64
 VMEM = 63 << 20
 PARTS = (80,)
 NX, NZ, NC = 4, 8, 2
@@ -173,7 +174,7 @@
 
 
 def refresh_kernel(
-    at, g0, g1, g2, g3, f0, f1, f2, f3, b_hi, b_lo, o_ref,
+    at, g0, g1, g2, g3, f0, f1, f2, f3, b_hi, b_lo, o0, o1, o2, o3,
     g_in, f_in, gbuf, xbuf, abuf, stack, x_ref, a_ref, g_sem, f_sem, b_sem,
 ):
     d = x_ref.shape[0]
@@ -255,7 +256,8 @@
         return carry
 
     lax.fori_loop(0, NS_ITERS, step, 0)
-    o_ref[...] = jnp.where(at[2] > 0, x_ref[...], 0.0)
+    for start, o_ref in zip(row_starts(at[0], rows, 4), (o0, o1, o2, o3)):
+        o_ref[...] = jnp.where(at[2] > 0, x_ref[pl.ds(start, rows), :], 0.0)
 
 
 def refresh(scalars, pieces, factors, b_hi, b_lo):
@@ -264,9 +266,9 @@
     hbm = pl.BlockSpec(memory_space=pltpu.HBM)
     return pl.pallas_call(
         refresh_kernel,
-        out_shape=jax.ShapeDtypeStruct((d, d), jnp.float32),
+        out_shape=[jax.ShapeDtypeStruct(factors[0].shape, jnp.float32)] * 4,
         in_specs=[pl.BlockSpec(memory_space=pltpu.SMEM)] + [hbm] * 10,
-        out_specs=pl.BlockSpec(memory_space=pltpu.VMEM),
+        out_specs=[pl.BlockSpec(memory_space=pltpu.VMEM)] * 4,
         scratch_shapes=[
             pltpu.VMEM((4, d, w), jnp.float32),
             pltpu.VMEM((d, d), jnp.float32),
@@ -296,7 +298,6 @@
     x, core = d // (NZ * NC), d % NC
     count, rows, cols = local.shape
     groups = NX * NZ * NC
-    along_x = [[line(a, b, c) for a in range(NX)] for b in range(NZ) for c in range(NC)]
     along_z = [[line(a, b, c) for b in range(NZ)] for a in range(NX) for c in range(NC)]
     across = [[line(a, b, c) for a in range(NX) for c in range(NC)] for b in range(NZ)]
     swap = [
@@ -314,27 +315,51 @@
     wanted = lax.dynamic_index_in_dim(matrix_of.reshape(NX, NZ, NC, SLOTS), x, 0, keepdims=False)
     wanted = lax.dynamic_index_in_dim(wanted, core, 1, keepdims=False).reshape(-1)
 
-    paired = local.reshape(NX, NC, NZ, rows // NZ, cols)
+    def along(shift):
+        return [
+            (line(a, b, c), line((a + shift) % NX, b, c))
+            for a in range(NX) for b in range(NZ) for c in range(NC)
+        ]
+
+    part = rows // NZ
+    rest = part - FIRST
+    paired = local.reshape(NX, NC, NZ, part, cols)
     others = lax.dynamic_index_in_dim(paired, 1 - core, 1, keepdims=False)
     kept = lax.dynamic_index_in_dim(paired, core, 1, keepdims=False)
-    outs = []
-    lead = 0
-    for size in PARTS:
-        came = lax.ppermute(
-            others[:, :, lead:lead + size].astype(jnp.float32).reshape(NX, NZ * size, cols), "dp", swap
-        )
-        chip = kept[:, :, lead:lead + size].astype(jnp.float32).reshape(NX, NZ * size, cols) + came
-        lead += size
-        outs.append(exchange(chip, along_x))
-    incoming = []
-    for part, size in enumerate(PARTS):
-        over_x = jnp.sum(outs[part], axis=0)
-        over_z = jnp.sum(exchange(over_x.reshape(NZ, size, cols), along_z), axis=0)
-        mean = over_z * (1.0 / groups)
-        everything = exchange(jnp.broadcast_to(mean[None], (count, size, cols)), across)
-        outgoing = jnp.take(everything, wanted, axis=0, mode="clip")
-        incoming.append(exchange(outgoing.reshape(NZ, SLOTS, size, cols), along_z))
-    return incoming
+    came = lax.ppermute(others.astype(jnp.float32), "dp", swap)
+    chip = kept.astype(jnp.float32) + came
+
+    def towards(shift):
+        near = lax.dynamic_index_in_dim(chip, (x + shift) % NX, 0, keepdims=False)
+        return near[:, :FIRST].reshape(NZ * FIRST, cols)
+
+    cut = NZ * FIRST // 2
+    far = towards(2)
+    far_up = lax.ppermute(far[:cut], "dp", along(1))
+    far_down = lax.ppermute(far[cut:], "dp", along(-1))
+    late = jnp.transpose(chip[:, :, FIRST:], (1, 0, 2, 3)).reshape(NZ, NX * rest, cols)
+    late = exchange(late, along_z)
+    up, down = towards(1), towards(3)
+    up = jnp.concatenate([up[:cut] + far_up, up[cut:]], axis=0)
+    down = jnp.concatenate([down[:cut], down[cut:] + far_down], axis=0)
+    from_up = lax.ppermute(up, "dp", along(1))
+    from_down = lax.ppermute(down, "dp", along(-1))
+    over_x = towards(0) + from_up + from_down
+    over_z = jnp.sum(exchange(over_x.reshape(NZ, FIRST, cols), along_z), axis=0)
+    mean = over_z * (1.0 / groups)
+    late = jnp.sum(late, axis=0)
+    late = (late + lax.ppermute(late, "dp", along(1))) + (
+        lax.ppermute(late, "dp", along(-1)) + lax.ppermute(late, "dp", along(2))
+    )
+    late = (late * (1.0 / groups)).reshape(NX, rest, cols)
+    other = lax.ppermute(late, "dp", swap)
+    late = jnp.stack(
+        [jnp.where(core == 0, late, other), jnp.where(core == 0, other, late)], axis=1
+    ).reshape(count, rest, cols)
+    everything = exchange(jnp.broadcast_to(mean[None], (count, FIRST, cols)), across)
+    everything = jnp.concatenate([everything, late], axis=1)
+    outgoing = jnp.take(everything, wanted, axis=0, mode="clip")
+    return [exchange(outgoing.reshape(NZ, SLOTS, part, cols), along_z)]
 
 
 def body(partials, owner, rowblock, factor, basis, moment1, moment2, master):
@@ -401,7 +426,7 @@
     chosen = jnp.sum(jnp.where(mine[:, :, None], rowblock[None], 0), axis=1)
     sent = update(chosen, incoming, halves, moment1[0], moment2[0], master[0])
     received = lax.all_to_all(sent, "dp", split_axis=0, concat_axis=0, tiled=True)
-    refreshed = refresh(scalars, pieces, factors, halves[0], halves[1])
+    own, after, across, before = refresh(scalars, pieces, factors, halves[0], halves[1])
 
     landed = jnp.take(received, owner, axis=0, mode="clip")
     block_rows = rows * cols // groups
@@ -409,13 +434,9 @@
         (slot == 0)[:, None, None], landed[:, :block_rows], landed[:, block_rows:2 * block_rows]
     )[:, None]
 
-    def row_block(at):
-        return lax.dynamic_slice_in_dim(refreshed, ((at + cols) % cols) * rows, rows, 0)
-
-    own = row_block(y)
-    from_left = move(row_block(y + 1), 1, 0)
-    from_far = move(row_block(y + 2), 2, 0)
-    from_right = move(row_block(y - 1), -1, 0)
+    from_left = move(after, 1, 0)
+    from_far = move(across, 2, 0)
+    from_right = move(before, -1, 0)
     near = jnp.where(even, own, from_left)
     far = jnp.where(even, from_far, from_right)
     near_first = jnp.where(even, own_slot, left_slot) == 0

time: 256 us -> 248 us (0.969)
  blocking collectives: 34.2 us -> 0 us
  starting transfers between devices: 53.5 us -> 67.8 us
  waiting for transfers between devices: 91.9 us -> 101 us
    all_to_all x1 -> x0, blocking collectives: 34.2 us -> none  [exchange(): return lax.all_to_all(v, 'dp', 0, 0, axis_index_groups=lines, tiled=True)]
    ppermute x1 -> x9, waiting for transfers between devices: 4.54 us -> 23.5 us  [the longest x1 9.53 us: owned_gradients(): from_down = lax.ppermute(down, 'dp', along(-1))]
    all_to_all x3 -> x4, waiting for transfers between devices: 28.5 us -> 19.8 us  [exchange(): return lax.all_to_all(v, 'dp', 0, 0, axis_index_groups=lines, tiled=True)]
    ppermute x1 -> x9, starting transfers between devices: 3.29 us -> 11.2 us  [the longest x1 3.49 us: owned_gradients(): from_down = lax.ppermute(down, 'dp', along(-1))]
    all_to_all x3 -> x4, starting transfers between devices: 17.7 us -> 24.5 us  [exchange(): return lax.all_to_all(v, 'dp', 0, 0, axis_index_groups=lines, tiled=True)]
    dynamic_slice x2 -> x0, local copies, waits for them, and re-layouts: 3.23 us -> none  [the longest x1 1.89 us: owned_gradients(): kept = lax.dynamic_index_in_dim(paired, core, 1, keepdims=False)]
    add x1 -> x4, other arithmetic: 0.41 us -> 3.41 us  [the longest x1 2.46 us: owned_gradients(): chip = kept.astype(jnp.float32) + came]
  transfers between devices with their start and end apart: 17 -> 26, of which waited for: 9 -> 13; matrix products, arithmetic and copies ran while one was open for 5% -> 5% of each run, Pallas kernels for 20% -> 21%
where the time goes in v5:
time: 248 us; the launch traced here: 247 us
  waiting for transfers between devices  101 us (41%)
  starting transfers between devices  67.8 us (27%)
  Pallas kernels  51.2 us (21%)
  local copies, waits for them, and re-layouts  13.1 us (5%)
  other arithmetic  11.1 us (4%)
    ppermute x12, waiting for transfers between devices, move(): return lax.ppermute(v, ('dp', 'mp'), ring(shift, parity))  58 us
    pallas_call x1, Pallas kernels, refresh(): pl.pallas_call(refresh_kernel, out_shape=[jax.ShapeDtypeStruct(factors[0]...  30.7 us
    all_to_all x4, starting transfers between devices, exchange(): return lax.all_to_all(v, 'dp', 0, 0, axis_index_groups=lines, tiled=True)  24.5 us
    ppermute x12, starting transfers between devices, move(): return lax.ppermute(v, ('dp', 'mp'), ring(shift, parity))  23.4 us
    all_to_all x4, waiting for transfers between devices, exchange(): return lax.all_to_all(v, 'dp', 0, 0, axis_index_groups=lines, tiled=True)  19.8 us
    pallas_call x1, Pallas kernels, update(): pl.pallas_call(update_kernel, out_shape=jax.ShapeDtypeStruct((groups, pad...  14.1 us
    ppermute x1, waiting for transfers between devices, owned_gradients(): from_down = lax.ppermute(down, 'dp', along(-1))  9.53 us
    all_to_all x1, starting transfers between devices, body(): lax.all_to_all(sent, 'dp', split_axis=0, concat_axis=0, tiled=True)  8.62 us
  transfers between devices with their start and end apart: 26, of which 13 were waited for; matrix products, arithmetic and copies ran while one was open for 5% of the time, Pallas kernels for 21%

profile of v5, /device:TPU:1, one launch (start us, length us, event | category | flops | bytes accessed | tf_op | source)
XLA Modules:
  0.0 246.7 jit_solution(4842101319125391974)
XLA Ops:
  0.6 1.6 bitcast_convert_fusion
  2.3 3.3 %collective-permute-start = (f32[4,8,80,256]{3,2,1,0:T(8,128)S(1)}, f32[4,8,80,256]{3,2,1,0:T(8,128)}, u32[]{:S(2)}, u32[]{:S(2)}) collective-permute-start(f32[4,8,80,256]{3,2,1,0:T(8,128)S(1)} %bitcast_convert_fusion), channel_id=1, source_target_pairs={{0,4},{4,0},{8,12},{12,8},{16,20},{20,16},{24,28},{28,24},{32,36},... | collective-permute-start | bytes 7864328 | tf_op jit(solution)/shard_map/ppermute | solution.py:329
  5.6 4.7 %collective-permute-done = f32[4,8,80,256]{3,2,1,0:T(8,128)} collective-permute-done((f32[4,8,80,256]{3,2,1,0:T(8,128)S(1)}, f32[4,8,80,256]{3,2,1,0:T(8,128)}, u32[]{:S(2)}, u32[]{:S(2)}) %collective-permute-start) | collective-permute-done | bytes 2621472 | tf_op jit(solution)/shard_map/ppermute | solution.py:329
  10.2 2.5 convert_add_fusion
  12.8 0.8 copy.37
  13.6 6.5 %all-to-all-start.2 = ((f32[8,64,256]{2,1,0:T(8,128)}), f32[8,64,256]{2,1,0:T(8,128)S(1)}, u32[]{:S(2)}, u32[]{:S(2)}) async-start(f32[8,64,256]{2,1,0:T(8,128)} %bitcast.82), calls=%async_computation.2 | async-start | bytes 1048576 | tf_op jit(solution)/shard_map/all_to_all | solution.py:309
  20.1 0.2 dynamic-slice_bitcast_fusion.3
  20.3 2.6 %collective-permute-start.3 = (f32[256,256]{1,0:T(8,128)S(1)}, f32[256,256]{1,0:T(8,128)S(1)}, u32[]{:S(2)}, u32[]{:S(2)}) collective-permute-start(f32[256,256]{1,0:T(8,128)S(1)} %bitcast.96), channel_id=1, source_target_pairs={{0,192},{4,196},{8,200},{12,204},{16,208},{20,212},{24,216},{28,22... | collective-permute-start | bytes 786440 | tf_op jit(solution)/shard_map/ppermute | solution.py:339
  23.1 4.8 %collective-permute-done.3 = f32[256,256]{1,0:T(8,128)S(1)} collective-permute-done((f32[256,256]{1,0:T(8,128)S(1)}, f32[256,256]{1,0:T(8,128)S(1)}, u32[]{:S(2)}, u32[]{:S(2)}) %collective-permute-start.3) | collective-permute-done | bytes 262176 | tf_op jit(solution)/shard_map/ppermute | solution.py:339
  28.0 3.5 %collective-permute-start.4 = (f32[512,256]{1,0:T(8,128)S(1)}, f32[512,256]{1,0:T(8,128)S(1)}, u32[]{:S(2)}, u32[]{:S(2)}) collective-permute-start(f32[512,256]{1,0:T(8,128)S(1)} %pad_maximum_fusion.3), channel_id=1, source_target_pairs={{0,192},{4,196},{8,200},{12,204},{16,208},{20,212},{24,216},{28,22... | collective-permute-start | bytes 1572872 | tf_op jit(solution)/shard_map/ppermute | solution.py:346
  31.7 9.5 %collective-permute-done.4 = f32[512,256]{1,0:T(8,128)S(1)} collective-permute-done((f32[512,256]{1,0:T(8,128)S(1)}, f32[512,256]{1,0:T(8,128)S(1)}, u32[]{:S(2)}, u32[]{:S(2)}) %collective-permute-start.4) | collective-permute-done | bytes 524320 | tf_op jit(solution)/shard_map/ppermute | solution.py:346
  41.2 3.3 %collective-permute-done.2 = f32[512,256]{1,0:T(8,128)S(1)} collective-permute-done((f32[512,256]{1,0:T(8,128)S(1)}, f32[512,256]{1,0:T(8,128)S(1)}, u32[]{:S(2)}, u32[]{:S(2)}) %collective-permute-start.2) | collective-permute-done | bytes 524320 | tf_op jit(solution)/shard_map/ppermute | solution.py:345
  44.5 0.9 fusion
  45.4 6.1 %all-to-all-start = ((f32[8,64,256]{2,1,0:T(8,128)}), f32[8,64,256]{2,1,0:T(8,128)S(1)}, u32[]{:S(2)}, u32[]{:S(2)}) async-start(f32[8,64,256]{2,1,0:T(8,128)} %bitcast.14), calls=%async_computation | async-start | bytes 1048576 | tf_op jit(solution)/shard_map/all_to_all | solution.py:309
  51.5 0.2 convert_reduce_fusion
  51.8 0.1 fusion.3
  52.2 0.1 copy.39
  52.4 0.2 collective-permute-start.6
  52.6 0.7 collective-permute-start.7
  53.4 0.6 collective-permute-start.5
  54.0 11.8 %all-to-all-done = f32[8,64,256]{2,1,0:T(8,128)S(1)} async-done(((f32[8,64,256]{2,1,0:T(8,128)}), f32[8,64,256]{2,1,0:T(8,128)S(1)}, u32[]{:S(2)}, u32[]{:S(2)}) %all-to-all-start) | async-done | bytes 524320 | tf_op jit(solution)/shard_map/all_to_all | solution.py:309
  65.9 0.8 broadcast_in_dim.79
  66.7 7.5 %all-to-all-start.1 = ((f32[8,64,256]{2,1,0:T(8,128)}), f32[8,64,256]{2,1,0:T(8,128)S(1)}, u32[]{:S(2)}, u32[]{:S(2)}) async-start(f32[8,64,256]{2,1,0:T(8,128)} %broadcast_in_dim.79), calls=%async_computation.1 | async-start | bytes 1048576 | tf_op jit(solution)/shard_map/all_to_all | solution.py:309
  74.3 0.2 collective-permute-start.8
  74.5 1.1 collective-permute-done.8
  75.7 8.0 %all-to-all-done.1 = f32[8,64,256]{2,1,0:T(8,128)S(1)} async-done(((f32[8,64,256]{2,1,0:T(8,128)}), f32[8,64,256]{2,1,0:T(8,128)S(1)}, u32[]{:S(2)}, u32[]{:S(2)}) %all-to-all-start.1) | async-done | bytes 524320 | tf_op jit(solution)/shard_map/all_to_all | solution.py:309
  83.7 1.7 gather_fusion
  85.4 4.4 %all-to-all-start.3 = ((f32[8,2,80,256]{3,2,1,0:T(8,128)}), f32[8,2,80,256]{3,2,1,0:T(8,128)}, u32[]{:S(2)}, u32[]{:S(2)}) async-start(f32[8,2,80,256]{3,2,1,0:T(8,128)} %bitcast.22), calls=%async_computation.3 | async-start | bytes 2621440 | tf_op jit(solution)/shard_map/all_to_all | solution.py:309
  89.8 0.6 fusion.5
  90.6 2.8 %collective-permute-start.9 = (f32[160,1280]{1,0:T(8,128)S(1)}, f32[160,1280]{1,0:T(8,128)S(1)}, u32[]{:S(2)}, u32[]{:S(2)}) collective-permute-start(f32[160,1280]{1,0:T(8,128)S(1)} %pad_maximum_fusion.b0), channel_id=1, source_target_pairs={{0,3},{1,0},{2,1},{3,2},{4,7},{5,4},{6,5},{7,6},{8,11},{9,8},{10,9... | collective-permute-start | bytes 2457608 | tf_op jit(solution)/shard_map/ppermute | solution.py:390
  93.4 0.4 collective-permute-start.10
  93.8 0.7 collective-permute-start.11
  94.5 0.6 fusion.4
  95.1 1.2 select_bitcast_fusion.2
  96.4 4.7 %collective-permute-start.15 = (f32[160,640]{1,0:T(8,128)}, f32[160,640]{1,0:T(8,128)}, u32[]{:S(2)}, u32[]{:S(2)}) collective-permute-start(f32[160,640]{1,0:T(8,128)} %get-tuple-element.39), channel_id=1, source_target_pairs={{1,0},{3,2},{4,7},{6,5},{9,8},{11,10},{12,15},{14,13},{17,16},{19,... | collective-permute-start | bytes 1228808 | tf_op jit(solution)/shard_map/ppermute | solution.py:390
  101.0 0.6 fusion.9
  102.9 0.6 pad_add_fusion.at
  103.5 0.6 select_reduce_fusion.1.chosen
  104.1 7.0 %collective-permute-done.9.b1 = f32[160,1280]{1,0:T(8,128)S(1)} collective-permute-done((f32[160,1280]{1,0:T(8,128)S(1)}, f32[160,1280]{1,0:T(8,128)S(1)}, u32[]{:S(2)}, u32[]{:S(2)}) %collective-permute-start.9) | collective-permute-done | bytes 819232 | tf_op jit(solution)/shard_map/ppermute | solution.py:390
  111.1 2.4 collective-permute-done.10.b2
  113.5 0.9 copy-done.4
  114.5 18.3 %collective-permute-done.11.b3 = f32[160,1280]{1,0:T(8,128)} collective-permute-done((f32[160,1280]{1,0:T(8,128)S(1)}, f32[160,1280]{1,0:T(8,128)}, u32[]{:S(2)}, u32[]{:S(2)}) %collective-permute-start.11) | collective-permute-done | bytes 819232 | tf_op jit(solution)/shard_map/ppermute | solution.py:390
  132.8 6.4 %prepare.1 = (bf16[2,640,640]{2,1,0:T(8,128)(2,1)}, bf16[2,640,640]{2,1,0:T(8,128)(2,1)}, bf16[2,640,640]{2,1,0:T(8,128)(2,1)}, bf16[2,640,640]{2,1,0:T(8,128)(2,1)}) custom-call(s32[3]{0:T(128)} %pad_add_fusion.at, f32[160,1280]{1,0:T(8,128)} %copy-done, f32[160,1280]{1,0:T(8,128)} %copy-done.3, f32[160,1280]{1,0:T(8,128)} %copy-done.4, ...), custom_call_target="tpu_custom_call" | custom-call | flops 3276800 | bytes 9830400 | tf_op jit(solution)/shard_map/prepare/pallas_call | solution.py:83
  139.2 14.1 %update.1 = f32[64,24,256]{2,1,0:T(8,128)} custom-call(s32[2,64]{1,0:T(2,128)} %select_reduce_fusion.1.chosen, f32[8,2,80,256]{3,2,1,0:T(8,128)} %all-to-all-done.3.refs_0_, bf16[2,640,640]{2,1,0:T(8,128)(2,1)} %get-tuple-element.10.refs_1_.b_hi, bf16[2,640,640]{2,1,0:T(8,128)(2,1)} %get-tuple-element.11.refs_2_.b_lo, ...), custom_call_target="tpu_custom_call" | custom-call | flops 2516582400 | bytes 5898240 | tf_op jit(solution)/shard_map/update/pallas_call | solution.py:152
  153.3 8.6 %all-to-all-start.4 = ((f32[64,24,256]{2,1,0:T(8,128)}), f32[64,24,256]{2,1,0:T(8,128)}, u32[]{:S(2)}, u32[]{:S(2)}) async-start(f32[64,24,256]{2,1,0:T(8,128)} %update.1), calls=%async_computation.4 | async-start | bytes 3145728 | tf_op jit(solution)/shard_map/all_to_all | solution.py:428
  161.9 2.5 %slice_select_fusion = (f32[8,1,80,256]{3,2,1,0:T(8,128)S(1)}, f32[8,1,80,256]{3,2,1,0:T(8,128)S(1)}, f32[8,1,80,256]{3,2,1,0:T(8,128)}, f32[8,1,80,256]{3,2,1,0:T(8,128)S(1)}) fusion(f32[8,2,80,256]{3,2,1,0:T(8,128)} %all-to-all-done.3.refs_0_, pred[]{:T(512)S(6)} %eq.129, pred[]{:T(512)S(6)} %eq.128, pred[]{:T(512)S(6)} %eq.124, pred[]{:T(512)S(6)} %eq.127), kind=kLoop, calls=%fused_computation.11 | loop fusion | flops 655360 | bytes 3932164 | tf_op jit(solution)/shard_map/jit(_where)/select_n | solution.py:419
  164.4 4.4 %collective-permute-start.12 = (f32[640,256]{1,0:T(8,128)S(1)}, f32[640,256]{1,0:T(8,128)S(1)}, u32[]{:S(2)}, u32[]{:S(2)}) collective-permute-start(f32[640,256]{1,0:T(8,128)S(1)} %bitcast.91), channel_id=1, source_target_pairs={{1,0},{3,2},{4,7},{6,5},{9,8},{11,10},{12,15},{14,13},{17,16},{19,... | collective-permute-start | bytes 1966088 | tf_op jit(solution)/shard_map/ppermute | solution.py:390
  168.8 0.7 collective-permute-start.13
  169.5 3.1 %collective-permute-start.14 = (f32[640,256]{1,0:T(8,128)S(1)}, f32[640,256]{1,0:T(8,128)S(1)}, u32[]{:S(2)}, u32[]{:S(2)}) collective-permute-start(f32[640,256]{1,0:T(8,128)S(1)} %bitcast.89), channel_id=1, source_target_pairs={{1,2},{3,0},{4,5},{6,7},{9,10},{11,8},{12,13},{14,15},{17,18},{19,... | collective-permute-start | bytes 1966088 | tf_op jit(solution)/shard_map/ppermute | solution.py:390
  172.6 0.7 collective-permute-start.16
  173.3 2.7 %collective-permute-start.17 = (f32[160,640]{1,0:T(8,128)S(1)}, f32[160,640]{1,0:T(8,128)S(1)}, u32[]{:S(2)}, u32[]{:S(2)}) collective-permute-start(f32[160,640]{1,0:T(8,128)S(1)} %copy-done.5), channel_id=1, source_target_pairs={{1,2},{3,0},{4,5},{6,7},{9,10},{11,8},{12,13},{14,15},{17,18},{19,... | collective-permute-start | bytes 1228808 | tf_op jit(solution)/shard_map/ppermute | solution.py:390
  176.1 16.2 %collective-permute-done.17.f3 = f32[160,640]{1,0:T(8,128)S(1)} collective-permute-done((f32[160,640]{1,0:T(8,128)S(1)}, f32[160,640]{1,0:T(8,128)S(1)}, u32[]{:S(2)}, u32[]{:S(2)}) %collective-permute-start.17) | collective-permute-done | bytes 409632 | tf_op jit(solution)/shard_map/ppermute | solution.py:390
  192.3 0.9 copy-done.10
  193.1 0.9 copy-done.11
  194.1 30.7 %refresh.1 = (f32[160,640]{1,0:T(8,128)}, f32[160,640]{1,0:T(8,128)}, f32[160,640]{1,0:T(8,128)}, f32[160,640]{1,0:T(8,128)}) custom-call(s32[3]{0:T(128)} %pad_add_fusion.at, f32[640,256]{1,0:T(8,128)} %bitcast.88, f32[640,256]{1,0:T(8,128)} %copy-done.9, f32[640,256]{1,0:T(8,128)} %copy-done.10, f32[640,256]{1,0:T(8,128)} %copy-done.11, ...), custom_call_target="tpu_custom_call" | custom-call | flops 15728640000 | bytes 6553600 | tf_op jit(solution)/shard_map/refresh/pallas_call | solution.py:267
  224.8 1.3 collective-permute-start.18
  226.1 0.7 collective-permute-start.19
  226.8 1.3 collective-permute-start.20
  228.1 7.2 %collective-permute-done.18 = f32[160,640]{1,0:T(8,128)S(1)} collective-permute-done((f32[160,640]{1,0:T(8,128)}, f32[160,640]{1,0:T(8,128)S(1)}, u32[]{:S(2)}, u32[]{:S(2)}) %collective-permute-start.18) | collective-permute-done | bytes 409632 | tf_op jit(solution)/shard_map/ppermute | solution.py:390
  235.3 6.9 %collective-permute-done.20 = f32[160,640]{1,0:T(8,128)S(1)} collective-permute-done((f32[160,640]{1,0:T(8,128)}, f32[160,640]{1,0:T(8,128)S(1)}, u32[]{:S(2)}, u32[]{:S(2)}) %collective-permute-start.20) | collective-permute-done | bytes 409632 | tf_op jit(solution)/shard_map/ppermute | solution.py:390
  242.2 0.1 select_bitcast_fusion.1
  242.4 1.5 copy.45
  244.0 2.0 gather_fusion.1
  246.0 0.7 copy.44
  (69 shorter events, 1.4 us)
Async XLA Ops:
  2.3 8.0 %collective-permute-start = (f32[4,8,80,256]{3,2,1,0:T(8,128)S(1)}, f32[4,8,80,256]{3,2,1,0:T(8,128)}, u32[]{:S(2)}, u32[]{:S(2)}) collective-permute-start(f32[4,8,80,256]{3,2,1,0:T(8,128)S(1)} %bitcast_convert_fusion), channel_id=1, source_target_pairs={{0,4},{4,0},{8,12},{12,8},{16,20},{20,16},{24,28},{28,24},{32,36},... | collective-permute-start | bytes 7864328 | tf_op jit(solution)/shard_map/ppermute | solution.py:329
  13.6 31.8 %all-to-all-start.2 = ((f32[8,64,256]{2,1,0:T(8,128)}), f32[8,64,256]{2,1,0:T(8,128)S(1)}, u32[]{:S(2)}, u32[]{:S(2)}) async-start(f32[8,64,256]{2,1,0:T(8,128)} %bitcast.82), calls=%async_computation.2 | async-start | bytes 1048576 | tf_op jit(solution)/shard_map/all_to_all | solution.py:309
  20.3 7.6 %collective-permute-start.3 = (f32[256,256]{1,0:T(8,128)S(1)}, f32[256,256]{1,0:T(8,128)S(1)}, u32[]{:S(2)}, u32[]{:S(2)}) collective-permute-start(f32[256,256]{1,0:T(8,128)S(1)} %bitcast.96), channel_id=1, source_target_pairs={{0,192},{4,196},{8,200},{12,204},{16,208},{20,212},{24,216},{28,22... | collective-permute-start | bytes 786440 | tf_op jit(solution)/shard_map/ppermute | solution.py:339
  22.9 8.5 %collective-permute-start.1 = (f32[256,256]{1,0:T(8,128)S(1)}, f32[256,256]{1,0:T(8,128)S(1)}, u32[]{:S(2)}, u32[]{:S(2)}) collective-permute-start(f32[256,256]{1,0:T(8,128)S(1)} %bitcast.95), channel_id=1, source_target_pairs={{0,64},{4,68},{8,72},{12,76},{16,80},{20,84},{24,88},{28,92},{32,9... | collective-permute-start | bytes 786440 | tf_op jit(solution)/shard_map/ppermute | solution.py:338
  28.0 13.3 %collective-permute-start.4 = (f32[512,256]{1,0:T(8,128)S(1)}, f32[512,256]{1,0:T(8,128)S(1)}, u32[]{:S(2)}, u32[]{:S(2)}) collective-permute-start(f32[512,256]{1,0:T(8,128)S(1)} %pad_maximum_fusion.3), channel_id=1, source_target_pairs={{0,192},{4,196},{8,200},{12,204},{16,208},{20,212},{24,216},{28,22... | collective-permute-start | bytes 1572872 | tf_op jit(solution)/shard_map/ppermute | solution.py:346
  31.5 13.0 %collective-permute-start.2 = (f32[512,256]{1,0:T(8,128)S(1)}, f32[512,256]{1,0:T(8,128)S(1)}, u32[]{:S(2)}, u32[]{:S(2)}) collective-permute-start(f32[512,256]{1,0:T(8,128)S(1)} %pad_maximum_fusion.2), channel_id=1, source_target_pairs={{0,64},{4,68},{8,72},{12,76},{16,80},{20,84},{24,88},{28,92},{32,9... | collective-permute-start | bytes 1572872 | tf_op jit(solution)/shard_map/ppermute | solution.py:345
  31.7 19.8 %copy-start.8 = (s32[8]{0:T(128)S(1)}, s32[8]{0:T(128)}, u32[]{:S(2)}) copy-start(s32[8]{0:T(128)} %param.9) | copy-start | bytes 100
  45.4 20.4 %all-to-all-start = ((f32[8,64,256]{2,1,0:T(8,128)}), f32[8,64,256]{2,1,0:T(8,128)S(1)}, u32[]{:S(2)}, u32[]{:S(2)}) async-start(f32[8,64,256]{2,1,0:T(8,128)} %bitcast.14), calls=%async_computation | async-start | bytes 1048576 | tf_op jit(solution)/shard_map/all_to_all | solution.py:309
  52.4 21.8 %collective-permute-start.6 = (f32[64,256]{1,0:T(8,128)S(1)}, f32[64,256]{1,0:T(8,128)S(1)}, u32[]{:S(2)}, u32[]{:S(2)}) collective-permute-start(f32[64,256]{1,0:T(8,128)S(1)} %reduce_sum.48), channel_id=1, source_target_pairs={{0,192},{4,196},{8,200},{12,204},{16,208},{20,212},{24,216},{28,22... | collective-permute-start | bytes 196616 | tf_op jit(solution)/shard_map/ppermute | solution.py:352
  52.6 21.6 %collective-permute-start.7 = (f32[64,256]{1,0:T(8,128)S(1)}, f32[64,256]{1,0:T(8,128)S(1)}, u32[]{:S(2)}, u32[]{:S(2)}) collective-permute-start(f32[64,256]{1,0:T(8,128)S(1)} %reduce_sum.48), channel_id=1, source_target_pairs={{0,128},{4,132},{8,136},{12,140},{16,144},{20,148},{24,152},{28,15... | collective-permute-start | bytes 196616 | tf_op jit(solution)/shard_map/ppermute | solution.py:352
  53.4 20.9 %collective-permute-start.5 = (f32[64,256]{1,0:T(8,128)S(1)}, f32[64,256]{1,0:T(8,128)S(1)}, u32[]{:S(2)}, u32[]{:S(2)}) collective-permute-start(f32[64,256]{1,0:T(8,128)S(1)} %reduce_sum.48), channel_id=1, source_target_pairs={{0,64},{4,68},{8,72},{12,76},{16,80},{20,84},{24,88},{28,92},{32,9... | collective-permute-start | bytes 196616 | tf_op jit(solution)/shard_map/ppermute | solution.py:351
  66.7 16.9 %all-to-all-start.1 = ((f32[8,64,256]{2,1,0:T(8,128)}), f32[8,64,256]{2,1,0:T(8,128)S(1)}, u32[]{:S(2)}, u32[]{:S(2)}) async-start(f32[8,64,256]{2,1,0:T(8,128)} %broadcast_in_dim.79), calls=%async_computation.1 | async-start | bytes 1048576 | tf_op jit(solution)/shard_map/all_to_all | solution.py:309
  74.3 1.3 collective-permute-start.8
  85.4 4.4 %copy-start.1 = (f32[1,160,2,640]{3,2,1,0:T(2,128)S(1)}, f32[1,160,2,640]{3,2,1,0:T(2,128)}, u32[]{:S(2)}) copy-start(f32[1,160,2,640]{3,2,1,0:T(2,128)} %param.12) | copy-start | bytes 2457604
  85.4 53.8 %all-to-all-start.3 = ((f32[8,2,80,256]{3,2,1,0:T(8,128)}), f32[8,2,80,256]{3,2,1,0:T(8,128)}, u32[]{:S(2)}, u32[]{:S(2)}) async-start(f32[8,2,80,256]{3,2,1,0:T(8,128)} %bitcast.22), calls=%async_computation.3 | async-start | bytes 2621440 | tf_op jit(solution)/shard_map/all_to_all | solution.py:309
  90.5 4.0 %copy-start.2 = (f32[1,160,2,640]{3,2,1,0:T(2,128)S(1)}, f32[1,160,2,640]{3,2,1,0:T(2,128)}, u32[]{:S(2)}) copy-start(f32[1,160,2,640]{3,2,1,0:T(2,128)} %param.11) | copy-start | bytes 2457604
  90.6 5.8 %copy-start = (f32[160,1280]{1,0:T(8,128)}, f32[160,1280]{1,0:T(8,128)S(1)}, u32[]{:S(2)}) copy-start(f32[160,1280]{1,0:T(8,128)S(1)} %pad_maximum_fusion.b0) | copy-start | bytes 2457604
  90.6 20.5 %collective-permute-start.9 = (f32[160,1280]{1,0:T(8,128)S(1)}, f32[160,1280]{1,0:T(8,128)S(1)}, u32[]{:S(2)}, u32[]{:S(2)}) collective-permute-start(f32[160,1280]{1,0:T(8,128)S(1)} %pad_maximum_fusion.b0), channel_id=1, source_target_pairs={{0,3},{1,0},{2,1},{3,2},{4,7},{5,4},{6,5},{7,6},{8,11},{9,8},{10,9... | collective-permute-start | bytes 2457608 | tf_op jit(solution)/shard_map/ppermute | solution.py:390
  93.4 20.1 %collective-permute-start.10 = (f32[160,1280]{1,0:T(8,128)S(1)}, f32[160,1280]{1,0:T(8,128)S(1)}, u32[]{:S(2)}, u32[]{:S(2)}) collective-permute-start(f32[160,1280]{1,0:T(8,128)S(1)} %pad_maximum_fusion.b0), channel_id=1, source_target_pairs={{0,2},{1,3},{2,0},{3,1},{4,6},{5,7},{6,4},{7,5},{8,10},{9,11},{10,... | collective-permute-start | bytes 2457608 | tf_op jit(solution)/shard_map/ppermute | solution.py:390
  93.8 39.0 %collective-permute-start.11 = (f32[160,1280]{1,0:T(8,128)S(1)}, f32[160,1280]{1,0:T(8,128)}, u32[]{:S(2)}, u32[]{:S(2)}) collective-permute-start(f32[160,1280]{1,0:T(8,128)S(1)} %pad_maximum_fusion.b0), channel_id=1, source_target_pairs={{0,1},{1,2},{2,3},{3,0},{4,5},{5,6},{6,7},{7,4},{8,9},{9,10},{10,1... | collective-permute-start | bytes 2457608 | tf_op jit(solution)/shard_map/ppermute | solution.py:390
  95.1 8.4 %copy-start.7 = (s32[8,64]{1,0:T(8,128)S(1)}, s32[8,64]{1,0:T(8,128)}, u32[]{:S(2)}) copy-start(s32[8,64]{1,0:T(8,128)} %param.10) | copy-start | bytes 6148
  96.4 77.0 %collective-permute-start.15 = (f32[160,640]{1,0:T(8,128)}, f32[160,640]{1,0:T(8,128)}, u32[]{:S(2)}, u32[]{:S(2)}) collective-permute-start(f32[160,640]{1,0:T(8,128)} %get-tuple-element.39), channel_id=1, source_target_pairs={{1,0},{3,2},{4,7},{6,5},{9,8},{11,10},{12,15},{14,13},{17,16},{19,... | collective-permute-start | bytes 1228808 | tf_op jit(solution)/shard_map/ppermute | solution.py:390
  111.1 21.6 %copy-start.3 = (f32[160,1280]{1,0:T(8,128)}, f32[160,1280]{1,0:T(8,128)S(1)}, u32[]{:S(2)}) copy-start(f32[160,1280]{1,0:T(8,128)S(1)} %collective-permute-done.9.b1) | copy-start | bytes 2457604
  113.5 0.9 copy-start.4
  153.3 90.7 %all-to-all-start.4 = ((f32[64,24,256]{2,1,0:T(8,128)}), f32[64,24,256]{2,1,0:T(8,128)}, u32[]{:S(2)}, u32[]{:S(2)}) async-start(f32[64,24,256]{2,1,0:T(8,128)} %update.1), calls=%async_computation.4 | async-start | bytes 3145728 | tf_op jit(solution)/shard_map/all_to_all | solution.py:428
  161.9 10.7 %copy-start.6 = (f32[160,640]{1,0:T(8,128)S(1)}, f32[160,640]{1,0:T(8,128)}, u32[]{:S(2)}) copy-start(f32[160,640]{1,0:T(8,128)} %get-tuple-element.40) | copy-start | bytes 1228804
  161.9 11.4 %copy-start.5 = (f32[160,640]{1,0:T(8,128)S(1)}, f32[160,640]{1,0:T(8,128)}, u32[]{:S(2)}) copy-start(f32[160,640]{1,0:T(8,128)} %get-tuple-element.38) | copy-start | bytes 1228804
  164.4 27.9 %collective-permute-start.12 = (f32[640,256]{1,0:T(8,128)S(1)}, f32[640,256]{1,0:T(8,128)S(1)}, u32[]{:S(2)}, u32[]{:S(2)}) collective-permute-start(f32[640,256]{1,0:T(8,128)S(1)} %bitcast.91), channel_id=1, source_target_pairs={{1,0},{3,2},{4,7},{6,5},{9,8},{11,10},{12,15},{14,13},{17,16},{19,... | collective-permute-start | bytes 1966088 | tf_op jit(solution)/shard_map/ppermute | solution.py:390
  168.8 23.4 %collective-permute-start.13 = (f32[640,256]{1,0:T(8,128)S(1)}, f32[640,256]{1,0:T(8,128)S(1)}, u32[]{:S(2)}, u32[]{:S(2)}) collective-permute-start(f32[640,256]{1,0:T(8,128)S(1)} %bitcast.90), channel_id=1, source_target_pairs={{0,2},{2,0},{5,7},{7,5},{8,10},{10,8},{13,15},{15,13},{16,18},{18,... | collective-permute-start | bytes 1966088 | tf_op jit(solution)/shard_map/ppermute | solution.py:390
  169.5 22.8 %collective-permute-start.14 = (f32[640,256]{1,0:T(8,128)S(1)}, f32[640,256]{1,0:T(8,128)S(1)}, u32[]{:S(2)}, u32[]{:S(2)}) collective-permute-start(f32[640,256]{1,0:T(8,128)S(1)} %bitcast.89), channel_id=1, source_target_pairs={{1,2},{3,0},{4,5},{6,7},{9,10},{11,8},{12,13},{14,15},{17,18},{19,... | collective-permute-start | bytes 1966088 | tf_op jit(solution)/shard_map/ppermute | solution.py:390
  172.6 3.5 %collective-permute-start.16 = (f32[160,640]{1,0:T(8,128)S(1)}, f32[160,640]{1,0:T(8,128)S(1)}, u32[]{:S(2)}, u32[]{:S(2)}) collective-permute-start(f32[160,640]{1,0:T(8,128)S(1)} %copy-done.6), channel_id=1, source_target_pairs={{0,2},{2,0},{5,7},{7,5},{8,10},{10,8},{13,15},{15,13},{16,18},{18,... | collective-permute-start | bytes 1228808 | tf_op jit(solution)/shard_map/ppermute | solution.py:390
  173.3 18.9 %collective-permute-start.17 = (f32[160,640]{1,0:T(8,128)S(1)}, f32[160,640]{1,0:T(8,128)S(1)}, u32[]{:S(2)}, u32[]{:S(2)}) collective-permute-start(f32[160,640]{1,0:T(8,128)S(1)} %copy-done.5), channel_id=1, source_target_pairs={{1,2},{3,0},{4,5},{6,7},{9,10},{11,8},{12,13},{14,15},{17,18},{19,... | collective-permute-start | bytes 1228808 | tf_op jit(solution)/shard_map/ppermute | solution.py:390
  176.1 18.0 %copy-start.12 = (f32[160,640]{1,0:T(8,128)}, f32[160,640]{1,0:T(8,128)S(1)}, u32[]{:S(2)}) copy-start(f32[160,640]{1,0:T(8,128)S(1)} %collective-permute-done.16.f2) | copy-start | bytes 1228804
  192.3 1.8 copy-start.13
  192.3 1.8 copy-start.9
  192.3 0.9 copy-start.10
  193.1 0.9 copy-start.11
  224.8 10.6 %collective-permute-start.18 = (f32[160,640]{1,0:T(8,128)}, f32[160,640]{1,0:T(8,128)S(1)}, u32[]{:S(2)}, u32[]{:S(2)}) collective-permute-start(f32[160,640]{1,0:T(8,128)} %get-tuple-element.15), channel_id=1, source_target_pairs={{0,1},{2,3},{5,6},{7,4},{8,9},{10,11},{13,14},{15,12},{16,17},{18,... | collective-permute-start | bytes 1228808 | tf_op jit(solution)/shard_map/ppermute | solution.py:390
  226.1 9.3 %collective-permute-start.19 = (f32[160,640]{1,0:T(8,128)}, f32[160,640]{1,0:T(8,128)S(1)}, u32[]{:S(2)}, u32[]{:S(2)}) collective-permute-start(f32[160,640]{1,0:T(8,128)} %get-tuple-element.16), channel_id=1, source_target_pairs={{0,2},{2,0},{5,7},{7,5},{8,10},{10,8},{13,15},{15,13},{16,18},{18,... | collective-permute-start | bytes 1228808 | tf_op jit(solution)/shard_map/ppermute | solution.py:390
  226.8 15.5 %collective-permute-start.20 = (f32[160,640]{1,0:T(8,128)}, f32[160,640]{1,0:T(8,128)S(1)}, u32[]{:S(2)}, u32[]{:S(2)}) collective-permute-start(f32[160,640]{1,0:T(8,128)} %get-tuple-element.17), channel_id=1, source_target_pairs={{0,3},{2,1},{5,4},{7,6},{8,11},{10,9},{13,12},{15,14},{16,19},{18,... | collective-permute-start | bytes 1228808 | tf_op jit(solution)/shard_map/ppermute | solution.py:390

commit v6 on v5

--- a/solution.py
+++ b/solution.py
@@ -282,12 +282,12 @@
             pltpu.SemaphoreType.DMA((4,)),
             pltpu.SemaphoreType.DMA((3,)),
         ],
-        compiler_params=pltpu.CompilerParams(vmem_limit_bytes=VMEM),
+        compiler_params=pltpu.CompilerParams(vmem_limit_bytes=44 << 20),
         cost_estimate=pl.CostEstimate(
             flops=6 * 10 * d**3, bytes_accessed=16 * d * d, transcendentals=0
         ),
         name="refresh",
-    )(scalars, *pieces, *factors, b_hi, b_lo)
+    )(scalars, *(pltpu.with_memory_space_constraint(v, pltpu.HBM) for v in (*pieces, *factors, b_hi, b_lo)))
 
 
 def line(x, z, core):
@@ -397,12 +397,8 @@
     left_slot = target_slot(y - 1)
 
     def to_targets(pick):
-        return (
-            pick(own_slot),
-            move(pick(left_slot), -1, 1),
-            move(pick(1 - own_slot), 2, 0),
-            move(pick(1 - left_slot), 1, 1),
-        )
+        back = pick(jnp.where(even, 1 - own_slot, left_slot))
+        return pick(own_slot), move(back, -1, 1), move(back, 2, 0), move(pick(1 - left_slot), 1, 1)
 
     keep = jnp.where(own_slot == 0, valid[0], valid[1])
     scalars = jnp.stack([y, own_slot, keep.astype(jnp.int32)]).astype(jnp.int32)
@@ -428,8 +424,8 @@
     received = lax.all_to_all(sent, "dp", split_axis=0, concat_axis=0, tiled=True)
     own, after, across, before = refresh(scalars, pieces, factors, halves[0], halves[1])
 
+    block_rows = rows * cols // groups
     landed = jnp.take(received, owner, axis=0, mode="clip")
-    block_rows = rows * cols // groups
     train_weights = jnp.where(
         (slot == 0)[:, None, None], landed[:, :block_rows], landed[:, block_rows:2 * block_rows]
     )[:, None]

time: 248 us -> 246 us (level)
  transfers between devices with their start and end apart: 26 -> 26, of which waited for: 13 -> 13; matrix products, arithmetic and copies ran while one was open for 5% -> 5% of each run, Pallas kernels for 21% -> 20%
where the time goes in v6:
time: 246 us; the launch traced here: 245 us
  waiting for transfers between devices  101 us (41%)
  starting transfers between devices  68.4 us (28%)
  Pallas kernels  50 us (20%)
  other arithmetic  12 us (5%)
  local copies, waits for them, and re-layouts  11.3 us (5%)
    ppermute x12, waiting for transfers between devices, move(): return lax.ppermute(v, ('dp', 'mp'), ring(shift, parity))  57.8 us
    pallas_call x1, Pallas kernels, refresh(): pl.pallas_call(refresh_kernel, out_shape=[jax.ShapeDtypeStruct(factors[0]...  29.5 us
    all_to_all x4, starting transfers between devices, exchange(): return lax.all_to_all(v, 'dp', 0, 0, axis_index_groups=lines, tiled=True)  24.5 us
    ppermute x12, starting transfers between devices, move(): return lax.ppermute(v, ('dp', 'mp'), ring(shift, parity))  24.1 us
    all_to_all x4, waiting for transfers between devices, exchange(): return lax.all_to_all(v, 'dp', 0, 0, axis_index_groups=lines, tiled=True)  19.8 us
    pallas_call x1, Pallas kernels, update(): pl.pallas_call(update_kernel, out_shape=jax.ShapeDtypeStruct((groups, pad...  14.1 us
    ppermute x1, waiting for transfers between devices, owned_gradients(): from_down = lax.ppermute(down, 'dp', along(-1))  9.54 us
    all_to_all x1, starting transfers between devices, body(): lax.all_to_all(sent, 'dp', split_axis=0, concat_axis=0, tiled=True)  8.46 us
  transfers between devices with their start and end apart: 26, of which 13 were waited for; matrix products, arithmetic and copies ran while one was open for 5% of the time, Pallas kernels for 20%

profile of v6, /device:TPU:1, one launch (start us, length us, event | category | flops | bytes accessed | tf_op | source)
XLA Modules:
  0.0 245.0 jit_solution(8627755160549371498)
XLA Ops:
  0.6 1.6 bitcast_convert_fusion
  2.3 3.3 %collective-permute-start = (f32[4,8,80,256]{3,2,1,0:T(8,128)S(1)}, f32[4,8,80,256]{3,2,1,0:T(8,128)}, u32[]{:S(2)}, u32[]{:S(2)}) collective-permute-start(f32[4,8,80,256]{3,2,1,0:T(8,128)S(1)} %bitcast_convert_fusion), channel_id=1, source_target_pairs={{0,4},{4,0},{8,12},{12,8},{16,20},{20,16},{24,28},{28,24},{32,36},... | collective-permute-start | bytes 7864328 | tf_op jit(solution)/shard_map/ppermute | solution.py:329
  5.6 4.7 %collective-permute-done = f32[4,8,80,256]{3,2,1,0:T(8,128)} collective-permute-done((f32[4,8,80,256]{3,2,1,0:T(8,128)S(1)}, f32[4,8,80,256]{3,2,1,0:T(8,128)}, u32[]{:S(2)}, u32[]{:S(2)}) %collective-permute-start) | collective-permute-done | bytes 2621472 | tf_op jit(solution)/shard_map/ppermute | solution.py:329
  10.2 2.5 %convert_add_fusion = f32[4,8,80,256]{3,2,1,0:T(8,128)S(1)} fusion(f32[4,8,80,256]{3,2,1,0:T(8,128)} %collective-permute-done, bf16[4,2,8,80,256]{4,3,2,1,0:T(8,128)(2,1)} %bitcast.78, s32[]{:T(128)S(6)} %select_n.194), kind=kLoop, calls=%fused_computation.2 | loop fusion | flops 1310720 | bytes 6553604 | tf_op jit(solution)/shard_map/add | solution.py:330
  12.8 0.8 copy.37
  13.6 6.5 %all-to-all-start.2 = ((f32[8,64,256]{2,1,0:T(8,128)}), f32[8,64,256]{2,1,0:T(8,128)S(1)}, u32[]{:S(2)}, u32[]{:S(2)}) async-start(f32[8,64,256]{2,1,0:T(8,128)} %bitcast.79), calls=%async_computation.2 | async-start | bytes 1048576 | tf_op jit(solution)/shard_map/all_to_all | solution.py:309
  20.1 0.2 dynamic-slice_bitcast_fusion.3
  20.3 2.6 %collective-permute-start.3 = (f32[256,256]{1,0:T(8,128)S(1)}, f32[256,256]{1,0:T(8,128)S(1)}, u32[]{:S(2)}, u32[]{:S(2)}) collective-permute-start(f32[256,256]{1,0:T(8,128)S(1)} %bitcast.93), channel_id=1, source_target_pairs={{0,192},{4,196},{8,200},{12,204},{16,208},{20,212},{24,216},{28,22... | collective-permute-start | bytes 786440 | tf_op jit(solution)/shard_map/ppermute | solution.py:339
  23.1 4.8 %collective-permute-done.3 = f32[256,256]{1,0:T(8,128)S(1)} collective-permute-done((f32[256,256]{1,0:T(8,128)S(1)}, f32[256,256]{1,0:T(8,128)S(1)}, u32[]{:S(2)}, u32[]{:S(2)}) %collective-permute-start.3) | collective-permute-done | bytes 262176 | tf_op jit(solution)/shard_map/ppermute | solution.py:339
  28.0 3.5 %collective-permute-start.4 = (f32[512,256]{1,0:T(8,128)S(1)}, f32[512,256]{1,0:T(8,128)S(1)}, u32[]{:S(2)}, u32[]{:S(2)}) collective-permute-start(f32[512,256]{1,0:T(8,128)S(1)} %pad_maximum_fusion.3), channel_id=1, source_target_pairs={{0,192},{4,196},{8,200},{12,204},{16,208},{20,212},{24,216},{28,22... | collective-permute-start | bytes 1572872 | tf_op jit(solution)/shard_map/ppermute | solution.py:346
  31.7 9.5 %collective-permute-done.4 = f32[512,256]{1,0:T(8,128)S(1)} collective-permute-done((f32[512,256]{1,0:T(8,128)S(1)}, f32[512,256]{1,0:T(8,128)S(1)}, u32[]{:S(2)}, u32[]{:S(2)}) %collective-permute-start.4) | collective-permute-done | bytes 524320 | tf_op jit(solution)/shard_map/ppermute | solution.py:346
  41.2 3.3 %collective-permute-done.2 = f32[512,256]{1,0:T(8,128)S(1)} collective-permute-done((f32[512,256]{1,0:T(8,128)S(1)}, f32[512,256]{1,0:T(8,128)S(1)}, u32[]{:S(2)}, u32[]{:S(2)}) %collective-permute-start.2) | collective-permute-done | bytes 524320 | tf_op jit(solution)/shard_map/ppermute | solution.py:345
  44.5 0.9 fusion
  45.4 6.1 %all-to-all-start = ((f32[8,64,256]{2,1,0:T(8,128)}), f32[8,64,256]{2,1,0:T(8,128)S(1)}, u32[]{:S(2)}, u32[]{:S(2)}) async-start(f32[8,64,256]{2,1,0:T(8,128)} %bitcast.14), calls=%async_computation | async-start | bytes 1048576 | tf_op jit(solution)/shard_map/all_to_all | solution.py:309
  51.5 0.2 convert_reduce_fusion
  52.5 0.2 collective-permute-start.6
  52.7 0.7 collective-permute-start.7
  53.4 0.6 collective-permute-start.5
  54.0 11.8 %all-to-all-done = f32[8,64,256]{2,1,0:T(8,128)S(1)} async-done(((f32[8,64,256]{2,1,0:T(8,128)}), f32[8,64,256]{2,1,0:T(8,128)S(1)}, u32[]{:S(2)}, u32[]{:S(2)}) %all-to-all-start) | async-done | bytes 524320 | tf_op jit(solution)/shard_map/all_to_all | solution.py:309
  65.9 0.8 broadcast_in_dim.79
  66.7 7.5 %all-to-all-start.1 = ((f32[8,64,256]{2,1,0:T(8,128)}), f32[8,64,256]{2,1,0:T(8,128)S(1)}, u32[]{:S(2)}, u32[]{:S(2)}) async-start(f32[8,64,256]{2,1,0:T(8,128)} %broadcast_in_dim.79), calls=%async_computation.1 | async-start | bytes 1048576 | tf_op jit(solution)/shard_map/all_to_all | solution.py:309
  74.3 0.2 collective-permute-start.8
  74.5 1.1 collective-permute-done.8
  75.7 8.0 %all-to-all-done.1 = f32[8,64,256]{2,1,0:T(8,128)S(1)} async-done(((f32[8,64,256]{2,1,0:T(8,128)}), f32[8,64,256]{2,1,0:T(8,128)S(1)}, u32[]{:S(2)}, u32[]{:S(2)}) %all-to-all-start.1) | async-done | bytes 524320 | tf_op jit(solution)/shard_map/all_to_all | solution.py:309
  83.7 1.7 gather_fusion
  85.4 4.4 %all-to-all-start.3 = ((f32[8,2,80,256]{3,2,1,0:T(8,128)}), f32[8,2,80,256]{3,2,1,0:T(8,128)}, u32[]{:S(2)}, u32[]{:S(2)}) async-start(f32[8,2,80,256]{3,2,1,0:T(8,128)} %bitcast.22), calls=%async_computation.3 | async-start | bytes 2621440 | tf_op jit(solution)/shard_map/all_to_all | solution.py:309
  89.8 0.6 fusion.5
  90.6 2.8 %collective-permute-start.9 = (f32[160,1280]{1,0:T(8,128)S(1)}, f32[160,1280]{1,0:T(8,128)S(1)}, u32[]{:S(2)}, u32[]{:S(2)}) collective-permute-start(f32[160,1280]{1,0:T(8,128)S(1)} %pad_maximum_fusion.b0), channel_id=1, source_target_pairs={{0,3},{1,0},{2,1},{3,2},{4,7},{5,4},{6,5},{7,6},{8,11},{9,8},{10,9... | collective-permute-start | bytes 2457608 | tf_op jit(solution)/shard_map/ppermute | solution.py:390
  93.5 0.4 collective-permute-start.10
  93.8 0.7 collective-permute-start.11
  94.5 0.6 fusion.4
  95.1 1.1 select_bitcast_fusion.2
  96.3 4.7 %collective-permute-start.15 = (f32[160,640]{1,0:T(8,128)}, f32[160,640]{1,0:T(8,128)}, u32[]{:S(2)}, u32[]{:S(2)}) collective-permute-start(f32[160,640]{1,0:T(8,128)} %get-tuple-element.38), channel_id=1, source_target_pairs={{1,0},{3,2},{4,7},{6,5},{9,8},{11,10},{12,15},{14,13},{17,16},{19,... | collective-permute-start | bytes 1228808 | tf_op jit(solution)/shard_map/ppermute | solution.py:390
  101.0 0.6 fusion.9
  102.8 0.6 pad_add_fusion.at
  103.4 0.6 select_reduce_fusion.1.chosen
  104.1 7.0 %collective-permute-done.9.b1 = f32[160,1280]{1,0:T(8,128)S(1)} collective-permute-done((f32[160,1280]{1,0:T(8,128)S(1)}, f32[160,1280]{1,0:T(8,128)S(1)}, u32[]{:S(2)}, u32[]{:S(2)}) %collective-permute-start.9) | collective-permute-done | bytes 819232 | tf_op jit(solution)/shard_map/ppermute | solution.py:390
  111.1 2.4 collective-permute-done.10.b2
  113.6 0.9 copy-done.5
  114.5 18.3 %collective-permute-done.11.b3 = f32[160,1280]{1,0:T(8,128)} collective-permute-done((f32[160,1280]{1,0:T(8,128)S(1)}, f32[160,1280]{1,0:T(8,128)}, u32[]{:S(2)}, u32[]{:S(2)}) %collective-permute-start.11) | collective-permute-done | bytes 819232 | tf_op jit(solution)/shard_map/ppermute | solution.py:390
  132.8 6.4 %prepare.1 = (bf16[2,640,640]{2,1,0:T(8,128)(2,1)}, bf16[2,640,640]{2,1,0:T(8,128)(2,1)}, bf16[2,640,640]{2,1,0:T(8,128)(2,1)}, bf16[2,640,640]{2,1,0:T(8,128)(2,1)}) custom-call(s32[3]{0:T(128)} %pad_add_fusion.at, f32[160,1280]{1,0:T(8,128)} %copy-done.1, f32[160,1280]{1,0:T(8,128)} %copy-done.4, f32[160,1280]{1,0:T(8,128)} %copy-done.5, ...), custom_call_target="tpu_custom_call" | custom-call | flops 3276800 | bytes 9830400 | tf_op jit(solution)/shard_map/prepare/pallas_call | solution.py:83
  139.2 14.1 %update.1 = f32[64,24,256]{2,1,0:T(8,128)} custom-call(s32[2,64]{1,0:T(2,128)} %select_reduce_fusion.1.chosen, f32[8,2,80,256]{3,2,1,0:T(8,128)} %all-to-all-done.3.refs_0_, bf16[2,640,640]{2,1,0:T(8,128)(2,1)} %get-tuple-element.10.refs_1_.b_hi, bf16[2,640,640]{2,1,0:T(8,128)(2,1)} %get-tuple-element.11.refs_2_.b_lo, ...), custom_call_target="tpu_custom_call" | custom-call | flops 2516582400 | bytes 5898240 | tf_op jit(solution)/shard_map/update/pallas_call | solution.py:152
  153.3 8.5 %all-to-all-start.4 = ((f32[64,24,256]{2,1,0:T(8,128)}), f32[64,24,256]{2,1,0:T(8,128)S(1)}, u32[]{:S(2)}, u32[]{:S(2)}) async-start(f32[64,24,256]{2,1,0:T(8,128)} %update.1), calls=%async_computation.4 | async-start | bytes 3145728 | tf_op jit(solution)/shard_map/all_to_all | solution.py:424
  161.8 2.4 slice_select_fusion
  164.2 4.4 %collective-permute-start.12 = (f32[640,256]{1,0:T(8,128)S(1)}, f32[640,256]{1,0:T(8,128)S(1)}, u32[]{:S(2)}, u32[]{:S(2)}) collective-permute-start(f32[640,256]{1,0:T(8,128)S(1)} %bitcast.87), channel_id=1, source_target_pairs={{1,0},{3,2},{4,7},{6,5},{9,8},{11,10},{12,15},{14,13},{17,16},{19,... | collective-permute-start | bytes 1966088 | tf_op jit(solution)/shard_map/ppermute | solution.py:390
  168.6 0.7 collective-permute-start.13
  169.3 3.1 %collective-permute-start.14 = (f32[640,256]{1,0:T(8,128)S(1)}, f32[640,256]{1,0:T(8,128)S(1)}, u32[]{:S(2)}, u32[]{:S(2)}) collective-permute-start(f32[640,256]{1,0:T(8,128)S(1)} %bitcast.86), channel_id=1, source_target_pairs={{1,2},{3,0},{4,5},{6,7},{9,10},{11,8},{12,13},{14,15},{17,18},{19,... | collective-permute-start | bytes 1966088 | tf_op jit(solution)/shard_map/ppermute | solution.py:390
  172.4 0.7 collective-permute-start.16
  173.1 2.7 %collective-permute-start.17 = (f32[160,640]{1,0:T(8,128)S(1)}, f32[160,640]{1,0:T(8,128)S(1)}, u32[]{:S(2)}, u32[]{:S(2)}) collective-permute-start(f32[160,640]{1,0:T(8,128)S(1)} %copy-done.6), channel_id=1, source_target_pairs={{1,2},{3,0},{4,5},{6,7},{9,10},{11,8},{12,13},{14,15},{17,18},{19,... | collective-permute-start | bytes 1228808 | tf_op jit(solution)/shard_map/ppermute | solution.py:390
  175.8 16.1 %collective-permute-done.17.f3 = f32[160,640]{1,0:T(8,128)S(1)} collective-permute-done((f32[160,640]{1,0:T(8,128)S(1)}, f32[160,640]{1,0:T(8,128)S(1)}, u32[]{:S(2)}, u32[]{:S(2)}) %collective-permute-start.17) | collective-permute-done | bytes 409632 | tf_op jit(solution)/shard_map/ppermute | solution.py:390
  192.0 0.7 copy-done.13
  192.7 0.2 copy-done.9
  192.9 0.2 copy-done.10
  193.1 0.2 copy-done.11
  193.4 29.5 %refresh.1 = (f32[160,640]{1,0:T(8,128)S(1)}, f32[160,640]{1,0:T(8,128)S(1)}, f32[160,640]{1,0:T(8,128)S(1)}, f32[160,640]{1,0:T(8,128)S(1)}) custom-call(s32[3]{0:T(128)S(1)} %copy-done, f32[640,256]{1,0:T(8,128)} %bitcast.85, f32[640,256]{1,0:T(8,128)} %copy-done.9, f32[640,256]{1,0:T(8,128)} %copy-done.10, f32[640,256]{1,0:T(8,128)} %copy-done.11, ...), custom_call_target="tpu_custom_call" | custom-call | flops 15728640000 | bytes 6553600 | tf_op jit(solution)/shard_map/refresh/pallas_call | solution.py:267
  222.8 1.3 collective-permute-start.18
  224.1 1.4 collective-permute-start.19
  225.6 1.3 collective-permute-start.20
  226.9 6.3 %collective-permute-done.18 = f32[160,640]{1,0:T(8,128)} collective-permute-done((f32[160,640]{1,0:T(8,128)S(1)}, f32[160,640]{1,0:T(8,128)}, u32[]{:S(2)}, u32[]{:S(2)}) %collective-permute-start.18) | collective-permute-done | bytes 409632 | tf_op jit(solution)/shard_map/ppermute | solution.py:390
  233.2 7.6 %collective-permute-done.20 = f32[160,640]{1,0:T(8,128)} collective-permute-done((f32[160,640]{1,0:T(8,128)S(1)}, f32[160,640]{1,0:T(8,128)}, u32[]{:S(2)}, u32[]{:S(2)}) %collective-permute-start.20) | collective-permute-done | bytes 409632 | tf_op jit(solution)/shard_map/ppermute | solution.py:390
  240.8 1.2 select_bitcast_fusion.1
  242.1 1.5 copy.45
  243.6 0.6 gather_fusion.1
  244.3 0.7 copy.44
  (69 shorter events, 1.7 us)
Async XLA Ops:
  2.3 8.0 %collective-permute-start = (f32[4,8,80,256]{3,2,1,0:T(8,128)S(1)}, f32[4,8,80,256]{3,2,1,0:T(8,128)}, u32[]{:S(2)}, u32[]{:S(2)}) collective-permute-start(f32[4,8,80,256]{3,2,1,0:T(8,128)S(1)} %bitcast_convert_fusion), channel_id=1, source_target_pairs={{0,4},{4,0},{8,12},{12,8},{16,20},{20,16},{24,28},{28,24},{32,36},... | collective-permute-start | bytes 7864328 | tf_op jit(solution)/shard_map/ppermute | solution.py:329
  13.6 31.8 %all-to-all-start.2 = ((f32[8,64,256]{2,1,0:T(8,128)}), f32[8,64,256]{2,1,0:T(8,128)S(1)}, u32[]{:S(2)}, u32[]{:S(2)}) async-start(f32[8,64,256]{2,1,0:T(8,128)} %bitcast.79), calls=%async_computation.2 | async-start | bytes 1048576 | tf_op jit(solution)/shard_map/all_to_all | solution.py:309
  20.3 7.6 %collective-permute-start.3 = (f32[256,256]{1,0:T(8,128)S(1)}, f32[256,256]{1,0:T(8,128)S(1)}, u32[]{:S(2)}, u32[]{:S(2)}) collective-permute-start(f32[256,256]{1,0:T(8,128)S(1)} %bitcast.93), channel_id=1, source_target_pairs={{0,192},{4,196},{8,200},{12,204},{16,208},{20,212},{24,216},{28,22... | collective-permute-start | bytes 786440 | tf_op jit(solution)/shard_map/ppermute | solution.py:339
  22.9 8.5 %collective-permute-start.1 = (f32[256,256]{1,0:T(8,128)S(1)}, f32[256,256]{1,0:T(8,128)S(1)}, u32[]{:S(2)}, u32[]{:S(2)}) collective-permute-start(f32[256,256]{1,0:T(8,128)S(1)} %bitcast.92), channel_id=1, source_target_pairs={{0,64},{4,68},{8,72},{12,76},{16,80},{20,84},{24,88},{28,92},{32,9... | collective-permute-start | bytes 786440 | tf_op jit(solution)/shard_map/ppermute | solution.py:338
  28.0 13.3 %collective-permute-start.4 = (f32[512,256]{1,0:T(8,128)S(1)}, f32[512,256]{1,0:T(8,128)S(1)}, u32[]{:S(2)}, u32[]{:S(2)}) collective-permute-start(f32[512,256]{1,0:T(8,128)S(1)} %pad_maximum_fusion.3), channel_id=1, source_target_pairs={{0,192},{4,196},{8,200},{12,204},{16,208},{20,212},{24,216},{28,22... | collective-permute-start | bytes 1572872 | tf_op jit(solution)/shard_map/ppermute | solution.py:346
  31.6 13.0 %collective-permute-start.2 = (f32[512,256]{1,0:T(8,128)S(1)}, f32[512,256]{1,0:T(8,128)S(1)}, u32[]{:S(2)}, u32[]{:S(2)}) collective-permute-start(f32[512,256]{1,0:T(8,128)S(1)} %pad_maximum_fusion.2), channel_id=1, source_target_pairs={{0,64},{4,68},{8,72},{12,76},{16,80},{20,84},{24,88},{28,92},{32,9... | collective-permute-start | bytes 1572872 | tf_op jit(solution)/shard_map/ppermute | solution.py:345
  31.7 19.8 %copy-start.8 = (s32[8]{0:T(128)S(1)}, s32[8]{0:T(128)}, u32[]{:S(2)}) copy-start(s32[8]{0:T(128)} %param.9) | copy-start | bytes 100
  45.4 20.4 %all-to-all-start = ((f32[8,64,256]{2,1,0:T(8,128)}), f32[8,64,256]{2,1,0:T(8,128)S(1)}, u32[]{:S(2)}, u32[]{:S(2)}) async-start(f32[8,64,256]{2,1,0:T(8,128)} %bitcast.14), calls=%async_computation | async-start | bytes 1048576 | tf_op jit(solution)/shard_map/all_to_all | solution.py:309
  52.5 21.8 %collective-permute-start.6 = (f32[64,256]{1,0:T(8,128)S(1)}, f32[64,256]{1,0:T(8,128)S(1)}, u32[]{:S(2)}, u32[]{:S(2)}) collective-permute-start(f32[64,256]{1,0:T(8,128)S(1)} %reduce_sum.48), channel_id=1, source_target_pairs={{0,192},{4,196},{8,200},{12,204},{16,208},{20,212},{24,216},{28,22... | collective-permute-start | bytes 196616 | tf_op jit(solution)/shard_map/ppermute | solution.py:352
  52.7 21.6 %collective-permute-start.7 = (f32[64,256]{1,0:T(8,128)S(1)}, f32[64,256]{1,0:T(8,128)S(1)}, u32[]{:S(2)}, u32[]{:S(2)}) collective-permute-start(f32[64,256]{1,0:T(8,128)S(1)} %reduce_sum.48), channel_id=1, source_target_pairs={{0,128},{4,132},{8,136},{12,140},{16,144},{20,148},{24,152},{28,15... | collective-permute-start | bytes 196616 | tf_op jit(solution)/shard_map/ppermute | solution.py:352
  53.4 20.9 %collective-permute-start.5 = (f32[64,256]{1,0:T(8,128)S(1)}, f32[64,256]{1,0:T(8,128)S(1)}, u32[]{:S(2)}, u32[]{:S(2)}) collective-permute-start(f32[64,256]{1,0:T(8,128)S(1)} %reduce_sum.48), channel_id=1, source_target_pairs={{0,64},{4,68},{8,72},{12,76},{16,80},{20,84},{24,88},{28,92},{32,9... | collective-permute-start | bytes 196616 | tf_op jit(solution)/shard_map/ppermute | solution.py:351
  66.7 16.9 %all-to-all-start.1 = ((f32[8,64,256]{2,1,0:T(8,128)}), f32[8,64,256]{2,1,0:T(8,128)S(1)}, u32[]{:S(2)}, u32[]{:S(2)}) async-start(f32[8,64,256]{2,1,0:T(8,128)} %broadcast_in_dim.79), calls=%async_computation.1 | async-start | bytes 1048576 | tf_op jit(solution)/shard_map/all_to_all | solution.py:309
  74.3 1.3 collective-permute-start.8
  85.4 4.4 %copy-start.2 = (f32[1,160,2,640]{3,2,1,0:T(2,128)S(1)}, f32[1,160,2,640]{3,2,1,0:T(2,128)}, u32[]{:S(2)}) copy-start(f32[1,160,2,640]{3,2,1,0:T(2,128)} %param.12) | copy-start | bytes 2457604
  85.4 53.8 %all-to-all-start.3 = ((f32[8,2,80,256]{3,2,1,0:T(8,128)}), f32[8,2,80,256]{3,2,1,0:T(8,128)}, u32[]{:S(2)}, u32[]{:S(2)}) async-start(f32[8,2,80,256]{3,2,1,0:T(8,128)} %bitcast.22), calls=%async_computation.3 | async-start | bytes 2621440 | tf_op jit(solution)/shard_map/all_to_all | solution.py:309
  90.5 4.0 %copy-start.3 = (f32[1,160,2,640]{3,2,1,0:T(2,128)S(1)}, f32[1,160,2,640]{3,2,1,0:T(2,128)}, u32[]{:S(2)}) copy-start(f32[1,160,2,640]{3,2,1,0:T(2,128)} %param.11) | copy-start | bytes 2457604
  90.6 5.7 %copy-start.1 = (f32[160,1280]{1,0:T(8,128)}, f32[160,1280]{1,0:T(8,128)S(1)}, u32[]{:S(2)}) copy-start(f32[160,1280]{1,0:T(8,128)S(1)} %pad_maximum_fusion.b0) | copy-start | bytes 2457604
  90.6 20.5 %collective-permute-start.9 = (f32[160,1280]{1,0:T(8,128)S(1)}, f32[160,1280]{1,0:T(8,128)S(1)}, u32[]{:S(2)}, u32[]{:S(2)}) collective-permute-start(f32[160,1280]{1,0:T(8,128)S(1)} %pad_maximum_fusion.b0), channel_id=1, source_target_pairs={{0,3},{1,0},{2,1},{3,2},{4,7},{5,4},{6,5},{7,6},{8,11},{9,8},{10,9... | collective-permute-start | bytes 2457608 | tf_op jit(solution)/shard_map/ppermute | solution.py:390
  93.5 20.1 %collective-permute-start.10 = (f32[160,1280]{1,0:T(8,128)S(1)}, f32[160,1280]{1,0:T(8,128)S(1)}, u32[]{:S(2)}, u32[]{:S(2)}) collective-permute-start(f32[160,1280]{1,0:T(8,128)S(1)} %pad_maximum_fusion.b0), channel_id=1, source_target_pairs={{0,2},{1,3},{2,0},{3,1},{4,6},{5,7},{6,4},{7,5},{8,10},{9,11},{10,... | collective-permute-start | bytes 2457608 | tf_op jit(solution)/shard_map/ppermute | solution.py:390
  93.8 39.0 %collective-permute-start.11 = (f32[160,1280]{1,0:T(8,128)S(1)}, f32[160,1280]{1,0:T(8,128)}, u32[]{:S(2)}, u32[]{:S(2)}) collective-permute-start(f32[160,1280]{1,0:T(8,128)S(1)} %pad_maximum_fusion.b0), channel_id=1, source_target_pairs={{0,1},{1,2},{2,3},{3,0},{4,5},{5,6},{6,7},{7,4},{8,9},{9,10},{10,1... | collective-permute-start | bytes 2457608 | tf_op jit(solution)/shard_map/ppermute | solution.py:390
  94.5 8.9 %copy-start.7 = (s32[8,64]{1,0:T(8,128)S(1)}, s32[8,64]{1,0:T(8,128)}, u32[]{:S(2)}) copy-start(s32[8,64]{1,0:T(8,128)} %param.10) | copy-start | bytes 6148
  96.3 76.8 %collective-permute-start.15 = (f32[160,640]{1,0:T(8,128)}, f32[160,640]{1,0:T(8,128)}, u32[]{:S(2)}, u32[]{:S(2)}) collective-permute-start(f32[160,640]{1,0:T(8,128)} %get-tuple-element.38), channel_id=1, source_target_pairs={{1,0},{3,2},{4,7},{6,5},{9,8},{11,10},{12,15},{14,13},{17,16},{19,... | collective-permute-start | bytes 1228808 | tf_op jit(solution)/shard_map/ppermute | solution.py:390
  111.1 21.6 %copy-start.4 = (f32[160,1280]{1,0:T(8,128)}, f32[160,1280]{1,0:T(8,128)S(1)}, u32[]{:S(2)}) copy-start(f32[160,1280]{1,0:T(8,128)S(1)} %collective-permute-done.9.b1) | copy-start | bytes 2457604
  113.6 0.9 copy-start.5
  153.3 90.3 %all-to-all-start.4 = ((f32[64,24,256]{2,1,0:T(8,128)}), f32[64,24,256]{2,1,0:T(8,128)S(1)}, u32[]{:S(2)}, u32[]{:S(2)}) async-start(f32[64,24,256]{2,1,0:T(8,128)} %update.1), calls=%async_computation.4 | async-start | bytes 3145728 | tf_op jit(solution)/shard_map/all_to_all | solution.py:424
  161.8 11.3 %copy-start.6 = (f32[160,640]{1,0:T(8,128)S(1)}, f32[160,640]{1,0:T(8,128)}, u32[]{:S(2)}) copy-start(f32[160,640]{1,0:T(8,128)} %get-tuple-element.37) | copy-start | bytes 1228804
  161.8 31.6 %copy-start = (s32[3]{0:T(128)S(1)}, s32[3]{0:T(128)}, u32[]{:S(2)}) copy-start(s32[3]{0:T(128)} %pad_add_fusion.at) | copy-start | bytes 40
  164.2 27.8 %collective-permute-start.12 = (f32[640,256]{1,0:T(8,128)S(1)}, f32[640,256]{1,0:T(8,128)S(1)}, u32[]{:S(2)}, u32[]{:S(2)}) collective-permute-start(f32[640,256]{1,0:T(8,128)S(1)} %bitcast.87), channel_id=1, source_target_pairs={{1,0},{3,2},{4,7},{6,5},{9,8},{11,10},{12,15},{14,13},{17,16},{19,... | collective-permute-start | bytes 1966088 | tf_op jit(solution)/shard_map/ppermute | solution.py:390
  168.6 23.4 %collective-permute-start.13 = (f32[640,256]{1,0:T(8,128)S(1)}, f32[640,256]{1,0:T(8,128)S(1)}, u32[]{:S(2)}, u32[]{:S(2)}) collective-permute-start(f32[640,256]{1,0:T(8,128)S(1)} %bitcast.88), channel_id=1, source_target_pairs={{0,2},{2,0},{5,7},{7,5},{8,10},{10,8},{13,15},{15,13},{16,18},{18,... | collective-permute-start | bytes 1966088 | tf_op jit(solution)/shard_map/ppermute | solution.py:390
  169.3 22.7 %collective-permute-start.14 = (f32[640,256]{1,0:T(8,128)S(1)}, f32[640,256]{1,0:T(8,128)S(1)}, u32[]{:S(2)}, u32[]{:S(2)}) collective-permute-start(f32[640,256]{1,0:T(8,128)S(1)} %bitcast.86), channel_id=1, source_target_pairs={{1,2},{3,0},{4,5},{6,7},{9,10},{11,8},{12,13},{14,15},{17,18},{19,... | collective-permute-start | bytes 1966088 | tf_op jit(solution)/shard_map/ppermute | solution.py:390
  172.4 3.5 %collective-permute-start.16 = (f32[160,640]{1,0:T(8,128)}, f32[160,640]{1,0:T(8,128)S(1)}, u32[]{:S(2)}, u32[]{:S(2)}) collective-permute-start(f32[160,640]{1,0:T(8,128)} %get-tuple-element.38), channel_id=1, source_target_pairs={{0,2},{2,0},{5,7},{7,5},{8,10},{10,8},{13,15},{15,13},{16,18},{18,... | collective-permute-start | bytes 1228808 | tf_op jit(solution)/shard_map/ppermute | solution.py:390
  173.1 18.9 %collective-permute-start.17 = (f32[160,640]{1,0:T(8,128)S(1)}, f32[160,640]{1,0:T(8,128)S(1)}, u32[]{:S(2)}, u32[]{:S(2)}) collective-permute-start(f32[160,640]{1,0:T(8,128)S(1)} %copy-done.6), channel_id=1, source_target_pairs={{1,2},{3,0},{4,5},{6,7},{9,10},{11,8},{12,13},{14,15},{17,18},{19,... | collective-permute-start | bytes 1228808 | tf_op jit(solution)/shard_map/ppermute | solution.py:390
  175.8 16.2 %copy-start.12 = (f32[160,640]{1,0:T(8,128)}, f32[160,640]{1,0:T(8,128)S(1)}, u32[]{:S(2)}) copy-start(f32[160,640]{1,0:T(8,128)S(1)} %collective-permute-done.16.f2) | copy-start | bytes 1228804
  191.9 0.8 copy-start.13
  191.9 1.0 copy-start.9
  191.9 1.2 copy-start.10
  192.0 1.4 copy-start.11
  222.8 10.4 %collective-permute-start.18 = (f32[160,640]{1,0:T(8,128)S(1)}, f32[160,640]{1,0:T(8,128)}, u32[]{:S(2)}, u32[]{:S(2)}) collective-permute-start(f32[160,640]{1,0:T(8,128)S(1)} %get-tuple-element.15), channel_id=1, source_target_pairs={{0,1},{2,3},{5,6},{7,4},{8,9},{10,11},{13,14},{15,12},{16,17},{18,... | collective-permute-start | bytes 1228808 | tf_op jit(solution)/shard_map/ppermute | solution.py:390
  224.1 9.1 %collective-permute-start.19 = (f32[160,640]{1,0:T(8,128)S(1)}, f32[160,640]{1,0:T(8,128)}, u32[]{:S(2)}, u32[]{:S(2)}) collective-permute-start(f32[160,640]{1,0:T(8,128)S(1)} %get-tuple-element.16), channel_id=1, source_target_pairs={{0,2},{2,0},{5,7},{7,5},{8,10},{10,8},{13,15},{15,13},{16,18},{18,... | collective-permute-start | bytes 1228808 | tf_op jit(solution)/shard_map/ppermute | solution.py:390
  225.6 15.2 %collective-permute-start.20 = (f32[160,640]{1,0:T(8,128)S(1)}, f32[160,640]{1,0:T(8,128)}, u32[]{:S(2)}, u32[]{:S(2)}) collective-permute-start(f32[160,640]{1,0:T(8,128)S(1)} %get-tuple-element.17), channel_id=1, source_target_pairs={{0,3},{2,1},{5,4},{7,6},{8,11},{10,9},{13,12},{15,14},{16,19},{18,... | collective-permute-start | bytes 1228808 | tf_op jit(solution)/shard_map/ppermute | solution.py:390

commit v7 on v6

--- a/solution.py
+++ b/solution.py
@@ -9,7 +9,7 @@
 NS_ITERS = 4
 SLOTS = 2
 BLOCK = 256
-FIRST = 64
+FIRST = 72
 VMEM = 63 << 20
 PARTS = (80,)
 NX, NZ, NC = 4, 8, 2
@@ -174,14 +174,21 @@
 
 
 def refresh_kernel(
-    at, g0, g1, g2, g3, f0, f1, f2, f3, b_hi, b_lo, o0, o1, o2, o3,
-    g_in, f_in, gbuf, xbuf, abuf, stack, x_ref, a_ref, g_sem, f_sem, b_sem,
+    at, came, g1, g2, g3, f0, f1, f2, f3, b_hi, b_lo, o0, o1, o2, o3,
+    g_in, f_in, gbuf, xbuf, abuf, stack, x_ref, a_ref, own_sem, g_sem, f_sem, b_sem,
 ):
     d = x_ref.shape[0]
-    w = g0.shape[1]
+    w = g1.shape[1]
     kc = 4 * w
     rows = f0.shape[0]
-    get_g = [pltpu.make_async_copy(r, g_in.at[k], g_sem.at[k]) for k, r in enumerate((g0, g1, g2, g3))]
+    part = came.shape[2]
+    get_own = [
+        pltpu.make_async_copy(came.at[z, at[1]], g_in.at[0, pl.ds(z * part, part)], own_sem.at[z])
+        for z in range(NZ)
+    ]
+    get_g = [get_own] + [
+        [pltpu.make_async_copy(r, g_in.at[k + 1], g_sem.at[k])] for k, r in enumerate((g1, g2, g3))
+    ]
     get_f = [
         pltpu.make_async_copy(r, f_in.at[pl.ds(start, rows)], f_sem.at[k])
         for k, (r, start) in enumerate(zip((f0, f1, f2, f3), row_starts(at[0], rows, 4)))
@@ -190,7 +197,8 @@
         pltpu.make_async_copy(r.at[at[1]], stack.at[pl.ds(k * d, d)], b_sem.at[k])
         for k, r in enumerate((b_hi, b_hi, b_lo))
     ]
-    start_all(get_g)
+    for copies in get_g:
+        start_all(copies)
     start_all(get_f)
     start_all(get_b)
 
@@ -214,7 +222,7 @@
         return mm(abuf[:, :2 * d], stack[:2 * d], NN) + mm(abuf[:, d:2 * d], stack[2 * d:], NN)
 
     for b in range(4):
-        get_g[b].wait()
+        wait_all(get_g[b])
         base = 0
         for part in range(len(PARTS)):
             for source, row, size in scattered(part):
@@ -262,7 +270,7 @@
 
 def refresh(scalars, pieces, factors, b_hi, b_lo):
     d = factors[0].shape[1]
-    w = pieces[0].shape[1]
+    w = pieces[1].shape[1]
     hbm = pl.BlockSpec(memory_space=pltpu.HBM)
     return pl.pallas_call(
         refresh_kernel,
@@ -278,7 +286,8 @@
             pltpu.VMEM((3 * d, d), jnp.bfloat16),
             pltpu.VMEM((d, d), jnp.float32),
             pltpu.VMEM((d, d), jnp.float32),
-            pltpu.SemaphoreType.DMA((4,)),
+            pltpu.SemaphoreType.DMA((NZ,)),
+            pltpu.SemaphoreType.DMA((3,)),
             pltpu.SemaphoreType.DMA((4,)),
             pltpu.SemaphoreType.DMA((3,)),
         ],
@@ -334,17 +343,18 @@
         return near[:, :FIRST].reshape(NZ * FIRST, cols)
 
     cut = NZ * FIRST // 2
-    far = towards(2)
+    far, up, down, home = towards(2), towards(1), towards(3), towards(0)
     far_up = lax.ppermute(far[:cut], "dp", along(1))
     far_down = lax.ppermute(far[cut:], "dp", along(-1))
+    up_late = lax.ppermute(up[cut:], "dp", along(1))
+    down_early = lax.ppermute(down[:cut], "dp", along(-1))
     late = jnp.transpose(chip[:, :, FIRST:], (1, 0, 2, 3)).reshape(NZ, NX * rest, cols)
     late = exchange(late, along_z)
-    up, down = towards(1), towards(3)
-    up = jnp.concatenate([up[:cut] + far_up, up[cut:]], axis=0)
-    down = jnp.concatenate([down[:cut], down[cut:] + far_down], axis=0)
-    from_up = lax.ppermute(up, "dp", along(1))
-    from_down = lax.ppermute(down, "dp", along(-1))
-    over_x = towards(0) + from_up + from_down
+    up_early = lax.ppermute(up[:cut] + far_up, "dp", along(1))
+    down_late = lax.ppermute(down[cut:] + far_down, "dp", along(-1))
+    over_x = jnp.concatenate(
+        [home[:cut] + up_early + down_early, home[cut:] + up_late + down_late], axis=0
+    )
     over_z = jnp.sum(exchange(over_x.reshape(NZ, FIRST, cols), along_z), axis=0)
     mean = over_z * (1.0 / groups)
     late = jnp.sum(late, axis=0)
@@ -396,16 +406,20 @@
     own_slot = target_slot(y)
     left_slot = target_slot(y - 1)
 
-    def to_targets(pick):
+    def to_targets(own, pick):
         back = pick(jnp.where(even, 1 - own_slot, left_slot))
-        return pick(own_slot), move(back, -1, 1), move(back, 2, 0), move(pick(1 - left_slot), 1, 1)
+        return own, move(back, -1, 1), move(back, 2, 0), move(pick(1 - left_slot), 1, 1)
 
     keep = jnp.where(own_slot == 0, valid[0], valid[1])
     scalars = jnp.stack([y, own_slot, keep.astype(jnp.int32)]).astype(jnp.int32)
     basis_rows = jnp.concatenate([basis[0, :, 0], basis[0, :, 1]], axis=1)
     blocks = (basis_rows, move(basis_rows, -1), move(basis_rows, 2), move(basis_rows, 1))
     halves = prepare(scalars, blocks)
-    factors = to_targets(lambda s: jnp.where(s == 0, factor[0, :, 0], factor[0, :, 1]))
+
+    def factor_of(s):
+        return jnp.where(s == 0, factor[0, :, 0], factor[0, :, 1])
+
+    factors = to_targets(factor_of(own_slot), factor_of)
 
     incoming = owned_gradients(partials[0], owner, slot, d)
 
@@ -418,7 +432,7 @@
             axis=0,
         )
 
-    pieces = to_targets(block_of)
+    pieces = to_targets(incoming[0], block_of)
     chosen = jnp.sum(jnp.where(mine[:, :, None], rowblock[None], 0), axis=1)
     sent = update(chosen, incoming, halves, moment1[0], moment2[0], master[0])
     received = lax.all_to_all(sent, "dp", split_axis=0, concat_axis=0, tiled=True)

time: 246 us -> 247 us (level)
    all_to_all x4, waiting for transfers between devices: 19.8 us -> 23.2 us  [exchange(): return lax.all_to_all(v, 'dp', 0, 0, axis_index_groups=lines, tiled=True)]
    ppermute x2 -> x4, starting transfers between devices: 3.57 us -> 6.4 us  [the longest x1 3.49 us: owned_gradients(): down_late = lax.ppermute(down[cut:] + far_down, 'dp', along(-1))]
    ppermute x2 -> x4, waiting for transfers between devices: 12.8 us -> 12.1 us  [the longest x1 5.86 us: owned_gradients(): up_late = lax.ppermute(up[cut:], 'dp', along(1))]
  transfers between devices with their start and end apart: 26 -> 28, of which waited for: 13 -> 14; matrix products, arithmetic and copies ran while one was open for 5% -> 5% of each run, Pallas kernels for 20% -> 20%
where the time goes in v7:
time: 247 us
  waiting for transfers between devices  101 us (41%)
  starting transfers between devices  70.4 us (29%)
  Pallas kernels  50.1 us (20%)
  local copies, waits for them, and re-layouts  11.2 us (5%)
  other arithmetic  11.1 us (4%)
    ppermute x12, waiting for transfers between devices, move(): return lax.ppermute(v, ('dp', 'mp'), ring(shift, parity))  57.7 us
    pallas_call x1, Pallas kernels, refresh(): pl.pallas_call(refresh_kernel, out_shape=[jax.ShapeDtypeStruct(factors[0]...  29.6 us
    ppermute x12, starting transfers between devices, move(): return lax.ppermute(v, ('dp', 'mp'), ring(shift, parity))  24.3 us
    all_to_all x4, starting transfers between devices, exchange(): return lax.all_to_all(v, 'dp', 0, 0, axis_index_groups=lines, tiled=True)  23.6 us
    all_to_all x4, waiting for transfers between devices, exchange(): return lax.all_to_all(v, 'dp', 0, 0, axis_index_groups=lines, tiled=True)  23.2 us
    pallas_call x1, Pallas kernels, update(): pl.pallas_call(update_kernel, out_shape=jax.ShapeDtypeStruct((groups, pad...  14.1 us
    all_to_all x1, starting transfers between devices, body(): lax.all_to_all(sent, 'dp', split_axis=0, concat_axis=0, tiled=True)  8.46 us
    pallas_call x1, Pallas kernels, prepare(): pl.pallas_call(prepare_kernel, out_shape=[half] * 4, in_specs=[pl.BlockSp...  6.41 us
  transfers between devices with their start and end apart: 28, of which 14 were waited for; matrix products, arithmetic and copies ran while one was open for 5% of the time, Pallas kernels for 20%

profile of v7, /device:TPU:1, one launch (start us, length us, event | category | flops | bytes accessed | tf_op | source)
XLA Modules:
  0.0 246.5 jit_solution(2444294081608788651)
XLA Ops:
  0.6 1.6 bitcast_convert_fusion
  2.3 3.3 %collective-permute-start = (f32[4,8,80,256]{3,2,1,0:T(8,128)S(1)}, f32[4,8,80,256]{3,2,1,0:T(8,128)}, u32[]{:S(2)}, u32[]{:S(2)}) collective-permute-start(f32[4,8,80,256]{3,2,1,0:T(8,128)S(1)} %bitcast_convert_fusion), channel_id=1, source_target_pairs={{0,4},{4,0},{8,12},{12,8},{16,20},{20,16},{24,28},{28,24},{32,36},... | collective-permute-start | bytes 7864328 | tf_op jit(solution)/shard_map/ppermute | solution.py:338
  5.6 4.7 %collective-permute-done = f32[4,8,80,256]{3,2,1,0:T(8,128)} collective-permute-done((f32[4,8,80,256]{3,2,1,0:T(8,128)S(1)}, f32[4,8,80,256]{3,2,1,0:T(8,128)}, u32[]{:S(2)}, u32[]{:S(2)}) %collective-permute-start) | collective-permute-done | bytes 2621472 | tf_op jit(solution)/shard_map/ppermute | solution.py:338
  10.2 2.5 %convert_add_fusion = f32[4,8,80,256]{3,2,1,0:T(8,128)S(1)} fusion(f32[4,8,80,256]{3,2,1,0:T(8,128)} %collective-permute-done, bf16[4,2,8,80,256]{4,3,2,1,0:T(8,128)(2,1)} %bitcast.86, s32[]{:T(128)S(6)} %select_n.184), kind=kLoop, calls=%fused_computation.2 | loop fusion | flops 1310720 | bytes 6553604 | tf_op jit(solution)/shard_map/add | solution.py:339
  12.7 0.7 copy_bitcast_fusion.2
  13.5 6.5 %all-to-all-start.2 = ((f32[8,32,256]{2,1,0:T(8,128)}), f32[8,32,256]{2,1,0:T(8,128)S(1)}, u32[]{:S(2)}, u32[]{:S(2)}) async-start(f32[8,32,256]{2,1,0:T(8,128)} %copy_bitcast_fusion.2), calls=%async_computation.2 | async-start | bytes 524288 | tf_op jit(solution)/shard_map/all_to_all | solution.py:318
  19.9 0.2 dynamic-slice_bitcast_fusion.3
  20.2 2.6 %collective-permute-start.5 = (f32[288,256]{1,0:T(8,128)S(1)}, f32[288,256]{1,0:T(8,128)S(1)}, u32[]{:S(2)}, u32[]{:S(2)}) collective-permute-start(f32[288,256]{1,0:T(8,128)S(1)} %bitcast.96), channel_id=1, source_target_pairs={{0,192},{4,196},{8,200},{12,204},{16,208},{20,212},{24,216},{28,22... | collective-permute-start | bytes 884744 | tf_op jit(solution)/shard_map/ppermute | solution.py:348
  22.9 0.3 collective-permute-start.4
  23.2 2.6 %collective-permute-start.3 = (f32[288,256]{1,0:T(8,128)S(1)}, f32[288,256]{1,0:T(8,128)S(1)}, u32[]{:S(2)}, u32[]{:S(2)}) collective-permute-start(f32[288,256]{1,0:T(8,128)S(1)} %bitcast.93), channel_id=1, source_target_pairs={{0,192},{4,196},{8,200},{12,204},{16,208},{20,212},{24,216},{28,22... | collective-permute-start | bytes 884744 | tf_op jit(solution)/shard_map/ppermute | solution.py:350
  25.8 2.7 %collective-permute-done.5 = f32[288,256]{1,0:T(8,128)S(1)} collective-permute-done((f32[288,256]{1,0:T(8,128)S(1)}, f32[288,256]{1,0:T(8,128)S(1)}, u32[]{:S(2)}, u32[]{:S(2)}) %collective-permute-start.5) | collective-permute-done | bytes 294944 | tf_op jit(solution)/shard_map/ppermute | solution.py:348
  28.5 3.5 %collective-permute-start.6 = (f32[288,256]{1,0:T(8,128)S(1)}, f32[288,256]{1,0:T(8,128)S(1)}, u32[]{:S(2)}, u32[]{:S(2)}) collective-permute-start(f32[288,256]{1,0:T(8,128)S(1)} %bitcast_add_fusion), channel_id=1, source_target_pairs={{0,192},{4,196},{8,200},{12,204},{16,208},{20,212},{24,216},{28,22... | collective-permute-start | bytes 884744 | tf_op jit(solution)/shard_map/ppermute | solution.py:354
  32.2 5.9 %collective-permute-done.4 = f32[288,256]{1,0:T(8,128)S(1)} collective-permute-done((f32[288,256]{1,0:T(8,128)S(1)}, f32[288,256]{1,0:T(8,128)S(1)}, u32[]{:S(2)}, u32[]{:S(2)}) %collective-permute-start.4) | collective-permute-done | bytes 294944 | tf_op jit(solution)/shard_map/ppermute | solution.py:349
  38.0 3.1 %collective-permute-done.6 = f32[288,256]{1,0:T(8,128)S(1)} collective-permute-done((f32[288,256]{1,0:T(8,128)S(1)}, f32[288,256]{1,0:T(8,128)S(1)}, u32[]{:S(2)}, u32[]{:S(2)}) %collective-permute-start.6) | collective-permute-done | bytes 294944 | tf_op jit(solution)/shard_map/ppermute | solution.py:354
  41.2 3.2 %collective-permute-done.2 = f32[288,256]{1,0:T(8,128)S(1)} collective-permute-done((f32[288,256]{1,0:T(8,128)S(1)}, f32[288,256]{1,0:T(8,128)S(1)}, u32[]{:S(2)}, u32[]{:S(2)}) %collective-permute-start.2) | collective-permute-done | bytes 294944 | tf_op jit(solution)/shard_map/ppermute | solution.py:353
  44.4 0.9 pad_maximum_fusion.2
  45.3 6.4 %all-to-all-start = ((f32[8,72,256]{2,1,0:T(8,128)}), f32[8,72,256]{2,1,0:T(8,128)S(1)}, u32[]{:S(2)}, u32[]{:S(2)}) async-start(f32[8,72,256]{2,1,0:T(8,128)} %bitcast.15), calls=%async_computation | async-start | bytes 1179648 | tf_op jit(solution)/shard_map/all_to_all | solution.py:318
  52.6 0.3 collective-permute-start.8
  52.9 0.6 collective-permute-start.9
  53.5 0.6 collective-permute-start.7
  54.1 14.5 %all-to-all-done = f32[8,72,256]{2,1,0:T(8,128)S(1)} async-done(((f32[8,72,256]{2,1,0:T(8,128)}), f32[8,72,256]{2,1,0:T(8,128)S(1)}, u32[]{:S(2)}, u32[]{:S(2)}) %all-to-all-start) | async-done | bytes 589856 | tf_op jit(solution)/shard_map/all_to_all | solution.py:318
  68.7 0.9 broadcast_in_dim.79
  69.5 6.3 %all-to-all-start.1 = ((f32[8,72,256]{2,1,0:T(8,128)}), f32[8,72,256]{2,1,0:T(8,128)S(1)}, u32[]{:S(2)}, u32[]{:S(2)}) async-start(f32[8,72,256]{2,1,0:T(8,128)} %broadcast_in_dim.79), calls=%async_computation.1 | async-start | bytes 1179648 | tf_op jit(solution)/shard_map/all_to_all | solution.py:318
  76.1 1.1 collective-permute-done.10
  77.2 8.7 %all-to-all-done.1 = f32[8,72,256]{2,1,0:T(8,128)S(1)} async-done(((f32[8,72,256]{2,1,0:T(8,128)}), f32[8,72,256]{2,1,0:T(8,128)S(1)}, u32[]{:S(2)}, u32[]{:S(2)}) %all-to-all-start.1) | async-done | bytes 589856 | tf_op jit(solution)/shard_map/all_to_all | solution.py:318
  86.0 1.7 gather_fusion
  87.7 4.4 %all-to-all-start.3 = ((f32[8,2,80,256]{3,2,1,0:T(8,128)}), f32[8,2,80,256]{3,2,1,0:T(8,128)}, u32[]{:S(2)}, u32[]{:S(2)}) async-start(f32[8,2,80,256]{3,2,1,0:T(8,128)} %bitcast.23), calls=%async_computation.3 | async-start | bytes 2621440 | tf_op jit(solution)/shard_map/all_to_all | solution.py:318
  92.1 0.6 fusion.6
  92.9 2.8 %collective-permute-start.11 = (f32[160,1280]{1,0:T(8,128)S(1)}, f32[160,1280]{1,0:T(8,128)S(1)}, u32[]{:S(2)}, u32[]{:S(2)}) collective-permute-start(f32[160,1280]{1,0:T(8,128)S(1)} %pad_maximum_fusion.b0), channel_id=1, source_target_pairs={{0,3},{1,0},{2,1},{3,2},{4,7},{5,4},{6,5},{7,6},{8,11},{9,8},{10,9... | collective-permute-start | bytes 2457608 | tf_op jit(solution)/shard_map/ppermute | solution.py:400
  95.8 0.5 collective-permute-start.12
  96.2 0.6 collective-permute-start.13
  96.8 0.6 fusion.5
  97.4 1.1 select_bitcast_fusion.2
  98.6 4.8 %collective-permute-start.17 = (f32[160,640]{1,0:T(8,128)}, f32[160,640]{1,0:T(8,128)}, u32[]{:S(2)}, u32[]{:S(2)}) collective-permute-start(f32[160,640]{1,0:T(8,128)} %get-tuple-element.37), channel_id=1, source_target_pairs={{1,0},{3,2},{4,7},{6,5},{9,8},{11,10},{12,15},{14,13},{17,16},{19,... | collective-permute-start | bytes 1228808 | tf_op jit(solution)/shard_map/ppermute | solution.py:400
  103.4 0.6 fusion.11
  105.2 0.7 pad_add_fusion.at
  105.9 0.6 select_reduce_fusion.1.chosen
  106.5 6.9 %collective-permute-done.11.b1 = f32[160,1280]{1,0:T(8,128)S(1)} collective-permute-done((f32[160,1280]{1,0:T(8,128)S(1)}, f32[160,1280]{1,0:T(8,128)S(1)}, u32[]{:S(2)}, u32[]{:S(2)}) %collective-permute-start.11) | collective-permute-done | bytes 819232 | tf_op jit(solution)/shard_map/ppermute | solution.py:400
  113.4 2.4 collective-permute-done.12.b2
  115.9 0.9 copy-done.5
  116.8 18.3 %collective-permute-done.13.b3 = f32[160,1280]{1,0:T(8,128)} collective-permute-done((f32[160,1280]{1,0:T(8,128)S(1)}, f32[160,1280]{1,0:T(8,128)}, u32[]{:S(2)}, u32[]{:S(2)}) %collective-permute-start.13) | collective-permute-done | bytes 819232 | tf_op jit(solution)/shard_map/ppermute | solution.py:400
  135.1 6.4 %prepare.1 = (bf16[2,640,640]{2,1,0:T(8,128)(2,1)}, bf16[2,640,640]{2,1,0:T(8,128)(2,1)}, bf16[2,640,640]{2,1,0:T(8,128)(2,1)}, bf16[2,640,640]{2,1,0:T(8,128)(2,1)}) custom-call(s32[3]{0:T(128)} %pad_add_fusion.at, f32[160,1280]{1,0:T(8,128)} %copy-done.1, f32[160,1280]{1,0:T(8,128)} %copy-done.4, f32[160,1280]{1,0:T(8,128)} %copy-done.5, ...), custom_call_target="tpu_custom_call" | custom-call | flops 3276800 | bytes 9830400 | tf_op jit(solution)/shard_map/prepare/pallas_call | solution.py:83
  141.5 14.1 %update.1 = f32[64,24,256]{2,1,0:T(8,128)} custom-call(s32[2,64]{1,0:T(2,128)} %select_reduce_fusion.1.chosen, f32[8,2,80,256]{3,2,1,0:T(8,128)} %all-to-all-done.3.refs_0_.came, bf16[2,640,640]{2,1,0:T(8,128)(2,1)} %get-tuple-element.10.refs_1_.b_hi, bf16[2,640,640]{2,1,0:T(8,128)(2,1)} %get-tuple-element.11.refs_2_.b_lo, ...), custom_call_target="tpu_custom_call" | custom-call | flops 2516582400 | bytes 5898240 | tf_op jit(solution)/shard_map/update/pallas_call | solution.py:152
  155.6 8.5 %all-to-all-start.4 = ((f32[64,24,256]{2,1,0:T(8,128)}), f32[64,24,256]{2,1,0:T(8,128)S(1)}, u32[]{:S(2)}, u32[]{:S(2)}) async-start(f32[64,24,256]{2,1,0:T(8,128)} %update.1), calls=%async_computation.4 | async-start | bytes 3145728 | tf_op jit(solution)/shard_map/all_to_all | solution.py:438
  164.1 1.4 slice_select_fusion
  165.5 4.4 %collective-permute-start.14 = (f32[640,256]{1,0:T(8,128)S(1)}, f32[640,256]{1,0:T(8,128)S(1)}, u32[]{:S(2)}, u32[]{:S(2)}) collective-permute-start(f32[640,256]{1,0:T(8,128)S(1)} %bitcast.91), channel_id=1, source_target_pairs={{1,0},{3,2},{4,7},{6,5},{9,8},{11,10},{12,15},{14,13},{17,16},{19,... | collective-permute-start | bytes 1966088 | tf_op jit(solution)/shard_map/ppermute | solution.py:400
  169.9 0.7 collective-permute-start.15
  170.6 3.1 %collective-permute-start.16 = (f32[640,256]{1,0:T(8,128)S(1)}, f32[640,256]{1,0:T(8,128)S(1)}, u32[]{:S(2)}, u32[]{:S(2)}) collective-permute-start(f32[640,256]{1,0:T(8,128)S(1)} %bitcast.90), channel_id=1, source_target_pairs={{1,2},{3,0},{4,5},{6,7},{9,10},{11,8},{12,13},{14,15},{17,18},{19,... | collective-permute-start | bytes 1966088 | tf_op jit(solution)/shard_map/ppermute | solution.py:400
  173.7 0.7 collective-permute-start.18
  174.4 2.7 %collective-permute-start.19 = (f32[160,640]{1,0:T(8,128)S(1)}, f32[160,640]{1,0:T(8,128)S(1)}, u32[]{:S(2)}, u32[]{:S(2)}) collective-permute-start(f32[160,640]{1,0:T(8,128)S(1)} %copy-done.6), channel_id=1, source_target_pairs={{1,2},{3,0},{4,5},{6,7},{9,10},{11,8},{12,13},{14,15},{17,18},{19,... | collective-permute-start | bytes 1228808 | tf_op jit(solution)/shard_map/ppermute | solution.py:400
  177.2 16.2 %collective-permute-done.19.f3 = f32[160,640]{1,0:T(8,128)S(1)} collective-permute-done((f32[160,640]{1,0:T(8,128)S(1)}, f32[160,640]{1,0:T(8,128)S(1)}, u32[]{:S(2)}, u32[]{:S(2)}) %collective-permute-start.19) | collective-permute-done | bytes 409632 | tf_op jit(solution)/shard_map/ppermute | solution.py:400
  193.5 0.7 copy-done.13
  194.2 0.2 copy-done.9
  194.6 0.2 copy-done.11
  194.8 29.6 %refresh.1 = (f32[160,640]{1,0:T(8,128)S(1)}, f32[160,640]{1,0:T(8,128)S(1)}, f32[160,640]{1,0:T(8,128)S(1)}, f32[160,640]{1,0:T(8,128)S(1)}) custom-call(s32[3]{0:T(128)S(1)} %copy-done, f32[8,2,80,256]{3,2,1,0:T(8,128)} %all-to-all-done.3.refs_0_.came, f32[640,256]{1,0:T(8,128)} %copy-done.9, f32[640,256]{1,0:T(8,128)} %copy-done.10, ...), custom_call_target="tpu_custom_call" | custom-call | flops 15728640000 | bytes 6553600 | tf_op jit(solution)/shard_map/refresh/pallas_call | solution.py:275
  224.5 1.3 collective-permute-start.20
  225.8 1.4 collective-permute-start.21
  227.2 1.3 collective-permute-start.22
  228.6 6.2 %collective-permute-done.20 = f32[160,640]{1,0:T(8,128)} collective-permute-done((f32[160,640]{1,0:T(8,128)S(1)}, f32[160,640]{1,0:T(8,128)}, u32[]{:S(2)}, u32[]{:S(2)}) %collective-permute-start.20) | collective-permute-done | bytes 409632 | tf_op jit(solution)/shard_map/ppermute | solution.py:400
  234.7 7.6 %collective-permute-done.22 = f32[160,640]{1,0:T(8,128)} collective-permute-done((f32[160,640]{1,0:T(8,128)S(1)}, f32[160,640]{1,0:T(8,128)}, u32[]{:S(2)}, u32[]{:S(2)}) %collective-permute-start.22) | collective-permute-done | bytes 409632 | tf_op jit(solution)/shard_map/ppermute | solution.py:400
  242.4 1.2 select_bitcast_fusion.1
  243.6 1.5 copy.46
  245.2 0.6 gather_fusion.1
  245.8 0.7 copy.45
  (72 shorter events, 2.3 us)
Async XLA Ops:
  2.3 8.0 %collective-permute-start = (f32[4,8,80,256]{3,2,1,0:T(8,128)S(1)}, f32[4,8,80,256]{3,2,1,0:T(8,128)}, u32[]{:S(2)}, u32[]{:S(2)}) collective-permute-start(f32[4,8,80,256]{3,2,1,0:T(8,128)S(1)} %bitcast_convert_fusion), channel_id=1, source_target_pairs={{0,4},{4,0},{8,12},{12,8},{16,20},{20,16},{24,28},{28,24},{32,36},... | collective-permute-start | bytes 7864328 | tf_op jit(solution)/shard_map/ppermute | solution.py:338
  13.5 31.8 %all-to-all-start.2 = ((f32[8,32,256]{2,1,0:T(8,128)}), f32[8,32,256]{2,1,0:T(8,128)S(1)}, u32[]{:S(2)}, u32[]{:S(2)}) async-start(f32[8,32,256]{2,1,0:T(8,128)} %copy_bitcast_fusion.2), calls=%async_computation.2 | async-start | bytes 524288 | tf_op jit(solution)/shard_map/all_to_all | solution.py:318
  20.2 8.3 %collective-permute-start.5 = (f32[288,256]{1,0:T(8,128)S(1)}, f32[288,256]{1,0:T(8,128)S(1)}, u32[]{:S(2)}, u32[]{:S(2)}) collective-permute-start(f32[288,256]{1,0:T(8,128)S(1)} %bitcast.96), channel_id=1, source_target_pairs={{0,192},{4,196},{8,200},{12,204},{16,208},{20,212},{24,216},{28,22... | collective-permute-start | bytes 884744 | tf_op jit(solution)/shard_map/ppermute | solution.py:348
  22.8 9.2 %collective-permute-start.1 = (f32[288,256]{1,0:T(8,128)S(1)}, f32[288,256]{1,0:T(8,128)S(1)}, u32[]{:S(2)}, u32[]{:S(2)}) collective-permute-start(f32[288,256]{1,0:T(8,128)S(1)} %bitcast.94), channel_id=1, source_target_pairs={{0,64},{4,68},{8,72},{12,76},{16,80},{20,84},{24,88},{28,92},{32,9... | collective-permute-start | bytes 884744 | tf_op jit(solution)/shard_map/ppermute | solution.py:347
  22.9 15.1 %collective-permute-start.4 = (f32[288,256]{1,0:T(8,128)S(1)}, f32[288,256]{1,0:T(8,128)S(1)}, u32[]{:S(2)}, u32[]{:S(2)}) collective-permute-start(f32[288,256]{1,0:T(8,128)S(1)} %bitcast.95), channel_id=1, source_target_pairs={{0,64},{4,68},{8,72},{12,76},{16,80},{20,84},{24,88},{28,92},{32,9... | collective-permute-start | bytes 884744 | tf_op jit(solution)/shard_map/ppermute | solution.py:349
  23.2 18.0 %collective-permute-start.3 = (f32[288,256]{1,0:T(8,128)S(1)}, f32[288,256]{1,0:T(8,128)S(1)}, u32[]{:S(2)}, u32[]{:S(2)}) collective-permute-start(f32[288,256]{1,0:T(8,128)S(1)} %bitcast.93), channel_id=1, source_target_pairs={{0,192},{4,196},{8,200},{12,204},{16,208},{20,212},{24,216},{28,22... | collective-permute-start | bytes 884744 | tf_op jit(solution)/shard_map/ppermute | solution.py:350
  28.5 12.6 %collective-permute-start.6 = (f32[288,256]{1,0:T(8,128)S(1)}, f32[288,256]{1,0:T(8,128)S(1)}, u32[]{:S(2)}, u32[]{:S(2)}) collective-permute-start(f32[288,256]{1,0:T(8,128)S(1)} %bitcast_add_fusion), channel_id=1, source_target_pairs={{0,192},{4,196},{8,200},{12,204},{16,208},{20,212},{24,216},{28,22... | collective-permute-start | bytes 884744 | tf_op jit(solution)/shard_map/ppermute | solution.py:354
  32.0 12.3 %collective-permute-start.2 = (f32[288,256]{1,0:T(8,128)S(1)}, f32[288,256]{1,0:T(8,128)S(1)}, u32[]{:S(2)}, u32[]{:S(2)}) collective-permute-start(f32[288,256]{1,0:T(8,128)S(1)} %bitcast_add_fusion.2), channel_id=1, source_target_pairs={{0,64},{4,68},{8,72},{12,76},{16,80},{20,84},{24,88},{28,92},{32,9... | collective-permute-start | bytes 884744 | tf_op jit(solution)/shard_map/ppermute | solution.py:353
  44.4 7.3 %copy-start.8 = (s32[8]{0:T(128)S(1)}, s32[8]{0:T(128)}, u32[]{:S(2)}) copy-start(s32[8]{0:T(128)} %param.9) | copy-start | bytes 100
  45.3 23.3 %all-to-all-start = ((f32[8,72,256]{2,1,0:T(8,128)}), f32[8,72,256]{2,1,0:T(8,128)S(1)}, u32[]{:S(2)}, u32[]{:S(2)}) async-start(f32[8,72,256]{2,1,0:T(8,128)} %bitcast.15), calls=%async_computation | async-start | bytes 1179648 | tf_op jit(solution)/shard_map/all_to_all | solution.py:318
  52.6 23.3 %collective-permute-start.8 = (f32[32,256]{1,0:T(8,128)S(1)}, f32[32,256]{1,0:T(8,128)S(1)}, u32[]{:S(2)}, u32[]{:S(2)}) collective-permute-start(f32[32,256]{1,0:T(8,128)S(1)} %reduce_sum.48), channel_id=1, source_target_pairs={{0,192},{4,196},{8,200},{12,204},{16,208},{20,212},{24,216},{28,22... | collective-permute-start | bytes 98312 | tf_op jit(solution)/shard_map/ppermute | solution.py:362
  52.9 23.0 %collective-permute-start.9 = (f32[32,256]{1,0:T(8,128)S(1)}, f32[32,256]{1,0:T(8,128)S(1)}, u32[]{:S(2)}, u32[]{:S(2)}) collective-permute-start(f32[32,256]{1,0:T(8,128)S(1)} %reduce_sum.48), channel_id=1, source_target_pairs={{0,128},{4,132},{8,136},{12,140},{16,144},{20,148},{24,152},{28,15... | collective-permute-start | bytes 98312 | tf_op jit(solution)/shard_map/ppermute | solution.py:362
  53.5 22.4 %collective-permute-start.7 = (f32[32,256]{1,0:T(8,128)S(1)}, f32[32,256]{1,0:T(8,128)S(1)}, u32[]{:S(2)}, u32[]{:S(2)}) collective-permute-start(f32[32,256]{1,0:T(8,128)S(1)} %reduce_sum.48), channel_id=1, source_target_pairs={{0,64},{4,68},{8,72},{12,76},{16,80},{20,84},{24,88},{28,92},{32,9... | collective-permute-start | bytes 98312 | tf_op jit(solution)/shard_map/ppermute | solution.py:361
  69.5 16.4 %all-to-all-start.1 = ((f32[8,72,256]{2,1,0:T(8,128)}), f32[8,72,256]{2,1,0:T(8,128)S(1)}, u32[]{:S(2)}, u32[]{:S(2)}) async-start(f32[8,72,256]{2,1,0:T(8,128)} %broadcast_in_dim.79), calls=%async_computation.1 | async-start | bytes 1179648 | tf_op jit(solution)/shard_map/all_to_all | solution.py:318
  75.9 1.3 collective-permute-start.10
  87.7 4.4 %copy-start.2 = (f32[1,160,2,640]{3,2,1,0:T(2,128)S(1)}, f32[1,160,2,640]{3,2,1,0:T(2,128)}, u32[]{:S(2)}) copy-start(f32[1,160,2,640]{3,2,1,0:T(2,128)} %param.12) | copy-start | bytes 2457604
  87.7 53.8 %all-to-all-start.3 = ((f32[8,2,80,256]{3,2,1,0:T(8,128)}), f32[8,2,80,256]{3,2,1,0:T(8,128)}, u32[]{:S(2)}, u32[]{:S(2)}) async-start(f32[8,2,80,256]{3,2,1,0:T(8,128)} %bitcast.23), calls=%async_computation.3 | async-start | bytes 2621440 | tf_op jit(solution)/shard_map/all_to_all | solution.py:318
  92.8 4.0 %copy-start.3 = (f32[1,160,2,640]{3,2,1,0:T(2,128)S(1)}, f32[1,160,2,640]{3,2,1,0:T(2,128)}, u32[]{:S(2)}) copy-start(f32[1,160,2,640]{3,2,1,0:T(2,128)} %param.11) | copy-start | bytes 2457604
  92.9 5.6 %copy-start.1 = (f32[160,1280]{1,0:T(8,128)}, f32[160,1280]{1,0:T(8,128)S(1)}, u32[]{:S(2)}) copy-start(f32[160,1280]{1,0:T(8,128)S(1)} %pad_maximum_fusion.b0) | copy-start | bytes 2457604
  92.9 20.5 %collective-permute-start.11 = (f32[160,1280]{1,0:T(8,128)S(1)}, f32[160,1280]{1,0:T(8,128)S(1)}, u32[]{:S(2)}, u32[]{:S(2)}) collective-permute-start(f32[160,1280]{1,0:T(8,128)S(1)} %pad_maximum_fusion.b0), channel_id=1, source_target_pairs={{0,3},{1,0},{2,1},{3,2},{4,7},{5,4},{6,5},{7,6},{8,11},{9,8},{10,9... | collective-permute-start | bytes 2457608 | tf_op jit(solution)/shard_map/ppermute | solution.py:400
  95.8 20.1 %collective-permute-start.12 = (f32[160,1280]{1,0:T(8,128)S(1)}, f32[160,1280]{1,0:T(8,128)S(1)}, u32[]{:S(2)}, u32[]{:S(2)}) collective-permute-start(f32[160,1280]{1,0:T(8,128)S(1)} %pad_maximum_fusion.b0), channel_id=1, source_target_pairs={{0,2},{1,3},{2,0},{3,1},{4,6},{5,7},{6,4},{7,5},{8,10},{9,11},{10,... | collective-permute-start | bytes 2457608 | tf_op jit(solution)/shard_map/ppermute | solution.py:400
  96.2 38.9 %collective-permute-start.13 = (f32[160,1280]{1,0:T(8,128)S(1)}, f32[160,1280]{1,0:T(8,128)}, u32[]{:S(2)}, u32[]{:S(2)}) collective-permute-start(f32[160,1280]{1,0:T(8,128)S(1)} %pad_maximum_fusion.b0), channel_id=1, source_target_pairs={{0,1},{1,2},{2,3},{3,0},{4,5},{5,6},{6,7},{7,4},{8,9},{9,10},{10,1... | collective-permute-start | bytes 2457608 | tf_op jit(solution)/shard_map/ppermute | solution.py:400
  96.8 9.1 %copy-start.7 = (s32[8,64]{1,0:T(8,128)S(1)}, s32[8,64]{1,0:T(8,128)}, u32[]{:S(2)}) copy-start(s32[8,64]{1,0:T(8,128)} %param.10) | copy-start | bytes 6148
  98.6 75.9 %collective-permute-start.17 = (f32[160,640]{1,0:T(8,128)}, f32[160,640]{1,0:T(8,128)}, u32[]{:S(2)}, u32[]{:S(2)}) collective-permute-start(f32[160,640]{1,0:T(8,128)} %get-tuple-element.37), channel_id=1, source_target_pairs={{1,0},{3,2},{4,7},{6,5},{9,8},{11,10},{12,15},{14,13},{17,16},{19,... | collective-permute-start | bytes 1228808 | tf_op jit(solution)/shard_map/ppermute | solution.py:400
  113.4 21.6 %copy-start.4 = (f32[160,1280]{1,0:T(8,128)}, f32[160,1280]{1,0:T(8,128)S(1)}, u32[]{:S(2)}) copy-start(f32[160,1280]{1,0:T(8,128)S(1)} %collective-permute-done.11.b1) | copy-start | bytes 2457604
  115.9 0.9 copy-start.5
  155.6 89.6 %all-to-all-start.4 = ((f32[64,24,256]{2,1,0:T(8,128)}), f32[64,24,256]{2,1,0:T(8,128)S(1)}, u32[]{:S(2)}, u32[]{:S(2)}) async-start(f32[64,24,256]{2,1,0:T(8,128)} %update.1), calls=%async_computation.4 | async-start | bytes 3145728 | tf_op jit(solution)/shard_map/all_to_all | solution.py:438
  164.1 10.4 %copy-start.6 = (f32[160,640]{1,0:T(8,128)S(1)}, f32[160,640]{1,0:T(8,128)}, u32[]{:S(2)}) copy-start(f32[160,640]{1,0:T(8,128)} %get-tuple-element.36) | copy-start | bytes 1228804
  164.1 30.8 %copy-start = (s32[3]{0:T(128)S(1)}, s32[3]{0:T(128)}, u32[]{:S(2)}) copy-start(s32[3]{0:T(128)} %pad_add_fusion.at) | copy-start | bytes 40
  165.5 27.9 %collective-permute-start.14 = (f32[640,256]{1,0:T(8,128)S(1)}, f32[640,256]{1,0:T(8,128)S(1)}, u32[]{:S(2)}, u32[]{:S(2)}) collective-permute-start(f32[640,256]{1,0:T(8,128)S(1)} %bitcast.91), channel_id=1, source_target_pairs={{1,0},{3,2},{4,7},{6,5},{9,8},{11,10},{12,15},{14,13},{17,16},{19,... | collective-permute-start | bytes 1966088 | tf_op jit(solution)/shard_map/ppermute | solution.py:400
  169.9 23.5 %collective-permute-start.15 = (f32[640,256]{1,0:T(8,128)S(1)}, f32[640,256]{1,0:T(8,128)S(1)}, u32[]{:S(2)}, u32[]{:S(2)}) collective-permute-start(f32[640,256]{1,0:T(8,128)S(1)} %bitcast.92), channel_id=1, source_target_pairs={{0,2},{2,0},{5,7},{7,5},{8,10},{10,8},{13,15},{15,13},{16,18},{18,... | collective-permute-start | bytes 1966088 | tf_op jit(solution)/shard_map/ppermute | solution.py:400
  170.6 22.8 %collective-permute-start.16 = (f32[640,256]{1,0:T(8,128)S(1)}, f32[640,256]{1,0:T(8,128)S(1)}, u32[]{:S(2)}, u32[]{:S(2)}) collective-permute-start(f32[640,256]{1,0:T(8,128)S(1)} %bitcast.90), channel_id=1, source_target_pairs={{1,2},{3,0},{4,5},{6,7},{9,10},{11,8},{12,13},{14,15},{17,18},{19,... | collective-permute-start | bytes 1966088 | tf_op jit(solution)/shard_map/ppermute | solution.py:400
  173.7 3.5 %collective-permute-start.18 = (f32[160,640]{1,0:T(8,128)}, f32[160,640]{1,0:T(8,128)S(1)}, u32[]{:S(2)}, u32[]{:S(2)}) collective-permute-start(f32[160,640]{1,0:T(8,128)} %get-tuple-element.37), channel_id=1, source_target_pairs={{0,2},{2,0},{5,7},{7,5},{8,10},{10,8},{13,15},{15,13},{16,18},{18,... | collective-permute-start | bytes 1228808 | tf_op jit(solution)/shard_map/ppermute | solution.py:400
  174.4 19.0 %collective-permute-start.19 = (f32[160,640]{1,0:T(8,128)S(1)}, f32[160,640]{1,0:T(8,128)S(1)}, u32[]{:S(2)}, u32[]{:S(2)}) collective-permute-start(f32[160,640]{1,0:T(8,128)S(1)} %copy-done.6), channel_id=1, source_target_pairs={{1,2},{3,0},{4,5},{6,7},{9,10},{11,8},{12,13},{14,15},{17,18},{19,... | collective-permute-start | bytes 1228808 | tf_op jit(solution)/shard_map/ppermute | solution.py:400
  177.2 16.3 %copy-start.12 = (f32[160,640]{1,0:T(8,128)}, f32[160,640]{1,0:T(8,128)S(1)}, u32[]{:S(2)}) copy-start(f32[160,640]{1,0:T(8,128)S(1)} %collective-permute-done.18.f2) | copy-start | bytes 1228804
  193.4 0.7 copy-start.13
  193.4 1.0 copy-start.9
  193.4 1.2 copy-start.10
  193.5 1.4 copy-start.11
  224.5 10.3 %collective-permute-start.20 = (f32[160,640]{1,0:T(8,128)S(1)}, f32[160,640]{1,0:T(8,128)}, u32[]{:S(2)}, u32[]{:S(2)}) collective-permute-start(f32[160,640]{1,0:T(8,128)S(1)} %get-tuple-element.15), channel_id=1, source_target_pairs={{0,1},{2,3},{5,6},{7,4},{8,9},{10,11},{13,14},{15,12},{16,17},{18,... | collective-permute-start | bytes 1228808 | tf_op jit(solution)/shard_map/ppermute | solution.py:400
  225.8 9.0 %collective-permute-start.21 = (f32[160,640]{1,0:T(8,128)S(1)}, f32[160,640]{1,0:T(8,128)}, u32[]{:S(2)}, u32[]{:S(2)}) collective-permute-start(f32[160,640]{1,0:T(8,128)S(1)} %get-tuple-element.16), channel_id=1, source_target_pairs={{0,2},{2,0},{5,7},{7,5},{8,10},{10,8},{13,15},{15,13},{16,18},{18,... | collective-permute-start | bytes 1228808 | tf_op jit(solution)/shard_map/ppermute | solution.py:400
  227.2 15.1 %collective-permute-start.22 = (f32[160,640]{1,0:T(8,128)S(1)}, f32[160,640]{1,0:T(8,128)}, u32[]{:S(2)}, u32[]{:S(2)}) collective-permute-start(f32[160,640]{1,0:T(8,128)S(1)} %get-tuple-element.17), channel_id=1, source_target_pairs={{0,3},{2,1},{5,4},{7,6},{8,11},{10,9},{13,12},{15,14},{16,19},{18,... | collective-permute-start | bytes 1228808 | tf_op jit(solution)/shard_map/ppermute | solution.py:400

commit v8 on v7

--- a/solution.py
+++ b/solution.py
@@ -9,7 +9,7 @@
 NS_ITERS = 4
 SLOTS = 2
 BLOCK = 256
-FIRST = 72
+FIRST = 64
 VMEM = 63 << 20
 PARTS = (80,)
 NX, NZ, NC = 4, 8, 2
@@ -343,18 +343,17 @@
         return near[:, :FIRST].reshape(NZ * FIRST, cols)
 
     cut = NZ * FIRST // 2
-    far, up, down, home = towards(2), towards(1), towards(3), towards(0)
+    far = towards(2)
     far_up = lax.ppermute(far[:cut], "dp", along(1))
     far_down = lax.ppermute(far[cut:], "dp", along(-1))
-    up_late = lax.ppermute(up[cut:], "dp", along(1))
-    down_early = lax.ppermute(down[:cut], "dp", along(-1))
     late = jnp.transpose(chip[:, :, FIRST:], (1, 0, 2, 3)).reshape(NZ, NX * rest, cols)
     late = exchange(late, along_z)
-    up_early = lax.ppermute(up[:cut] + far_up, "dp", along(1))
-    down_late = lax.ppermute(down[cut:] + far_down, "dp", along(-1))
-    over_x = jnp.concatenate(
-        [home[:cut] + up_early + down_early, home[cut:] + up_late + down_late], axis=0
-    )
+    up, down = towards(1), towards(3)
+    up = jnp.concatenate([up[:cut] + far_up, up[cut:]], axis=0)
+    down = jnp.concatenate([down[:cut], down[cut:] + far_down], axis=0)
+    from_up = lax.ppermute(up, "dp", along(1))
+    from_down = lax.ppermute(down, "dp", along(-1))
+    over_x = towards(0) + from_up + from_down
     over_z = jnp.sum(exchange(over_x.reshape(NZ, FIRST, cols), along_z), axis=0)
     mean = over_z * (1.0 / groups)
     late = jnp.sum(late, axis=0)

time: 247 us -> 245 us (level)
    all_to_all x4, waiting for transfers between devices: 23.2 us -> 19.8 us  [exchange(): return lax.all_to_all(v, 'dp', 0, 0, axis_index_groups=lines, tiled=True)]
    ppermute x4 -> x2, starting transfers between devices: 6.4 us -> 3.57 us  [the longest x1 3.49 us: owned_gradients(): from_down = lax.ppermute(down, 'dp', along(-1))]
    ppermute x4 -> x2, waiting for transfers between devices: 12.1 us -> 12.8 us  [the longest x1 9.54 us: owned_gradients(): from_down = lax.ppermute(down, 'dp', along(-1))]
  transfers between devices with their start and end apart: 28 -> 26, of which waited for: 14 -> 13; matrix products, arithmetic and copies ran while one was open for 5% -> 5% of each run, Pallas kernels for 20% -> 21%
where the time goes in v8:
time: 245 us; the launch traced here: 244 us
  waiting for transfers between devices  101 us (41%)
  starting transfers between devices  68.4 us (28%)
  Pallas kernels  50.1 us (20%)
  local copies, waits for them, and re-layouts  11.3 us (5%)
  other arithmetic  11.1 us (5%)
    ppermute x12, waiting for transfers between devices, move(): return lax.ppermute(v, ('dp', 'mp'), ring(shift, parity))  57.8 us
    pallas_call x1, Pallas kernels, refresh(): pl.pallas_call(refresh_kernel, out_shape=[jax.ShapeDtypeStruct(factors[0]...  29.6 us
    all_to_all x4, starting transfers between devices, exchange(): return lax.all_to_all(v, 'dp', 0, 0, axis_index_groups=lines, tiled=True)  24.5 us
    ppermute x12, starting transfers between devices, move(): return lax.ppermute(v, ('dp', 'mp'), ring(shift, parity))  24.1 us
    all_to_all x4, waiting for transfers between devices, exchange(): return lax.all_to_all(v, 'dp', 0, 0, axis_index_groups=lines, tiled=True)  19.8 us
    pallas_call x1, Pallas kernels, update(): pl.pallas_call(update_kernel, out_shape=jax.ShapeDtypeStruct((groups, pad...  14.1 us
    ppermute x1, waiting for transfers between devices, owned_gradients(): from_down = lax.ppermute(down, 'dp', along(-1))  9.54 us
    all_to_all x1, starting transfers between devices, body(): lax.all_to_all(sent, 'dp', split_axis=0, concat_axis=0, tiled=True)  8.46 us
  transfers between devices with their start and end apart: 26, of which 13 were waited for; matrix products, arithmetic and copies ran while one was open for 5% of the time, Pallas kernels for 21%

profile of v8, /device:TPU:1, one launch (start us, length us, event | category | flops | bytes accessed | tf_op | source)
XLA Modules:
  0.0 244.3 jit_solution(12230364205656316895)
XLA Ops:
  0.6 1.6 bitcast_convert_fusion
  2.3 3.3 %collective-permute-start = (f32[4,8,80,256]{3,2,1,0:T(8,128)S(1)}, f32[4,8,80,256]{3,2,1,0:T(8,128)}, u32[]{:S(2)}, u32[]{:S(2)}) collective-permute-start(f32[4,8,80,256]{3,2,1,0:T(8,128)S(1)} %bitcast_convert_fusion), channel_id=1, source_target_pairs={{0,4},{4,0},{8,12},{12,8},{16,20},{20,16},{24,28},{28,24},{32,36},... | collective-permute-start | bytes 7864328 | tf_op jit(solution)/shard_map/ppermute | solution.py:338
  5.6 4.7 %collective-permute-done = f32[4,8,80,256]{3,2,1,0:T(8,128)} collective-permute-done((f32[4,8,80,256]{3,2,1,0:T(8,128)S(1)}, f32[4,8,80,256]{3,2,1,0:T(8,128)}, u32[]{:S(2)}, u32[]{:S(2)}) %collective-permute-start) | collective-permute-done | bytes 2621472 | tf_op jit(solution)/shard_map/ppermute | solution.py:338
  10.2 2.5 %convert_add_fusion = f32[4,8,80,256]{3,2,1,0:T(8,128)S(1)} fusion(f32[4,8,80,256]{3,2,1,0:T(8,128)} %collective-permute-done, bf16[4,2,8,80,256]{4,3,2,1,0:T(8,128)(2,1)} %bitcast.77, s32[]{:T(128)S(6)} %select_n.184), kind=kLoop, calls=%fused_computation.2 | loop fusion | flops 1310720 | bytes 6553604 | tf_op jit(solution)/shard_map/add | solution.py:339
  12.8 0.8 copy.37
  13.6 6.5 %all-to-all-start.2 = ((f32[8,64,256]{2,1,0:T(8,128)}), f32[8,64,256]{2,1,0:T(8,128)S(1)}, u32[]{:S(2)}, u32[]{:S(2)}) async-start(f32[8,64,256]{2,1,0:T(8,128)} %bitcast.78), calls=%async_computation.2 | async-start | bytes 1048576 | tf_op jit(solution)/shard_map/all_to_all | solution.py:318
  20.1 0.2 dynamic-slice_bitcast_fusion.3
  20.3 2.6 %collective-permute-start.3 = (f32[256,256]{1,0:T(8,128)S(1)}, f32[256,256]{1,0:T(8,128)S(1)}, u32[]{:S(2)}, u32[]{:S(2)}) collective-permute-start(f32[256,256]{1,0:T(8,128)S(1)} %bitcast.91), channel_id=1, source_target_pairs={{0,192},{4,196},{8,200},{12,204},{16,208},{20,212},{24,216},{28,22... | collective-permute-start | bytes 786440 | tf_op jit(solution)/shard_map/ppermute | solution.py:348
  23.1 4.8 %collective-permute-done.3 = f32[256,256]{1,0:T(8,128)S(1)} collective-permute-done((f32[256,256]{1,0:T(8,128)S(1)}, f32[256,256]{1,0:T(8,128)S(1)}, u32[]{:S(2)}, u32[]{:S(2)}) %collective-permute-start.3) | collective-permute-done | bytes 262176 | tf_op jit(solution)/shard_map/ppermute | solution.py:348
  28.0 3.5 %collective-permute-start.4 = (f32[512,256]{1,0:T(8,128)S(1)}, f32[512,256]{1,0:T(8,128)S(1)}, u32[]{:S(2)}, u32[]{:S(2)}) collective-permute-start(f32[512,256]{1,0:T(8,128)S(1)} %pad_maximum_fusion.3), channel_id=1, source_target_pairs={{0,192},{4,196},{8,200},{12,204},{16,208},{20,212},{24,216},{28,22... | collective-permute-start | bytes 1572872 | tf_op jit(solution)/shard_map/ppermute | solution.py:355
  31.7 9.5 %collective-permute-done.4 = f32[512,256]{1,0:T(8,128)S(1)} collective-permute-done((f32[512,256]{1,0:T(8,128)S(1)}, f32[512,256]{1,0:T(8,128)S(1)}, u32[]{:S(2)}, u32[]{:S(2)}) %collective-permute-start.4) | collective-permute-done | bytes 524320 | tf_op jit(solution)/shard_map/ppermute | solution.py:355
  41.2 3.3 %collective-permute-done.2 = f32[512,256]{1,0:T(8,128)S(1)} collective-permute-done((f32[512,256]{1,0:T(8,128)S(1)}, f32[512,256]{1,0:T(8,128)S(1)}, u32[]{:S(2)}, u32[]{:S(2)}) %collective-permute-start.2) | collective-permute-done | bytes 524320 | tf_op jit(solution)/shard_map/ppermute | solution.py:354
  44.5 0.9 fusion
  45.4 6.1 %all-to-all-start = ((f32[8,64,256]{2,1,0:T(8,128)}), f32[8,64,256]{2,1,0:T(8,128)S(1)}, u32[]{:S(2)}, u32[]{:S(2)}) async-start(f32[8,64,256]{2,1,0:T(8,128)} %bitcast.14), calls=%async_computation | async-start | bytes 1048576 | tf_op jit(solution)/shard_map/all_to_all | solution.py:318
  51.5 0.2 convert_reduce_fusion
  52.5 0.2 collective-permute-start.6
  52.7 0.7 collective-permute-start.7
  53.4 0.6 collective-permute-start.5
  54.0 11.8 %all-to-all-done = f32[8,64,256]{2,1,0:T(8,128)S(1)} async-done(((f32[8,64,256]{2,1,0:T(8,128)}), f32[8,64,256]{2,1,0:T(8,128)S(1)}, u32[]{:S(2)}, u32[]{:S(2)}) %all-to-all-start) | async-done | bytes 524320 | tf_op jit(solution)/shard_map/all_to_all | solution.py:318
  65.9 0.8 broadcast_in_dim.79
  66.7 7.5 %all-to-all-start.1 = ((f32[8,64,256]{2,1,0:T(8,128)}), f32[8,64,256]{2,1,0:T(8,128)S(1)}, u32[]{:S(2)}, u32[]{:S(2)}) async-start(f32[8,64,256]{2,1,0:T(8,128)} %broadcast_in_dim.79), calls=%async_computation.1 | async-start | bytes 1048576 | tf_op jit(solution)/shard_map/all_to_all | solution.py:318
  74.3 0.2 collective-permute-start.8
  74.5 1.1 collective-permute-done.8
  75.7 8.0 %all-to-all-done.1 = f32[8,64,256]{2,1,0:T(8,128)S(1)} async-done(((f32[8,64,256]{2,1,0:T(8,128)}), f32[8,64,256]{2,1,0:T(8,128)S(1)}, u32[]{:S(2)}, u32[]{:S(2)}) %all-to-all-start.1) | async-done | bytes 524320 | tf_op jit(solution)/shard_map/all_to_all | solution.py:318
  83.7 1.7 gather_fusion
  85.4 4.4 %all-to-all-start.3 = ((f32[8,2,80,256]{3,2,1,0:T(8,128)}), f32[8,2,80,256]{3,2,1,0:T(8,128)}, u32[]{:S(2)}, u32[]{:S(2)}) async-start(f32[8,2,80,256]{3,2,1,0:T(8,128)} %bitcast.22), calls=%async_computation.3 | async-start | bytes 2621440 | tf_op jit(solution)/shard_map/all_to_all | solution.py:318
  89.8 0.6 fusion.5
  90.6 2.8 %collective-permute-start.9 = (f32[160,1280]{1,0:T(8,128)S(1)}, f32[160,1280]{1,0:T(8,128)S(1)}, u32[]{:S(2)}, u32[]{:S(2)}) collective-permute-start(f32[160,1280]{1,0:T(8,128)S(1)} %pad_maximum_fusion.b0), channel_id=1, source_target_pairs={{0,3},{1,0},{2,1},{3,2},{4,7},{5,4},{6,5},{7,6},{8,11},{9,8},{10,9... | collective-permute-start | bytes 2457608 | tf_op jit(solution)/shard_map/ppermute | solution.py:399
  93.5 0.4 collective-permute-start.10
  93.8 0.7 collective-permute-start.11
  94.5 0.6 fusion.4
  95.1 1.1 select_bitcast_fusion.2
  96.3 4.7 %collective-permute-start.15 = (f32[160,640]{1,0:T(8,128)}, f32[160,640]{1,0:T(8,128)}, u32[]{:S(2)}, u32[]{:S(2)}) collective-permute-start(f32[160,640]{1,0:T(8,128)} %get-tuple-element.37), channel_id=1, source_target_pairs={{1,0},{3,2},{4,7},{6,5},{9,8},{11,10},{12,15},{14,13},{17,16},{19,... | collective-permute-start | bytes 1228808 | tf_op jit(solution)/shard_map/ppermute | solution.py:399
  101.0 0.6 fusion.9
  102.8 0.6 pad_add_fusion.at
  103.4 0.6 select_reduce_fusion.1.chosen
  104.1 7.0 %collective-permute-done.9.b1 = f32[160,1280]{1,0:T(8,128)S(1)} collective-permute-done((f32[160,1280]{1,0:T(8,128)S(1)}, f32[160,1280]{1,0:T(8,128)S(1)}, u32[]{:S(2)}, u32[]{:S(2)}) %collective-permute-start.9) | collective-permute-done | bytes 819232 | tf_op jit(solution)/shard_map/ppermute | solution.py:399
  111.1 2.4 collective-permute-done.10.b2
  113.6 0.9 copy-done.5
  114.5 18.3 %collective-permute-done.11.b3 = f32[160,1280]{1,0:T(8,128)} collective-permute-done((f32[160,1280]{1,0:T(8,128)S(1)}, f32[160,1280]{1,0:T(8,128)}, u32[]{:S(2)}, u32[]{:S(2)}) %collective-permute-start.11) | collective-permute-done | bytes 819232 | tf_op jit(solution)/shard_map/ppermute | solution.py:399
  132.8 6.4 %prepare.1 = (bf16[2,640,640]{2,1,0:T(8,128)(2,1)}, bf16[2,640,640]{2,1,0:T(8,128)(2,1)}, bf16[2,640,640]{2,1,0:T(8,128)(2,1)}, bf16[2,640,640]{2,1,0:T(8,128)(2,1)}) custom-call(s32[3]{0:T(128)} %pad_add_fusion.at, f32[160,1280]{1,0:T(8,128)} %copy-done.1, f32[160,1280]{1,0:T(8,128)} %copy-done.4, f32[160,1280]{1,0:T(8,128)} %copy-done.5, ...), custom_call_target="tpu_custom_call" | custom-call | flops 3276800 | bytes 9830400 | tf_op jit(solution)/shard_map/prepare/pallas_call | solution.py:83
  139.2 14.1 %update.1 = f32[64,24,256]{2,1,0:T(8,128)} custom-call(s32[2,64]{1,0:T(2,128)} %select_reduce_fusion.1.chosen, f32[8,2,80,256]{3,2,1,0:T(8,128)} %all-to-all-done.3.refs_0_.came, bf16[2,640,640]{2,1,0:T(8,128)(2,1)} %get-tuple-element.10.refs_1_.b_hi, bf16[2,640,640]{2,1,0:T(8,128)(2,1)} %get-tuple-element.11.refs_2_.b_lo, ...), custom_call_target="tpu_custom_call" | custom-call | flops 2516582400 | bytes 5898240 | tf_op jit(solution)/shard_map/update/pallas_call | solution.py:152
  153.3 8.5 %all-to-all-start.4 = ((f32[64,24,256]{2,1,0:T(8,128)}), f32[64,24,256]{2,1,0:T(8,128)S(1)}, u32[]{:S(2)}, u32[]{:S(2)}) async-start(f32[64,24,256]{2,1,0:T(8,128)} %update.1), calls=%async_computation.4 | async-start | bytes 3145728 | tf_op jit(solution)/shard_map/all_to_all | solution.py:437
  161.8 1.4 slice_select_fusion
  163.2 4.4 %collective-permute-start.12 = (f32[640,256]{1,0:T(8,128)S(1)}, f32[640,256]{1,0:T(8,128)S(1)}, u32[]{:S(2)}, u32[]{:S(2)}) collective-permute-start(f32[640,256]{1,0:T(8,128)S(1)} %bitcast.85), channel_id=1, source_target_pairs={{1,0},{3,2},{4,7},{6,5},{9,8},{11,10},{12,15},{14,13},{17,16},{19,... | collective-permute-start | bytes 1966088 | tf_op jit(solution)/shard_map/ppermute | solution.py:399
  167.7 0.7 collective-permute-start.13
  168.4 3.1 %collective-permute-start.14 = (f32[640,256]{1,0:T(8,128)S(1)}, f32[640,256]{1,0:T(8,128)S(1)}, u32[]{:S(2)}, u32[]{:S(2)}) collective-permute-start(f32[640,256]{1,0:T(8,128)S(1)} %bitcast.84), channel_id=1, source_target_pairs={{1,2},{3,0},{4,5},{6,7},{9,10},{11,8},{12,13},{14,15},{17,18},{19,... | collective-permute-start | bytes 1966088 | tf_op jit(solution)/shard_map/ppermute | solution.py:399
  171.5 0.7 collective-permute-start.16
  172.2 2.7 %collective-permute-start.17 = (f32[160,640]{1,0:T(8,128)S(1)}, f32[160,640]{1,0:T(8,128)S(1)}, u32[]{:S(2)}, u32[]{:S(2)}) collective-permute-start(f32[160,640]{1,0:T(8,128)S(1)} %copy-done.6), channel_id=1, source_target_pairs={{1,2},{3,0},{4,5},{6,7},{9,10},{11,8},{12,13},{14,15},{17,18},{19,... | collective-permute-start | bytes 1228808 | tf_op jit(solution)/shard_map/ppermute | solution.py:399
  174.9 16.1 %collective-permute-done.17.f3 = f32[160,640]{1,0:T(8,128)S(1)} collective-permute-done((f32[160,640]{1,0:T(8,128)S(1)}, f32[160,640]{1,0:T(8,128)S(1)}, u32[]{:S(2)}, u32[]{:S(2)}) %collective-permute-start.17) | collective-permute-done | bytes 409632 | tf_op jit(solution)/shard_map/ppermute | solution.py:399
  191.1 0.7 copy-done.13
  191.8 0.2 copy-done.9
  192.0 0.2 copy-done.10
  192.2 0.3 copy-done.11
  192.5 29.6 %refresh.1 = (f32[160,640]{1,0:T(8,128)S(1)}, f32[160,640]{1,0:T(8,128)S(1)}, f32[160,640]{1,0:T(8,128)S(1)}, f32[160,640]{1,0:T(8,128)S(1)}) custom-call(s32[3]{0:T(128)S(1)} %copy-done, f32[8,2,80,256]{3,2,1,0:T(8,128)} %all-to-all-done.3.refs_0_.came, f32[640,256]{1,0:T(8,128)} %copy-done.9, f32[640,256]{1,0:T(8,128)} %copy-done.10, ...), custom_call_target="tpu_custom_call" | custom-call | flops 15728640000 | bytes 6553600 | tf_op jit(solution)/shard_map/refresh/pallas_call | solution.py:275
  222.1 1.3 collective-permute-start.18
  223.4 1.4 collective-permute-start.19
  224.8 1.3 collective-permute-start.20
  226.2 6.3 %collective-permute-done.18 = f32[160,640]{1,0:T(8,128)} collective-permute-done((f32[160,640]{1,0:T(8,128)S(1)}, f32[160,640]{1,0:T(8,128)}, u32[]{:S(2)}, u32[]{:S(2)}) %collective-permute-start.18) | collective-permute-done | bytes 409632 | tf_op jit(solution)/shard_map/ppermute | solution.py:399
  232.5 7.6 %collective-permute-done.20 = f32[160,640]{1,0:T(8,128)} collective-permute-done((f32[160,640]{1,0:T(8,128)S(1)}, f32[160,640]{1,0:T(8,128)}, u32[]{:S(2)}, u32[]{:S(2)}) %collective-permute-start.20) | collective-permute-done | bytes 409632 | tf_op jit(solution)/shard_map/ppermute | solution.py:399
  240.1 1.2 select_bitcast_fusion.1
  241.4 1.5 copy.45
  242.9 0.6 gather_fusion.1
  243.5 0.7 copy.44
  (69 shorter events, 1.7 us)
Async XLA Ops:
  2.3 8.0 %collective-permute-start = (f32[4,8,80,256]{3,2,1,0:T(8,128)S(1)}, f32[4,8,80,256]{3,2,1,0:T(8,128)}, u32[]{:S(2)}, u32[]{:S(2)}) collective-permute-start(f32[4,8,80,256]{3,2,1,0:T(8,128)S(1)} %bitcast_convert_fusion), channel_id=1, source_target_pairs={{0,4},{4,0},{8,12},{12,8},{16,20},{20,16},{24,28},{28,24},{32,36},... | collective-permute-start | bytes 7864328 | tf_op jit(solution)/shard_map/ppermute | solution.py:338
  13.6 31.8 %all-to-all-start.2 = ((f32[8,64,256]{2,1,0:T(8,128)}), f32[8,64,256]{2,1,0:T(8,128)S(1)}, u32[]{:S(2)}, u32[]{:S(2)}) async-start(f32[8,64,256]{2,1,0:T(8,128)} %bitcast.78), calls=%async_computation.2 | async-start | bytes 1048576 | tf_op jit(solution)/shard_map/all_to_all | solution.py:318
  20.3 7.6 %collective-permute-start.3 = (f32[256,256]{1,0:T(8,128)S(1)}, f32[256,256]{1,0:T(8,128)S(1)}, u32[]{:S(2)}, u32[]{:S(2)}) collective-permute-start(f32[256,256]{1,0:T(8,128)S(1)} %bitcast.91), channel_id=1, source_target_pairs={{0,192},{4,196},{8,200},{12,204},{16,208},{20,212},{24,216},{28,22... | collective-permute-start | bytes 786440 | tf_op jit(solution)/shard_map/ppermute | solution.py:348
  22.9 8.5 %collective-permute-start.1 = (f32[256,256]{1,0:T(8,128)S(1)}, f32[256,256]{1,0:T(8,128)S(1)}, u32[]{:S(2)}, u32[]{:S(2)}) collective-permute-start(f32[256,256]{1,0:T(8,128)S(1)} %bitcast.90), channel_id=1, source_target_pairs={{0,64},{4,68},{8,72},{12,76},{16,80},{20,84},{24,88},{28,92},{32,9... | collective-permute-start | bytes 786440 | tf_op jit(solution)/shard_map/ppermute | solution.py:347
  28.0 13.3 %collective-permute-start.4 = (f32[512,256]{1,0:T(8,128)S(1)}, f32[512,256]{1,0:T(8,128)S(1)}, u32[]{:S(2)}, u32[]{:S(2)}) collective-permute-start(f32[512,256]{1,0:T(8,128)S(1)} %pad_maximum_fusion.3), channel_id=1, source_target_pairs={{0,192},{4,196},{8,200},{12,204},{16,208},{20,212},{24,216},{28,22... | collective-permute-start | bytes 1572872 | tf_op jit(solution)/shard_map/ppermute | solution.py:355
  31.6 13.0 %collective-permute-start.2 = (f32[512,256]{1,0:T(8,128)S(1)}, f32[512,256]{1,0:T(8,128)S(1)}, u32[]{:S(2)}, u32[]{:S(2)}) collective-permute-start(f32[512,256]{1,0:T(8,128)S(1)} %pad_maximum_fusion.2), channel_id=1, source_target_pairs={{0,64},{4,68},{8,72},{12,76},{16,80},{20,84},{24,88},{28,92},{32,9... | collective-permute-start | bytes 1572872 | tf_op jit(solution)/shard_map/ppermute | solution.py:354
  31.7 19.8 %copy-start.8 = (s32[8]{0:T(128)S(1)}, s32[8]{0:T(128)}, u32[]{:S(2)}) copy-start(s32[8]{0:T(128)} %param.9) | copy-start | bytes 100
  45.4 20.4 %all-to-all-start = ((f32[8,64,256]{2,1,0:T(8,128)}), f32[8,64,256]{2,1,0:T(8,128)S(1)}, u32[]{:S(2)}, u32[]{:S(2)}) async-start(f32[8,64,256]{2,1,0:T(8,128)} %bitcast.14), calls=%async_computation | async-start | bytes 1048576 | tf_op jit(solution)/shard_map/all_to_all | solution.py:318
  52.5 21.8 %collective-permute-start.6 = (f32[64,256]{1,0:T(8,128)S(1)}, f32[64,256]{1,0:T(8,128)S(1)}, u32[]{:S(2)}, u32[]{:S(2)}) collective-permute-start(f32[64,256]{1,0:T(8,128)S(1)} %reduce_sum.48), channel_id=1, source_target_pairs={{0,192},{4,196},{8,200},{12,204},{16,208},{20,212},{24,216},{28,22... | collective-permute-start | bytes 196616 | tf_op jit(solution)/shard_map/ppermute | solution.py:361
  52.7 21.6 %collective-permute-start.7 = (f32[64,256]{1,0:T(8,128)S(1)}, f32[64,256]{1,0:T(8,128)S(1)}, u32[]{:S(2)}, u32[]{:S(2)}) collective-permute-start(f32[64,256]{1,0:T(8,128)S(1)} %reduce_sum.48), channel_id=1, source_target_pairs={{0,128},{4,132},{8,136},{12,140},{16,144},{20,148},{24,152},{28,15... | collective-permute-start | bytes 196616 | tf_op jit(solution)/shard_map/ppermute | solution.py:361
  53.4 20.9 %collective-permute-start.5 = (f32[64,256]{1,0:T(8,128)S(1)}, f32[64,256]{1,0:T(8,128)S(1)}, u32[]{:S(2)}, u32[]{:S(2)}) collective-permute-start(f32[64,256]{1,0:T(8,128)S(1)} %reduce_sum.48), channel_id=1, source_target_pairs={{0,64},{4,68},{8,72},{12,76},{16,80},{20,84},{24,88},{28,92},{32,9... | collective-permute-start | bytes 196616 | tf_op jit(solution)/shard_map/ppermute | solution.py:360
  66.7 16.9 %all-to-all-start.1 = ((f32[8,64,256]{2,1,0:T(8,128)}), f32[8,64,256]{2,1,0:T(8,128)S(1)}, u32[]{:S(2)}, u32[]{:S(2)}) async-start(f32[8,64,256]{2,1,0:T(8,128)} %broadcast_in_dim.79), calls=%async_computation.1 | async-start | bytes 1048576 | tf_op jit(solution)/shard_map/all_to_all | solution.py:318
  74.3 1.3 collective-permute-start.8
  85.4 4.4 %copy-start.2 = (f32[1,160,2,640]{3,2,1,0:T(2,128)S(1)}, f32[1,160,2,640]{3,2,1,0:T(2,128)}, u32[]{:S(2)}) copy-start(f32[1,160,2,640]{3,2,1,0:T(2,128)} %param.12) | copy-start | bytes 2457604
  85.4 53.8 %all-to-all-start.3 = ((f32[8,2,80,256]{3,2,1,0:T(8,128)}), f32[8,2,80,256]{3,2,1,0:T(8,128)}, u32[]{:S(2)}, u32[]{:S(2)}) async-start(f32[8,2,80,256]{3,2,1,0:T(8,128)} %bitcast.22), calls=%async_computation.3 | async-start | bytes 2621440 | tf_op jit(solution)/shard_map/all_to_all | solution.py:318
  90.5 4.0 %copy-start.3 = (f32[1,160,2,640]{3,2,1,0:T(2,128)S(1)}, f32[1,160,2,640]{3,2,1,0:T(2,128)}, u32[]{:S(2)}) copy-start(f32[1,160,2,640]{3,2,1,0:T(2,128)} %param.11) | copy-start | bytes 2457604
  90.6 5.7 %copy-start.1 = (f32[160,1280]{1,0:T(8,128)}, f32[160,1280]{1,0:T(8,128)S(1)}, u32[]{:S(2)}) copy-start(f32[160,1280]{1,0:T(8,128)S(1)} %pad_maximum_fusion.b0) | copy-start | bytes 2457604
  90.6 20.5 %collective-permute-start.9 = (f32[160,1280]{1,0:T(8,128)S(1)}, f32[160,1280]{1,0:T(8,128)S(1)}, u32[]{:S(2)}, u32[]{:S(2)}) collective-permute-start(f32[160,1280]{1,0:T(8,128)S(1)} %pad_maximum_fusion.b0), channel_id=1, source_target_pairs={{0,3},{1,0},{2,1},{3,2},{4,7},{5,4},{6,5},{7,6},{8,11},{9,8},{10,9... | collective-permute-start | bytes 2457608 | tf_op jit(solution)/shard_map/ppermute | solution.py:399
  93.5 20.1 %collective-permute-start.10 = (f32[160,1280]{1,0:T(8,128)S(1)}, f32[160,1280]{1,0:T(8,128)S(1)}, u32[]{:S(2)}, u32[]{:S(2)}) collective-permute-start(f32[160,1280]{1,0:T(8,128)S(1)} %pad_maximum_fusion.b0), channel_id=1, source_target_pairs={{0,2},{1,3},{2,0},{3,1},{4,6},{5,7},{6,4},{7,5},{8,10},{9,11},{10,... | collective-permute-start | bytes 2457608 | tf_op jit(solution)/shard_map/ppermute | solution.py:399
  93.8 39.0 %collective-permute-start.11 = (f32[160,1280]{1,0:T(8,128)S(1)}, f32[160,1280]{1,0:T(8,128)}, u32[]{:S(2)}, u32[]{:S(2)}) collective-permute-start(f32[160,1280]{1,0:T(8,128)S(1)} %pad_maximum_fusion.b0), channel_id=1, source_target_pairs={{0,1},{1,2},{2,3},{3,0},{4,5},{5,6},{6,7},{7,4},{8,9},{9,10},{10,1... | collective-permute-start | bytes 2457608 | tf_op jit(solution)/shard_map/ppermute | solution.py:399
  94.5 8.9 %copy-start.7 = (s32[8,64]{1,0:T(8,128)S(1)}, s32[8,64]{1,0:T(8,128)}, u32[]{:S(2)}) copy-start(s32[8,64]{1,0:T(8,128)} %param.10) | copy-start | bytes 6148
  96.3 75.9 %collective-permute-start.15 = (f32[160,640]{1,0:T(8,128)}, f32[160,640]{1,0:T(8,128)}, u32[]{:S(2)}, u32[]{:S(2)}) collective-permute-start(f32[160,640]{1,0:T(8,128)} %get-tuple-element.37), channel_id=1, source_target_pairs={{1,0},{3,2},{4,7},{6,5},{9,8},{11,10},{12,15},{14,13},{17,16},{19,... | collective-permute-start | bytes 1228808 | tf_op jit(solution)/shard_map/ppermute | solution.py:399
  111.1 21.6 %copy-start.4 = (f32[160,1280]{1,0:T(8,128)}, f32[160,1280]{1,0:T(8,128)S(1)}, u32[]{:S(2)}) copy-start(f32[160,1280]{1,0:T(8,128)S(1)} %collective-permute-done.9.b1) | copy-start | bytes 2457604
  113.6 0.9 copy-start.5
  153.3 89.6 %all-to-all-start.4 = ((f32[64,24,256]{2,1,0:T(8,128)}), f32[64,24,256]{2,1,0:T(8,128)S(1)}, u32[]{:S(2)}, u32[]{:S(2)}) async-start(f32[64,24,256]{2,1,0:T(8,128)} %update.1), calls=%async_computation.4 | async-start | bytes 3145728 | tf_op jit(solution)/shard_map/all_to_all | solution.py:437
  161.8 10.4 %copy-start.6 = (f32[160,640]{1,0:T(8,128)S(1)}, f32[160,640]{1,0:T(8,128)}, u32[]{:S(2)}) copy-start(f32[160,640]{1,0:T(8,128)} %get-tuple-element.36) | copy-start | bytes 1228804
  161.8 30.7 %copy-start = (s32[3]{0:T(128)S(1)}, s32[3]{0:T(128)}, u32[]{:S(2)}) copy-start(s32[3]{0:T(128)} %pad_add_fusion.at) | copy-start | bytes 40
  163.2 27.8 %collective-permute-start.12 = (f32[640,256]{1,0:T(8,128)S(1)}, f32[640,256]{1,0:T(8,128)S(1)}, u32[]{:S(2)}, u32[]{:S(2)}) collective-permute-start(f32[640,256]{1,0:T(8,128)S(1)} %bitcast.85), channel_id=1, source_target_pairs={{1,0},{3,2},{4,7},{6,5},{9,8},{11,10},{12,15},{14,13},{17,16},{19,... | collective-permute-start | bytes 1966088 | tf_op jit(solution)/shard_map/ppermute | solution.py:399
  167.7 23.4 %collective-permute-start.13 = (f32[640,256]{1,0:T(8,128)S(1)}, f32[640,256]{1,0:T(8,128)S(1)}, u32[]{:S(2)}, u32[]{:S(2)}) collective-permute-start(f32[640,256]{1,0:T(8,128)S(1)} %bitcast.86), channel_id=1, source_target_pairs={{0,2},{2,0},{5,7},{7,5},{8,10},{10,8},{13,15},{15,13},{16,18},{18,... | collective-permute-start | bytes 1966088 | tf_op jit(solution)/shard_map/ppermute | solution.py:399
  168.4 22.7 %collective-permute-start.14 = (f32[640,256]{1,0:T(8,128)S(1)}, f32[640,256]{1,0:T(8,128)S(1)}, u32[]{:S(2)}, u32[]{:S(2)}) collective-permute-start(f32[640,256]{1,0:T(8,128)S(1)} %bitcast.84), channel_id=1, source_target_pairs={{1,2},{3,0},{4,5},{6,7},{9,10},{11,8},{12,13},{14,15},{17,18},{19,... | collective-permute-start | bytes 1966088 | tf_op jit(solution)/shard_map/ppermute | solution.py:399
  171.5 3.5 %collective-permute-start.16 = (f32[160,640]{1,0:T(8,128)}, f32[160,640]{1,0:T(8,128)S(1)}, u32[]{:S(2)}, u32[]{:S(2)}) collective-permute-start(f32[160,640]{1,0:T(8,128)} %get-tuple-element.37), channel_id=1, source_target_pairs={{0,2},{2,0},{5,7},{7,5},{8,10},{10,8},{13,15},{15,13},{16,18},{18,... | collective-permute-start | bytes 1228808 | tf_op jit(solution)/shard_map/ppermute | solution.py:399
  172.2 18.9 %collective-permute-start.17 = (f32[160,640]{1,0:T(8,128)S(1)}, f32[160,640]{1,0:T(8,128)S(1)}, u32[]{:S(2)}, u32[]{:S(2)}) collective-permute-start(f32[160,640]{1,0:T(8,128)S(1)} %copy-done.6), channel_id=1, source_target_pairs={{1,2},{3,0},{4,5},{6,7},{9,10},{11,8},{12,13},{14,15},{17,18},{19,... | collective-permute-start | bytes 1228808 | tf_op jit(solution)/shard_map/ppermute | solution.py:399
  174.9 16.2 %copy-start.12 = (f32[160,640]{1,0:T(8,128)}, f32[160,640]{1,0:T(8,128)S(1)}, u32[]{:S(2)}) copy-start(f32[160,640]{1,0:T(8,128)S(1)} %collective-permute-done.16.f2) | copy-start | bytes 1228804
  191.0 0.8 copy-start.13
  191.0 1.0 copy-start.9
  191.0 1.2 copy-start.10
  191.1 1.4 copy-start.11
  222.1 10.4 %collective-permute-start.18 = (f32[160,640]{1,0:T(8,128)S(1)}, f32[160,640]{1,0:T(8,128)}, u32[]{:S(2)}, u32[]{:S(2)}) collective-permute-start(f32[160,640]{1,0:T(8,128)S(1)} %get-tuple-element.15), channel_id=1, source_target_pairs={{0,1},{2,3},{5,6},{7,4},{8,9},{10,11},{13,14},{15,12},{16,17},{18,... | collective-permute-start | bytes 1228808 | tf_op jit(solution)/shard_map/ppermute | solution.py:399
  223.4 9.1 %collective-permute-start.19 = (f32[160,640]{1,0:T(8,128)S(1)}, f32[160,640]{1,0:T(8,128)}, u32[]{:S(2)}, u32[]{:S(2)}) collective-permute-start(f32[160,640]{1,0:T(8,128)S(1)} %get-tuple-element.16), channel_id=1, source_target_pairs={{0,2},{2,0},{5,7},{7,5},{8,10},{10,8},{13,15},{15,13},{16,18},{18,... | collective-permute-start | bytes 1228808 | tf_op jit(solution)/shard_map/ppermute | solution.py:399
  224.8 15.2 %collective-permute-start.20 = (f32[160,640]{1,0:T(8,128)S(1)}, f32[160,640]{1,0:T(8,128)}, u32[]{:S(2)}, u32[]{:S(2)}) collective-permute-start(f32[160,640]{1,0:T(8,128)S(1)} %get-tuple-element.17), channel_id=1, source_target_pairs={{0,3},{2,1},{5,4},{7,6},{8,11},{10,9},{13,12},{15,14},{16,19},{18,... | collective-permute-start | bytes 1228808 | tf_op jit(solution)/shard_map/ppermute | solution.py:399
